TPU v7x, 32 devices: a whole 2x2x4 slice. The times are simulated.
32 devices in a mesh: rep: 2 (over x), space: 16 (over z, y, core).
Axes of the slice: x: 2, y: 2, z: 4, core: 2. Of those that a mesh axis runs over, the one named last changes fastest.
Arguments:
- positions: float32 [15, 16, 32, 128], P(None, None, ('rep', 'space')), parts along dimension 2, may hold values from -1.5 to 1.5
- momenta: float32 [15, 16, 32, 128], P(None, None, ('rep', 'space')), parts along dimension 2, may hold values from -5 to 5
- masses: float32 [15], replicated, may hold values from 1 to 4
- step_size: float32 [1], replicated, may hold values from 0.25 to 0.5
- cycle_frequency: float32 [1], replicated, may hold values from 0.5 to 1
- layer_one: bfloat16 [256, 405], replicated, may hold values from -0.625 to 0.625
- bias_one: float32 [256], replicated, may hold values from -3 to 3
- layer_two: bfloat16 [256, 256], replicated, may hold values from -0.375 to 0.375
- bias_two: float32 [256], replicated, may hold values from -3 to 3
- readout: float32 [256], replicated, may hold values from -1.5 to 1.5
- wavevectors: int32 [3, 4096], replicated, may hold values from -8 to 7
Outputs:
- positions_final: float32 [15, 16, 32, 128], P(None, None, ('rep', 'space')), parts along dimension 2
- momenta_final: float32 [15, 16, 32, 128], P(None, None, ('rep', 'space')), parts along dimension 2
- spectrum: float32 [8192, 480], P(('rep', 'space')), parts along dimension 0
There are 2 independent parts, one for each index of `rep`. A program takes and returns all parts, laid end to end along the dimension named above; an argument that names none is the same for every part. Nothing has to cross between parts.
All inputs are finite; a program needn't handle non-finite values.
Results may differ from a plain program's by a relative error of at most 0.0044.
Values may be sent and summed in bfloat16 or wider, within the bound.
No kernel may reach another device: no remote copies, remote signals or barrier semaphores. Data moves between devices by JAX's collectives and lax.ppermute only.
A program may use at most 64 MiB of HBM per device.

v0:
```python
import functools
import math

import jax
import jax.numpy as jnp
import numpy as np
from jax import lax
from jax.experimental import pallas as pl
from jax.experimental.pallas import tpu as pltpu
from jax.sharding import PartitionSpec as P


NY = 8
NZ = 16
CELLS = NY * NZ
PAD = 16
BLOCK = 9 * PAD
DEPTH = 256
GROUP = 4
SHIFTS = [(b, d) for b in (-1, 0, 1) for d in (-1, 0, 1)]
HIGHEST = lax.Precision.HIGHEST
TWO_PI = 6.283185307179586
VMEM = pl.BlockSpec(memory_space=pltpu.VMEM)
SMEM = pl.BlockSpec(memory_space=pltpu.SMEM)
HBM = pl.BlockSpec(memory_space=pltpu.MemorySpace.HBM)
shape = jax.ShapeDtypeStruct
f32, bf16 = jnp.float32, jnp.bfloat16

call = functools.partial(pl.pallas_call, compiler_params=pltpu.CompilerParams(vmem_limit_bytes=16 << 20))
dot = functools.partial(jnp.dot, preferred_element_type=jnp.float32)
exact_dot = functools.partial(jnp.dot, precision=HIGHEST, preferred_element_type=jnp.float32)


def in_hbm(value):
    return pltpu.with_memory_space_constraint(value, pltpu.MemorySpace.HBM)


def roll(values, amount):
    amount = amount % CELLS
    return values if amount == 0 else pltpu.roll(values, amount, 1)


def shift_y(values, step):
    return roll(values, -step * NZ)


def shift_z(values, step, inner):
    if step == 0:
        return values
    edge = NZ - 1 if step == 1 else 0
    return jnp.where(inner == edge, roll(values, step * (NZ - 1)), roll(values, -step))


def z_index(rows):
    return lax.broadcasted_iota(jnp.int32, (rows, CELLS), 1) % NZ


def load_kernel(*refs):
    count = (len(refs) - 2) // 2
    sources, rounded_ref, targets, semaphores = refs[:count], refs[count], refs[count + 1 : -1], refs[-1]
    copies = [pltpu.make_async_copy(a, b, semaphores.at[i]) for i, (a, b) in enumerate(zip(sources, targets))]
    for copy in copies:
        copy.start()
    copies[0].wait()
    rounded_ref[...] = targets[0][...].astype(bf16)
    for copy in copies[1:]:
        copy.wait()


def setup_kernel(
    coords, beads, masses_hbm, step_hbm, cycle_hbm, one_ref, bias_one_ref, two_ref, bias_two_ref, readout_ref,
    q_ref, p_ref, modes_ref, modes_t_ref, forward_ref, outer_forward_ref, backward_ref, two_t_ref, wide_ref,
    q_base_ref, q_map_ref, p_base_ref, pushed_ref, cosine_ref, finish_ref, half_ref,
    rows, masses_ref, step_ref, cycle_ref, semaphores
):
    copies = [
        pltpu.make_async_copy(masses_hbm, masses_ref, semaphores.at[0]),
        pltpu.make_async_copy(step_hbm, step_ref, semaphores.at[1]),
        pltpu.make_async_copy(cycle_hbm, cycle_ref, semaphores.at[2]),
    ]
    for copy in copies:
        copy.start()
    is_odd = lax.axis_index("space") % 2 == 1
    hidden = one_ref.shape[1]
    rows[: one_ref.shape[0], :] = one_ref[...].astype(f32)
    rows[one_ref.shape[0] :, :] = jnp.zeros((rows.shape[0] - one_ref.shape[0], hidden), f32)
    at = lax.broadcasted_iota(jnp.int32, (PAD, hidden), 0)
    real = at < coords
    rest = bias_one_ref[...]
    turned = []
    for along_x in range(3):
        for o in range(9):
            even, odd = ((a * 9 + o) * coords for a in (along_x, 2 - along_x))
            taken = rows[even : even + PAD, :]
            if odd != even:
                taken = jnp.where(is_odd, rows[odd : odd + PAD, :], taken)
            taken = jnp.where(real, taken, 0.0)
            top = (along_x * 9 + o) * PAD
            backward_ref[top : top + PAD, :] = taken.astype(bf16)
            if along_x == 0 and o < 3:
                term = rest.astype(bf16).astype(f32)
                rest = rest - term
                taken = jnp.where(real, taken, jnp.broadcast_to(term, taken.shape))
                taken = jnp.where(at <= coords, taken, 0.0)
            turned.append(taken)
    forward = jnp.concatenate(turned).T.astype(bf16)
    forward_ref[...] = forward
    outer_forward_ref[...] = jnp.concatenate([forward[:, BLOCK:], forward[:, :BLOCK]], axis=1)
    two_t_ref[...] = two_ref[...].astype(f32).T.astype(bf16)
    columns = jnp.concatenate([bias_two_ref[...], readout_ref[...], jnp.zeros((6, hidden), f32)]).T
    for i in range(2):
        wide_ref[i] = jnp.broadcast_to(columns[:, i : i + 1], (hidden, CELLS))

    for copy in copies:
        copy.wait()
    total = coords * beads
    order = (lax.broadcasted_iota(jnp.int32, (total, CELLS), 0) % beads).astype(f32)
    mass = jnp.concatenate([jnp.full((beads, CELLS), masses_ref[c], f32) for c in range(coords)])
    step = step_ref[0]
    half = 0.5 * step
    frequency = 2.0 * cycle_ref[0] * jnp.sin(order * (0.5 * TWO_PI / beads))
    phase = frequency * step
    cosine, sine = jnp.cos(phase), jnp.sin(phase)
    drift = step * jnp.where(order == 0, 1.0, sine / jnp.where(order == 0, 1.0, phase)) / mass
    spring = mass * frequency * sine
    mode = exact_dot(modes_t_ref[...], jnp.concatenate([q_ref[...], p_ref[...]], axis=1))
    mode_q, mode_p = mode[:, :CELLS], mode[:, CELLS:]
    moved = cosine * mode_q + drift * mode_p
    pushed = cosine * mode_p - spring * mode_q
    base = exact_dot(modes_ref[...], jnp.concatenate([moved, pushed], axis=1))
    q_base_ref[...] = base[:, :CELLS]
    p_base_ref[...] = base[:, CELLS:]
    pushed_ref[...] = pushed
    cosine_ref[...] = cosine
    q_map_ref[...] = exact_dot(modes_ref[...], (half * drift[:, :1]) * modes_t_ref[...])
    finish_ref[...] = jnp.concatenate([half / mass, 1.0 / mass], axis=1)
    half_ref[...] = jnp.full(half_ref.shape, half, f32)


def put_features(coords, beads, plane_ref, stage, features, top):
    stage[...] = plane_ref[...].astype(f32)
    filler = jnp.ones((PAD - coords, CELLS), f32)
    pieces = []
    for j in range(beads):
        pieces += [stage[pl.ds(j, coords, stride=beads), :], filler]
    plane = jnp.concatenate(pieces)
    inner_z = z_index(beads * PAD)
    along = {d: shift_z(plane, d, inner_z) for d in (-1, 0, 1)}
    for o, (b, d) in enumerate(SHIFTS):
        moved = shift_y(along[d], b).astype(bf16)
        first = top + o * PAD
        for j in range(beads):
            features[first : first + PAD, j * CELLS : (j + 1) * CELLS] = moved[j * PAD : (j + 1) * PAD]


def back_one(first, two_ref, two_t_ref, wide_ref):
    bias, readout = (jnp.concatenate([wide_ref[i]] * GROUP, axis=1) for i in range(2))
    hidden = jnp.tanh(first).astype(bf16)
    second = jnp.tanh(dot(two_ref[...], hidden) + bias)
    back = (readout * (1.0 - second * second)).astype(bf16)
    widened = hidden.astype(f32)
    return (dot(two_t_ref[...], back) * (1.0 - widened * widened)).astype(bf16)


def shifted_sum(sums, at):
    inner_z = z_index(PAD)
    total = None
    for d in (-1, 0, 1):
        part = None
        for b in (-1, 0, 1):
            o = (b + 1) * 3 + d + 1
            moved = shift_y(sums[o * PAD : (o + 1) * PAD, at * CELLS : (at + 1) * CELLS], -b)
            part = moved if part is None else part + moved
        part = shift_z(part, -d, inner_z)
        total = part if total is None else total + part
    return total


def own_kernel(
    coords, beads, tied, outer_ref, own_ref, inner_ref, forward_ref, backward_ref, two_ref, two_t_ref, wide_ref, *refs
):
    sent_ref, kept_ref, features, stage = refs[tied:]
    for place, ref in enumerate((outer_ref, own_ref, inner_ref)):
        put_features(coords, beads, ref, stage, features, place * BLOCK)
    for first in range(0, beads, GROUP):
        columns = slice(first * CELLS, (first + GROUP) * CELLS)
        back = back_one(dot(forward_ref[...], features[:, columns]), two_ref, two_t_ref, wide_ref)
        sums = dot(backward_ref[BLOCK:], back)
        for at in range(GROUP):
            rows = pl.ds(first + at, coords, stride=beads)
            kept_ref[rows, :] = shifted_sum(sums[:BLOCK], at)[:coords]
            sent_ref[rows, :] = shifted_sum(sums[BLOCK:], at)[:coords]


def outer_kernel(
    coords, beads, outer2_ref, features_ref, kept_in_ref, forward_ref, backward_ref, two_ref, two_t_ref, wide_ref,
    kept_ref, features, stage
):
    extra = 2 * BLOCK - DEPTH
    put_features(coords, beads, outer2_ref, stage, features, extra)
    features[:extra, :] = features_ref[DEPTH : 2 * BLOCK, :]
    for first in range(0, beads, GROUP):
        columns = slice(first * CELLS, (first + GROUP) * CELLS)
        pre = dot(forward_ref[:, :DEPTH], features_ref[:DEPTH, columns])
        pre = pre + dot(forward_ref[:, DEPTH:], features[:, columns])
        sums = dot(backward_ref[2 * BLOCK :], back_one(pre, two_ref, two_t_ref, wide_ref))
        for at in range(GROUP):
            rows = pl.ds(first + at, coords, stride=beads)
            kept_ref[rows, :] = kept_in_ref[rows, :] + shifted_sum(sums, at)[:coords]


def move_kernel(q_base_ref, q_map_ref, kept_ref, came_ref, q_out, rounded_out, sum_out):
    sums = kept_ref[...] + came_ref[...]
    sum_out[...] = sums
    q = q_base_ref[...] - exact_dot(q_map_ref[...], sums)
    q_out[...] = q
    rounded_out[...] = q.astype(bf16)


def push_kernel(
    share, planes_at, half_ref, sum_ref, p_base_ref, pushed_ref, cosine_ref, finish_ref, modes_ref, modes_t_ref,
    vectors_ref, p_out, velocity_out, velocity_map_out, planes_out, cells_out
):
    kick = cosine_ref[...] * exact_dot(modes_t_ref[...], half_ref[0:1, :] * sum_ref[...])
    p_out[...] = p_base_ref[...] - exact_dot(modes_ref[...], kick)
    velocity_out[...] = (pushed_ref[...] - kick) * finish_ref[:, CELLS:]
    velocity_map_out[...] = finish_ref[:, :1] * modes_t_ref[...]
    extent_x = len(planes_at)
    whole = extent_x * CELLS
    here = lax.axis_index("space")
    if vectors_ref.shape[1] == share:
        vectors = vectors_ref[...]
    else:
        vectors = vectors_ref[:, pl.ds(pl.multiple_of(here * share, CELLS), share)]
    cell = lax.broadcasted_iota(jnp.int32, (CELLS, share), 0)
    along = vectors[1:2] * ((cell // NZ) * (extent_x * NZ)) + vectors[2:3] * ((cell % NZ) * (extent_x * NY))
    across = jnp.concatenate([vectors[0:1] * ((here ^ at) * CELLS) for at in planes_at])
    for numerator, out in ((across, planes_out), (along, cells_out)):
        angle = TWO_PI * (numerator & (whole - 1)).astype(f32) / whole
        out[0] = jnp.cos(angle)
        out[1] = jnp.sin(angle)


def finish_kernel(half_ref, velocity_ref, map_ref, kept_ref, came_ref, velocity_out, kick_out):
    sums = kept_ref[...] + came_ref[...]
    velocity_out[...] = (velocity_ref[...] - exact_dot(map_ref[...], sums)).astype(bf16)
    kick_out[...] = half_ref[0:1, :] * sums


def project_kernel(scale, velocity_ref, planes_ref, cells_ref, out_ref):
    count, fields, _ = velocity_ref.shape
    cos_cell, sin_cell = cells_ref[0], cells_ref[1]

    def trig(i):
        cos_plane, sin_plane = planes_ref[0, i : i + 1, :], planes_ref[1, i : i + 1, :]
        cosine = cos_plane * cos_cell - sin_plane * sin_cell
        sine = sin_plane * cos_cell + cos_plane * sin_cell
        return cosine.astype(bf16), sine.astype(bf16)

    cos_sum = sin_sum = 0.0
    for i in range(0, count, 2):
        (cos_0, sin_0), (cos_1, sin_1) = trig(i), trig(i + 1)
        block = jnp.concatenate([velocity_ref[i], velocity_ref[i + 1]], axis=1)
        cos_sum += dot(block, jnp.concatenate([cos_0, cos_1]))
        sin_sum += dot(block, jnp.concatenate([sin_0, sin_1]))
    out_ref[:fields, :] = cos_sum * scale
    out_ref[fields:, :] = sin_sum * scale


def mode_matrix(coords, beads):
    j = np.arange(beads)[:, None]
    k = np.arange(beads)[None, :]
    angles = 2.0 * np.pi * ((j * k) % beads) / beads
    edge = np.cos(angles) / math.sqrt(beads)
    inside = np.where(k < beads // 2, np.cos(angles), np.sin(angles)) * math.sqrt(2.0 / beads)
    matrix = np.where((k == 0) | (k == beads // 2), edge, inside)
    modes = np.einsum("ab,jk->ajbk", np.eye(coords), matrix).reshape(coords * beads, coords * beads)
    return modes.astype(np.float32)


def swap(value, distance):
    return lax.ppermute(value, "space", [(i, i ^ distance) for i in range(lax.axis_size("space"))])


def neighbour_planes(plane):
    count = lax.axis_size("space")
    step = [1 if i % 2 else -1 for i in range(count)]
    outer = lax.ppermute(plane, "space", [(i, (i + step[i]) % count) for i in range(count)])
    inner = swap(plane, 1)
    outer2 = lax.ppermute(plane, "space", [(i, (i - 2 * step[i]) % count) for i in range(count)])
    return outer2, outer, inner


def gather_order(count):
    order, distance = [0], count // 2
    while distance:
        if distance == 4:
            order, distance = [i ^ d for d in (0, 2, 4, 6) for i in order], 1
        else:
            order, distance = [i ^ d for d in (0, distance) for i in order], distance // 2
    return order


def gather_planes(velocity):
    held, distance = velocity[None], lax.axis_size("space") // 2
    while distance:
        if distance == 4:
            near, far = swap(held, 2), swap(held, 4)
            held, distance = jnp.concatenate([held, near, far, swap(near, 4)]), 1
        else:
            held, distance = jnp.concatenate([held, swap(held, distance)]), distance // 2
    return held


def on_device(
    positions, momenta, masses, step_size, cycle_frequency,
    layer_one, bias_one, layer_two, bias_two, readout, wavevectors
):
    coords, beads, planes, cells = positions.shape
    devices = lax.axis_size("space")
    assert planes == 1 and cells == CELLS and devices & (devices - 1) == 0 and devices > 1
    total = coords * beads
    hidden = layer_one.shape[0]
    width = 27 * PAD
    field, narrow = shape((total, CELLS), f32), shape((total, CELLS), bf16)
    square = shape((total, total), f32)

    modes = mode_matrix(coords, beads)
    share = wavevectors.shape[1] // devices
    if share % CELLS:
        wavevectors = lax.dynamic_slice_in_dim(wavevectors, lax.axis_index("space") * share, share, 1)
    inputs = (
        positions.reshape(total, CELLS), momenta.reshape(total, CELLS),
        layer_one.T, bias_one.reshape(1, hidden), layer_two, bias_two.reshape(1, hidden), readout.reshape(1, hidden),
        jnp.asarray(modes), jnp.asarray(modes.T), wavevectors,
    )
    rounded, q, p, one_t, bias_one, two, bias_two, readout, modes, modes_t, wavevectors = call(
        load_kernel,
        out_shape=(narrow,) + tuple(shape(x.shape, x.dtype) for x in inputs),
        in_specs=[HBM] * len(inputs), out_specs=(VMEM,) * (len(inputs) + 1),
        scratch_shapes=[pltpu.SemaphoreType.DMA((len(inputs),))],
    )(*map(in_hbm, inputs))

    (
        forward, outer_forward, backward, two_t, wide, q_base, q_map, p_base, pushed, cosine, finish, half
    ) = call(
        functools.partial(setup_kernel, coords, beads),
        out_shape=(
            shape((hidden, width), bf16), shape((hidden, width), bf16), shape((width, hidden), bf16),
            shape((hidden, hidden), bf16), shape((2, hidden, CELLS), f32),
            field, square, field, field, field, shape((total, 2 * CELLS), f32), shape((8, CELLS), f32),
        ),
        in_specs=[HBM] * 3 + [VMEM] * 9, out_specs=(VMEM,) * 12,
        scratch_shapes=[
            pltpu.VMEM((width, hidden), f32), pltpu.SMEM((coords,), f32), pltpu.SMEM((1,), f32),
            pltpu.SMEM((1,), f32), pltpu.SemaphoreType.DMA((3,)),
        ],
    )(
        in_hbm(masses), step_size, cycle_frequency, one_t, bias_one, two, bias_two, readout, q, p, modes, modes_t
    )
    layers = (backward, two, two_t, wide)
    stage = pltpu.VMEM((total, CELLS), f32)

    def forces(plane, *tied):
        outer2, outer, inner = neighbour_planes(plane)
        sent, kept, features = call(
            functools.partial(own_kernel, coords, beads, len(tied)),
            out_shape=(field, field, shape((width, beads * CELLS), bf16)),
            in_specs=[VMEM] * (8 + len(tied)), out_specs=(VMEM,) * 3, scratch_shapes=[stage],
        )(outer, plane, inner, forward, *layers, *tied)
        came = swap(sent, 1)
        kept = call(
            functools.partial(outer_kernel, coords, beads),
            out_shape=field, in_specs=[VMEM] * 8, out_specs=VMEM,
            scratch_shapes=[pltpu.VMEM((width - DEPTH, beads * CELLS), bf16), stage],
        )(outer2, features, kept, outer_forward, *layers)
        return kept, came

    q_new, rounded, sums = call(
        move_kernel, out_shape=(field, narrow, field), in_specs=[VMEM] * 4, out_specs=(VMEM,) * 3,
    )(q_base, q_map, *forces(rounded))
    order = gather_order(devices)
    p_mid, velocity_base, velocity_map, across, along = call(
        functools.partial(push_kernel, share, order),
        out_shape=(field, field, square, shape((2, devices, share), f32), shape((2, CELLS, share), f32)),
        in_specs=[VMEM] * 9, out_specs=(VMEM,) * 5,
    )(half, sums, p_base, pushed, cosine, finish, modes, modes_t, wavevectors)
    velocity, kick = call(
        finish_kernel, out_shape=(narrow, field), in_specs=[VMEM] * 5, out_specs=(VMEM,) * 2,
    )(half, velocity_base, velocity_map, *forces(rounded))
    p_new = p_mid - kick
    spectrum = call(
        functools.partial(project_kernel, 1.0 / math.sqrt(devices * CELLS)),
        out_shape=shape((2 * total, share), f32), in_specs=[VMEM] * 3, out_specs=VMEM,
    )(gather_planes(velocity), across, along)
    return q_new.reshape(positions.shape), p_new.reshape(momenta.shape), spectrum.T


def solution(mesh):
    field = P(None, None, ("rep", "space"), None)

    return jax.shard_map(
        on_device,
        mesh=mesh,
        in_specs=(field, field) + (P(),) * 9,
        out_specs=(field, field, P(("rep", "space"), None)),
        check_vma=False,
    )
```

profile of v0, /device:TPU:0, one launch (start us, length us, event | category | flops | bytes accessed | tf_op | source)
XLA Modules:
  0.0 67.7 jit_solution(2534557446750711260)
XLA Ops:
  0.6 1.5 %shard_map.148 = (bf16[240,128]{1,0:T(8,128)(2,1)S(1)}, f32[240,128]{1,0:T(8,128)S(1)}, f32[240,128]{1,0:T(8,128)S(1)}, bf16[405,256]{1,0:T(8,128)(2,1)S(1)}, f3...) custom-call(f32[240,128]{1,0:T(8,128)} %bitcast.21, ...), custom_call_target="tpu_custom_call" | custom-call | tf_op jit(solution)/shard_map/pallas_call | solution.py:337
  2.1 5.5 %collective-permute-start.1 = (bf16[240,128]{1,0:T(8,128)(2,1)S(1)}, bf16[240,128]{1,0:T(8,128)(2,1)S(1)}, u32[]{:S(2)}, u32[]{:S(2)}) collective-permute-start(bf16[240,128]{1,0:T(8,128)(2,1)S(1)} %get-tuple-element.53.own_ref), channel_id=1, source_target_pairs={{0,15},{1,2},{2,1},{3,4},{4,3},{5,6},{6,5},{7,8},{8,7},{9,10},{10,... | collective-permute-start | bytes 184328 | tf_op jit(solution)/shard_map/ppermute | solution.py:288
  7.6 0.0 collective-permute-start.2
  8.9 2.7 %shard_map.149 = (bf16[256,432]{1,0:T(8,128)(2,1)S(1)}, bf16[256,432]{1,0:T(8,128)(2,1)S(1)}, bf16[432,256]{1,0:T(8,128)(2,1)S(1)}, bf16[256,256]{1,0:T(8,128)(2...) custom-call(f32[15]{0:T(128)} %masses_hbm.1, ...), custom_call_target="tpu_custom_call" | custom-call | tf_op jit(solution)/shard_map/pallas_call | solution.py:346
  11.7 0.0 collective-permute-done.1.outer_ref
  11.7 0.0 collective-permute-done.2.inner_ref
  11.7 3.9 %shard_map.150 = (f32[240,128]{1,0:T(8,128)S(1)}, f32[240,128]{1,0:T(8,128)S(1)}, bf16[432,2048]{1,0:T(8,128)(2,1)S(1)}) custom-call(bf16[240,128]{1,0:T(8,128)(2,1)S(1)} %collective-permute-done.1.outer_ref, bf16[240,128]{1,0:T(8,128)(2,1)S(1)} %get-tuple-element.53.own_ref, bf16[240,128]{1,0:T(8,128)(2,1)S(1)} %collective-permute-done.2.inner_ref, ...), custom_call_target="tpu_custom_call" | custom-call | tf_op jit(solution)/shard_map/pallas_call | solution.py:366
  15.6 0.6 collective-permute-start.3
  16.2 0.0 collective-permute-start
  16.2 6.9 %collective-permute-done.outer2_ref = bf16[240,128]{1,0:T(8,128)(2,1)S(1)} collective-permute-done((bf16[240,128]{1,0:T(8,128)(2,1)S(1)}, bf16[240,128]{1,0:T(8,128)(2,1)S(1)}, u32[]{:S(2)}, u32[]{:S(2)}) %collective-permute-start) | collective-permute-done | bytes 61472 | tf_op jit(solution)/shard_map/ppermute | solution.py:290
  23.1 3.5 %shard_map.151.kept_ref = f32[240,128]{1,0:T(8,128)S(1)} custom-call(bf16[240,128]{1,0:T(8,128)(2,1)S(1)} %collective-permute-done.outer2_ref, bf16[432,2048]{1,0:T(8,128)(2,1)S(1)} %get-tuple-element.58.features_ref, f32[240,128]{1,0:T(8,128)S(1)} %get-tuple-element.59.kept_in_ref, bf16[256,432]{1,0:T(8,128)(2,1)S(1)} %get-tuple-element.60.forward_ref, ...), custom_call_target="tpu_custom_call" | custom-call | tf_op jit(solution)/shard_map/pallas_call | solution.py:372
  26.6 0.0 collective-permute-done.3.came_ref
  26.6 1.0 %shard_map.152 = (f32[240,128]{1,0:T(8,128)}, bf16[240,128]{1,0:T(8,128)(2,1)S(1)}, f32[240,128]{1,0:T(8,128)S(1)}) custom-call(f32[240,128]{1,0:T(8,128)S(1)} %get-tuple-element.51.q_base_ref, f32[240,240]{1,0:T(8,128)S(1)} %get-tuple-element.52.q_map_ref, f32[240,128]{1,0:T(8,128)S(1)} %shard_map.151.kept_ref, f32[240,128]{1,0:T(8,128)S(1)} %collective-permute-done.3.came_ref), custom_call_target="tpu_custom_call" | custom-call | tf_op jit(solution)/shard_map/pallas_call | solution.py:379
  27.6 0.7 %collective-permute-start.5 = (bf16[240,128]{1,0:T(8,128)(2,1)S(1)}, bf16[240,128]{1,0:T(8,128)(2,1)S(1)}, u32[]{:S(2)}, u32[]{:S(2)}) collective-permute-start(bf16[240,128]{1,0:T(8,128)(2,1)S(1)} %get-tuple-element.73.own_ref), channel_id=1, source_target_pairs={{0,15},{1,2},{2,1},{3,4},{4,3},{5,6},{6,5},{7,8},{8,7},{9,10},{10,... | collective-permute-start | bytes 184328 | tf_op jit(solution)/shard_map/ppermute | solution.py:288
  28.3 0.0 collective-permute-start.6
  28.3 5.7 %collective-permute-done.5.outer_ref = bf16[240,128]{1,0:T(8,128)(2,1)S(1)} collective-permute-done((bf16[240,128]{1,0:T(8,128)(2,1)S(1)}, bf16[240,128]{1,0:T(8,128)(2,1)S(1)}, u32[]{:S(2)}, u32[]{:S(2)}) %collective-permute-start.5) | collective-permute-done | bytes 61472 | tf_op jit(solution)/shard_map/ppermute | solution.py:288
  34.0 0.0 collective-permute-done.6.inner_ref
  34.0 3.9 %shard_map.154 = (f32[240,128]{1,0:T(8,128)S(1)}, f32[240,128]{1,0:T(8,128)S(1)}, bf16[432,2048]{1,0:T(8,128)(2,1)S(1)}) custom-call(bf16[240,128]{1,0:T(8,128)(2,1)S(1)} %collective-permute-done.5.outer_ref, bf16[240,128]{1,0:T(8,128)(2,1)S(1)} %get-tuple-element.73.own_ref, bf16[240,128]{1,0:T(8,128)(2,1)S(1)} %collective-permute-done.6.inner_ref, ...), custom_call_target="tpu_custom_call" | custom-call | tf_op jit(solution)/shard_map/pallas_call | solution.py:366
  37.9 0.1 collective-permute-start.7
  38.0 0.2 collective-permute-start.4
  38.2 1.6 %shard_map.153 = (f32[240,128]{1,0:T(8,128)S(1)}, f32[240,128]{1,0:T(8,128)S(1)}, f32[240,240]{1,0:T(8,128)S(1)}, f32[2,16,256]{2,1,0:T(8,128)S(1)}, f32[2,128,256]{2,1,0:T(8,128)S(1)}) custom-call(f32[8,128]{1,0:T(8,128)S(1)} %get-tuple-element.63.half_ref, f32[240,128]{1,0:T(8,128)S(1)} %get-tuple-element.64.sum_ref, ...), custom_call_target="tpu_custom_call" | custom-call | tf_op jit(solution)/shard_map/pallas_call | solution.py:383
  39.8 5.3 %collective-permute-done.4.outer2_ref = bf16[240,128]{1,0:T(8,128)(2,1)S(1)} collective-permute-done((bf16[240,128]{1,0:T(8,128)(2,1)S(1)}, bf16[240,128]{1,0:T(8,128)(2,1)S(1)}, u32[]{:S(2)}, u32[]{:S(2)}) %collective-permute-start.4) | collective-permute-done | bytes 61472 | tf_op jit(solution)/shard_map/ppermute | solution.py:290
  45.1 3.5 %shard_map.155.kept_ref = f32[240,128]{1,0:T(8,128)S(1)} custom-call(bf16[240,128]{1,0:T(8,128)(2,1)S(1)} %collective-permute-done.4.outer2_ref, bf16[432,2048]{1,0:T(8,128)(2,1)S(1)} %get-tuple-element.74.features_ref, f32[240,128]{1,0:T(8,128)S(1)} %get-tuple-element.75.kept_in_ref, bf16[256,432]{1,0:T(8,128)(2,1)S(1)} %get-tuple-element.60.forward_ref, ...), custom_call_target="tpu_custom_call" | custom-call | tf_op jit(solution)/shard_map/pallas_call | solution.py:372
  48.6 0.0 collective-permute-done.7.came_ref
  48.6 0.4 shard_map.156
  49.0 0.1 collective-permute-start.8
  49.1 5.2 %collective-permute-done.8 = bf16[1,240,128]{2,1,0:T(8,128)(2,1)S(1)} collective-permute-done((bf16[1,240,128]{2,1,0:T(8,128)(2,1)S(1)}, bf16[1,240,128]{2,1,0:T(8,128)(2,1)S(1)}, u32[]{:S(2)}, u32[]{:S(2)}) %collective-permute-start.8) | collective-permute-done | bytes 61472 | tf_op jit(solution)/shard_map/ppermute | solution.py:282
  54.3 0.1 collective-permute-start.9
  54.4 0.1 collective-permute-start.10
  54.5 4.7 %collective-permute-done.9 = bf16[2,240,128]{2,1,0:T(8,128)(2,1)S(1)} collective-permute-done((bf16[2,240,128]{2,1,0:T(8,128)(2,1)S(1)}, bf16[2,240,128]{2,1,0:T(8,128)(2,1)S(1)}, u32[]{:S(2)}, u32[]{:S(2)}) %collective-permute-start.9) | collective-permute-done | bytes 122912 | tf_op jit(solution)/shard_map/ppermute | solution.py:282
  59.3 0.0 collective-permute-start.11
  59.3 0.0 collective-permute-done.10
  59.4 4.7 %collective-permute-done.11 = bf16[2,240,128]{2,1,0:T(8,128)(2,1)S(1)} collective-permute-done((bf16[2,240,128]{2,1,0:T(8,128)(2,1)S(1)}, bf16[2,240,128]{2,1,0:T(8,128)(2,1)S(1)}, u32[]{:S(2)}, u32[]{:S(2)}) %collective-permute-start.11) | collective-permute-done | bytes 122912 | tf_op jit(solution)/shard_map/ppermute | solution.py:282
  64.2 0.1 collective-permute-start.12
  64.3 0.7 sub.3
  64.9 1.2 %collective-permute-done.12 = bf16[8,240,128]{2,1,0:T(8,128)(2,1)S(1)} collective-permute-done((bf16[8,240,128]{2,1,0:T(8,128)(2,1)S(1)}, bf16[8,240,128]{2,1,0:T(8,128)(2,1)S(1)}, u32[]{:S(2)}, u32[]{:S(2)}) %collective-permute-start.12) | collective-permute-done | bytes 491552 | tf_op jit(solution)/shard_map/ppermute | solution.py:282
  66.1 0.1 constant_dynamic-update-slice_fusion.5.velocity_ref
  66.2 1.5 %shard_map.157 = f32[480,256]{1,0:T(8,128)} custom-call(bf16[16,240,128]{2,1,0:T(8,128)(2,1)S(1)} %constant_dynamic-update-slice_fusion.5.velocity_ref, f32[2,16,256]{2,1,0:T(8,128)S(1)} %get-tuple-element.79.planes_ref, f32[2,128,256]{2,1,0:T(8,128)S(1)} %get-tuple-element.80.cells_ref), custom_call_target="tpu_custom_call" | custom-call | tf_op jit(solution)/shard_map/pallas_call | solution.py:392
  (6 shorter events, 0.2 us)
Async XLA Ops:
  2.1 9.6 %collective-permute-start.1 = (bf16[240,128]{1,0:T(8,128)(2,1)S(1)}, bf16[240,128]{1,0:T(8,128)(2,1)S(1)}, u32[]{:S(2)}, u32[]{:S(2)}) collective-permute-start(bf16[240,128]{1,0:T(8,128)(2,1)S(1)} %get-tuple-element.53.own_ref), channel_id=1, source_target_pairs={{0,15},{1,2},{2,1},{3,4},{4,3},{5,6},{6,5},{7,8},{8,7},{9,10},{10,... | collective-permute-start | bytes 184328 | tf_op jit(solution)/shard_map/ppermute | solution.py:288
  7.6 4.1 %collective-permute-start.2 = (bf16[240,128]{1,0:T(8,128)(2,1)S(1)}, bf16[240,128]{1,0:T(8,128)(2,1)S(1)}, u32[]{:S(2)}, u32[]{:S(2)}) collective-permute-start(bf16[240,128]{1,0:T(8,128)(2,1)S(1)} %get-tuple-element.53.own_ref), channel_id=1, source_target_pairs={{0,1},{1,0},{2,3},{3,2},{4,5},{5,4},{6,7},{7,6},{8,9},{9,8},{10,11... | collective-permute-start | bytes 184328 | tf_op jit(solution)/shard_map/ppermute | solution.py:282
  15.6 11.0 %collective-permute-start.3 = (f32[240,128]{1,0:T(8,128)S(1)}, f32[240,128]{1,0:T(8,128)S(1)}, u32[]{:S(2)}, u32[]{:S(2)}) collective-permute-start(f32[240,128]{1,0:T(8,128)S(1)} %get-tuple-element.61), channel_id=1, source_target_pairs={{0,1},{1,0},{2,3},{3,2},{4,5},{5,4},{6,7},{7,6},{8,9},{9,8},{10,11... | collective-permute-start | bytes 368648 | tf_op jit(solution)/shard_map/ppermute | solution.py:282
  16.2 6.9 %collective-permute-start = (bf16[240,128]{1,0:T(8,128)(2,1)S(1)}, bf16[240,128]{1,0:T(8,128)(2,1)S(1)}, u32[]{:S(2)}, u32[]{:S(2)}) collective-permute-start(bf16[240,128]{1,0:T(8,128)(2,1)S(1)} %get-tuple-element.53.own_ref), channel_id=1, source_target_pairs={{0,2},{1,15},{2,4},{3,1},{4,6},{5,3},{6,8},{7,5},{8,10},{9,7},{10,... | collective-permute-start | bytes 184328 | tf_op jit(solution)/shard_map/ppermute | solution.py:290
  27.6 6.3 %collective-permute-start.5 = (bf16[240,128]{1,0:T(8,128)(2,1)S(1)}, bf16[240,128]{1,0:T(8,128)(2,1)S(1)}, u32[]{:S(2)}, u32[]{:S(2)}) collective-permute-start(bf16[240,128]{1,0:T(8,128)(2,1)S(1)} %get-tuple-element.73.own_ref), channel_id=1, source_target_pairs={{0,15},{1,2},{2,1},{3,4},{4,3},{5,6},{6,5},{7,8},{8,7},{9,10},{10,... | collective-permute-start | bytes 184328 | tf_op jit(solution)/shard_map/ppermute | solution.py:288
  28.3 5.7 %collective-permute-start.6 = (bf16[240,128]{1,0:T(8,128)(2,1)S(1)}, bf16[240,128]{1,0:T(8,128)(2,1)S(1)}, u32[]{:S(2)}, u32[]{:S(2)}) collective-permute-start(bf16[240,128]{1,0:T(8,128)(2,1)S(1)} %get-tuple-element.73.own_ref), channel_id=1, source_target_pairs={{0,1},{1,0},{2,3},{3,2},{4,5},{5,4},{6,7},{7,6},{8,9},{9,8},{10,11... | collective-permute-start | bytes 184328 | tf_op jit(solution)/shard_map/ppermute | solution.py:282
  37.9 10.7 %collective-permute-start.7 = (f32[240,128]{1,0:T(8,128)S(1)}, f32[240,128]{1,0:T(8,128)S(1)}, u32[]{:S(2)}, u32[]{:S(2)}) collective-permute-start(f32[240,128]{1,0:T(8,128)S(1)} %get-tuple-element.76), channel_id=1, source_target_pairs={{0,1},{1,0},{2,3},{3,2},{4,5},{5,4},{6,7},{7,6},{8,9},{9,8},{10,11... | collective-permute-start | bytes 368648 | tf_op jit(solution)/shard_map/ppermute | solution.py:282
  38.0 7.2 %collective-permute-start.4 = (bf16[240,128]{1,0:T(8,128)(2,1)S(1)}, bf16[240,128]{1,0:T(8,128)(2,1)S(1)}, u32[]{:S(2)}, u32[]{:S(2)}) collective-permute-start(bf16[240,128]{1,0:T(8,128)(2,1)S(1)} %get-tuple-element.73.own_ref), channel_id=1, source_target_pairs={{0,2},{1,15},{2,4},{3,1},{4,6},{5,3},{6,8},{7,5},{8,10},{9,7},{10,... | collective-permute-start | bytes 184328 | tf_op jit(solution)/shard_map/ppermute | solution.py:290
  49.0 5.3 %collective-permute-start.8 = (bf16[1,240,128]{2,1,0:T(8,128)(2,1)S(1)}, bf16[1,240,128]{2,1,0:T(8,128)(2,1)S(1)}, u32[]{:S(2)}, u32[]{:S(2)}) collective-permute-start(bf16[1,240,128]{2,1,0:T(8,128)(2,1)S(1)} %bitcast.16), channel_id=1, source_target_pairs={{0,8},{1,9},{2,10},{3,11},{4,12},{5,13},{6,14},{7,15},{8,0},{9,1},... | collective-permute-start | bytes 184328 | tf_op jit(solution)/shard_map/ppermute | solution.py:282
  54.3 4.9 %collective-permute-start.9 = (bf16[2,240,128]{2,1,0:T(8,128)(2,1)S(1)}, bf16[2,240,128]{2,1,0:T(8,128)(2,1)S(1)}, u32[]{:S(2)}, u32[]{:S(2)}) collective-permute-start(bf16[2,240,128]{2,1,0:T(8,128)(2,1)S(1)} %pad_maximum_fusion), channel_id=1, source_target_pairs={{0,2},{1,3},{2,0},{3,1},{4,6},{5,7},{6,4},{7,5},{8,10},{9,11},{10,... | collective-permute-start | bytes 368648 | tf_op jit(solution)/shard_map/ppermute | solution.py:282
  54.4 4.9 %collective-permute-start.10 = (bf16[2,240,128]{2,1,0:T(8,128)(2,1)S(1)}, bf16[2,240,128]{2,1,0:T(8,128)(2,1)S(1)}, u32[]{:S(2)}, u32[]{:S(2)}) collective-permute-start(bf16[2,240,128]{2,1,0:T(8,128)(2,1)S(1)} %pad_maximum_fusion), channel_id=1, source_target_pairs={{0,4},{1,5},{2,6},{3,7},{4,0},{5,1},{6,2},{7,3},{8,12},{9,13},{10,... | collective-permute-start | bytes 368648 | tf_op jit(solution)/shard_map/ppermute | solution.py:282
  59.3 4.9 %collective-permute-start.11 = (bf16[2,240,128]{2,1,0:T(8,128)(2,1)S(1)}, bf16[2,240,128]{2,1,0:T(8,128)(2,1)S(1)}, u32[]{:S(2)}, u32[]{:S(2)}) collective-permute-start(bf16[2,240,128]{2,1,0:T(8,128)(2,1)S(1)} %collective-permute-done.9), channel_id=1, source_target_pairs={{0,4},{1,5},{2,6},{3,7},{4,0},{5,1},{6,2},{7,3},{8,12},{9,13},{10,... | collective-permute-start | bytes 368648 | tf_op jit(solution)/shard_map/ppermute | solution.py:282
  64.2 1.9 %collective-permute-start.12 = (bf16[8,240,128]{2,1,0:T(8,128)(2,1)S(1)}, bf16[8,240,128]{2,1,0:T(8,128)(2,1)S(1)}, u32[]{:S(2)}, u32[]{:S(2)}) collective-permute-start(bf16[8,240,128]{2,1,0:T(8,128)(2,1)S(1)} %get-tuple-element.84), channel_id=1, source_target_pairs={{0,1},{1,0},{2,3},{3,2},{4,5},{5,4},{6,7},{7,6},{8,9},{9,8},{10,11... | collective-permute-start | bytes 1474568 | tf_op jit(solution)/shard_map/ppermute | solution.py:282
where the time goes:
time: 67.9 us; the launch traced here: 67.7 us
  waiting for transfers between devices  33.8 us (50%)
  Pallas kernels  23.5 us (35%)
  starting transfers between devices  7.39 us (11%)
  between operations  2.11 us (3%)
  other arithmetic  0.68 us (1%)
    ppermute x9, waiting for transfers between devices, swap(): lax.ppermute(value, 'space', [(i, i ^ distance) for i in range(lax.axis_s...  15.9 us
    ppermute x2, waiting for transfers between devices, neighbour_planes(): lax.ppermute(plane, 'space', [(i, (i - 2 * step[i]) % count) for i in ran...  12.3 us
    pallas_call x2, Pallas kernels, forces(): call(functools.partial(own_kernel, coords, beads, len(tied)), out_shape=(...  7.81 us
    pallas_call x2, Pallas kernels, forces(): call(functools.partial(outer_kernel, coords, beads), out_shape=field, in_...  6.99 us
    ppermute x2, starting transfers between devices, neighbour_planes(): lax.ppermute(plane, 'space', [(i, (i + step[i]) % count) for i in range(c...  6.22 us
    ppermute x2, waiting for transfers between devices, neighbour_planes(): lax.ppermute(plane, 'space', [(i, (i + step[i]) % count) for i in range(c...  5.66 us
    pallas_call x1, Pallas kernels, on_device(): call(functools.partial(setup_kernel, coords, beads), out_shape=(shape((hi...  2.74 us
    pallas_call x1, Pallas kernels, on_device(): call(functools.partial(push_kernel, share, order), out_shape=(field, fiel...  1.56 us
  transfers between devices with their start and end apart: 13, of which 7 were waited for; matrix products, arithmetic and copies ran while one was open for 1% of the time, Pallas kernels for 17%

commit v1 on v0

--- a/solution.py
+++ b/solution.py
@@ -16,7 +16,8 @@
 PAD = 16
 BLOCK = 9 * PAD
 DEPTH = 256
-GROUP = 4
+SIZES = (8,8,)
+SKEW = 1
 SHIFTS = [(b, d) for b in (-1, 0, 1) for d in (-1, 0, 1)]
 HIGHEST = lax.Precision.HIGHEST
 TWO_PI = 6.283185307179586
@@ -55,31 +56,31 @@
     return lax.broadcasted_iota(jnp.int32, (rows, CELLS), 1) % NZ
 
 
-def load_kernel(*refs):
-    count = (len(refs) - 2) // 2
-    sources, rounded_ref, targets, semaphores = refs[:count], refs[count], refs[count + 1 : -1], refs[-1]
-    copies = [pltpu.make_async_copy(a, b, semaphores.at[i]) for i, (a, b) in enumerate(zip(sources, targets))]
+def round_kernel(q_hbm, rounded_ref, q_ref, semaphore):
+    copy = pltpu.make_async_copy(q_hbm, q_ref, semaphore)
+    copy.start()
+    copy.wait()
+    rounded_ref[...] = q_ref[...].astype(bf16)
+
+
+def setup_kernel(
+    coords, beads, masses_hbm, step_hbm, cycle_hbm, one_hbm, bias_one_hbm, bias_two_hbm, readout_hbm, p_hbm,
+    two_hbm, modes_hbm, modes_t_hbm, vectors_hbm, q_ref,
+    forward_ref, outer_forward_ref, backward_ref, two_t_ref, wide_ref,
+    q_base_ref, q_map_ref, p_base_ref, pushed_ref, cosine_ref, finish_ref, half_ref,
+    two_ref, modes_ref, modes_t_ref, vectors_ref,
+    rows, masses_ref, step_ref, cycle_ref, one_ref, bias_one_ref, bias_two_ref, readout_ref, p_ref, semaphores
+):
+    moves = (
+        (one_hbm, one_ref), (bias_one_hbm, bias_one_ref), (bias_two_hbm, bias_two_ref), (readout_hbm, readout_ref),
+        (two_hbm, two_ref), (masses_hbm, masses_ref), (step_hbm, step_ref), (cycle_hbm, cycle_ref),
+        (p_hbm, p_ref), (modes_hbm, modes_ref), (modes_t_hbm, modes_t_ref), (vectors_hbm, vectors_ref),
+    )
+    copies = [pltpu.make_async_copy(a, b, semaphores.at[i]) for i, (a, b) in enumerate(moves)]
     for copy in copies:
         copy.start()
-    copies[0].wait()
-    rounded_ref[...] = targets[0][...].astype(bf16)
-    for copy in copies[1:]:
+    for copy in copies[:5]:
         copy.wait()
-
-
-def setup_kernel(
-    coords, beads, masses_hbm, step_hbm, cycle_hbm, one_ref, bias_one_ref, two_ref, bias_two_ref, readout_ref,
-    q_ref, p_ref, modes_ref, modes_t_ref, forward_ref, outer_forward_ref, backward_ref, two_t_ref, wide_ref,
-    q_base_ref, q_map_ref, p_base_ref, pushed_ref, cosine_ref, finish_ref, half_ref,
-    rows, masses_ref, step_ref, cycle_ref, semaphores
-):
-    copies = [
-        pltpu.make_async_copy(masses_hbm, masses_ref, semaphores.at[0]),
-        pltpu.make_async_copy(step_hbm, step_ref, semaphores.at[1]),
-        pltpu.make_async_copy(cycle_hbm, cycle_ref, semaphores.at[2]),
-    ]
-    for copy in copies:
-        copy.start()
     is_odd = lax.axis_index("space") % 2 == 1
     hidden = one_ref.shape[1]
     rows[: one_ref.shape[0], :] = one_ref[...].astype(f32)
@@ -111,18 +112,20 @@
     for i in range(2):
         wide_ref[i] = jnp.broadcast_to(columns[:, i : i + 1], (hidden, CELLS))
 
-    for copy in copies:
+    for copy in copies[5:]:
         copy.wait()
-    total = coords * beads
-    order = (lax.broadcasted_iota(jnp.int32, (total, CELLS), 0) % beads).astype(f32)
+    order = lax.broadcasted_iota(jnp.int32, (beads, CELLS), 0).astype(f32)
     mass = jnp.concatenate([jnp.full((beads, CELLS), masses_ref[c], f32) for c in range(coords)])
     step = step_ref[0]
     half = 0.5 * step
     frequency = 2.0 * cycle_ref[0] * jnp.sin(order * (0.5 * TWO_PI / beads))
     phase = frequency * step
-    cosine, sine = jnp.cos(phase), jnp.sin(phase)
-    drift = step * jnp.where(order == 0, 1.0, sine / jnp.where(order == 0, 1.0, phase)) / mass
-    spring = mass * frequency * sine
+    sine = jnp.sin(phase)
+    ratio = jnp.where(order == 0, 1.0, sine / jnp.where(order == 0, 1.0, phase))
+    cosine, drift, spring = (
+        jnp.concatenate([term] * coords) for term in (jnp.cos(phase), step * ratio, frequency * sine)
+    )
+    drift, spring = drift / mass, mass * spring
     mode = exact_dot(modes_t_ref[...], jnp.concatenate([q_ref[...], p_ref[...]], axis=1))
     mode_q, mode_p = mode[:, :CELLS], mode[:, CELLS:]
     moved = cosine * mode_q + drift * mode_p
@@ -137,29 +140,46 @@
     half_ref[...] = jnp.full(half_ref.shape, half, f32)
 
 
-def put_features(coords, beads, plane_ref, stage, features, top):
-    stage[...] = plane_ref[...].astype(f32)
+def put_features(coords, beads, chosen, stage, features, top):
     filler = jnp.ones((PAD - coords, CELLS), f32)
-    pieces = []
-    for j in range(beads):
-        pieces += [stage[pl.ds(j, coords, stride=beads), :], filler]
-    plane = jnp.concatenate(pieces)
-    inner_z = z_index(beads * PAD)
-    along = {d: shift_z(plane, d, inner_z) for d in (-1, 0, 1)}
-    for o, (b, d) in enumerate(SHIFTS):
-        moved = shift_y(along[d], b).astype(bf16)
-        first = top + o * PAD
-        for j in range(beads):
-            features[first : first + PAD, j * CELLS : (j + 1) * CELLS] = moved[j * PAD : (j + 1) * PAD]
-
-
-def back_one(first, two_ref, two_t_ref, wide_ref):
-    bias, readout = (jnp.concatenate([wide_ref[i]] * GROUP, axis=1) for i in range(2))
-    hidden = jnp.tanh(first).astype(bf16)
-    second = jnp.tanh(dot(two_ref[...], hidden) + bias)
-    back = (readout * (1.0 - second * second)).astype(bf16)
-    widened = hidden.astype(f32)
-    return (dot(two_t_ref[...], back) * (1.0 - widened * widened)).astype(bf16)
+    inner_z = z_index(PAD)
+    for j in chosen:
+        plane = jnp.concatenate([stage[pl.ds(j, coords, stride=beads), :], filler]).astype(bf16)
+        along = {d: shift_z(plane, d, inner_z) for d in (-1, 0, 1)}
+        for o, (b, d) in enumerate(SHIFTS):
+            first = top + o * PAD
+            features[first : first + PAD, j * CELLS : (j + 1) * CELLS] = shift_y(along[d], b)
+
+
+def groups_of(beads):
+    sizes = SIZES if sum(SIZES) == beads else (beads,)
+    starts = np.cumsum((0,) + sizes)
+    return [range(int(first), int(first) + size) for first, size in zip(starts, sizes)]
+
+
+def columns_of(chosen):
+    return slice(chosen[0] * CELLS, (chosen[-1] + 1) * CELLS)
+
+
+def run_skewed(groups, stages):
+    state = [() for _ in groups]
+    order = sorted((SKEW * g + s, -s, g) for g in range(len(groups)) for s in range(len(stages)))
+    for _, s, g in order:
+        state[g] = stages[-s](groups[g], *state[g])
+
+
+def back_stages(two_ref, two_t_ref, wide_ref):
+    def second(chosen, first):
+        bias, readout = (jnp.concatenate([wide_ref[i]] * len(chosen), axis=1) for i in range(2))
+        hidden = jnp.tanh(first).astype(bf16)
+        second = jnp.tanh(dot(two_ref[...], hidden) + bias)
+        return hidden, (readout * (1.0 - second * second)).astype(bf16)
+
+    def third(chosen, hidden, back):
+        widened = hidden.astype(f32)
+        return ((dot(two_t_ref[...], back) * (1.0 - widened * widened)).astype(bf16),)
+
+    return second, third
 
 
 def shifted_sum(sums, at):
@@ -181,15 +201,26 @@
 ):
     sent_ref, kept_ref, features, stage = refs[tied:]
     for place, ref in enumerate((outer_ref, own_ref, inner_ref)):
-        put_features(coords, beads, ref, stage, features, place * BLOCK)
-    for first in range(0, beads, GROUP):
-        columns = slice(first * CELLS, (first + GROUP) * CELLS)
-        back = back_one(dot(forward_ref[...], features[:, columns]), two_ref, two_t_ref, wide_ref)
-        sums = dot(backward_ref[BLOCK:], back)
-        for at in range(GROUP):
-            rows = pl.ds(first + at, coords, stride=beads)
+        stage[place] = ref[...].astype(f32)
+
+    def put(chosen):
+        for place in range(3):
+            put_features(coords, beads, chosen, stage.at[place], features, place * BLOCK)
+        return ()
+
+    def first(chosen):
+        return (dot(forward_ref[...], features[:, columns_of(chosen)]),)
+
+    def last(chosen, back):
+        return (dot(backward_ref[BLOCK:], back),)
+
+    def store(chosen, sums):
+        for at, j in enumerate(chosen):
+            rows = pl.ds(j, coords, stride=beads)
             kept_ref[rows, :] = shifted_sum(sums[:BLOCK], at)[:coords]
             sent_ref[rows, :] = shifted_sum(sums[BLOCK:], at)[:coords]
+
+    run_skewed(groups_of(beads), (put, first, *back_stages(two_ref, two_t_ref, wide_ref), last, store))
 
 
 def outer_kernel(
@@ -197,16 +228,26 @@
     kept_ref, features, stage
 ):
     extra = 2 * BLOCK - DEPTH
-    put_features(coords, beads, outer2_ref, stage, features, extra)
-    features[:extra, :] = features_ref[DEPTH : 2 * BLOCK, :]
-    for first in range(0, beads, GROUP):
-        columns = slice(first * CELLS, (first + GROUP) * CELLS)
-        pre = dot(forward_ref[:, :DEPTH], features_ref[:DEPTH, columns])
-        pre = pre + dot(forward_ref[:, DEPTH:], features[:, columns])
-        sums = dot(backward_ref[2 * BLOCK :], back_one(pre, two_ref, two_t_ref, wide_ref))
-        for at in range(GROUP):
-            rows = pl.ds(first + at, coords, stride=beads)
+    stage[...] = outer2_ref[...].astype(f32)
+
+    def put(chosen):
+        put_features(coords, beads, chosen, stage, features, extra)
+        features[:extra, columns_of(chosen)] = features_ref[DEPTH : 2 * BLOCK, columns_of(chosen)]
+        return ()
+
+    def first(chosen):
+        near = dot(forward_ref[:, :DEPTH], features_ref[:DEPTH, columns_of(chosen)])
+        return (near + dot(forward_ref[:, DEPTH:], features[:, columns_of(chosen)]),)
+
+    def last(chosen, back):
+        return (dot(backward_ref[2 * BLOCK :], back),)
+
+    def store(chosen, sums):
+        for at, j in enumerate(chosen):
+            rows = pl.ds(j, coords, stride=beads)
             kept_ref[rows, :] = kept_in_ref[rows, :] + shifted_sum(sums, at)[:coords]
+
+    run_skewed(groups_of(beads), (put, first, *back_stages(two_ref, two_t_ref, wide_ref), last, store))
 
 
 def move_kernel(q_base_ref, q_map_ref, kept_ref, came_ref, q_out, rounded_out, sum_out):
@@ -329,35 +370,33 @@
     share = wavevectors.shape[1] // devices
     if share % CELLS:
         wavevectors = lax.dynamic_slice_in_dim(wavevectors, lax.axis_index("space") * share, share, 1)
+    rounded, q = call(
+        round_kernel, out_shape=(narrow, field), in_specs=[HBM], out_specs=(VMEM,) * 2,
+        scratch_shapes=[pltpu.SemaphoreType.DMA],
+    )(in_hbm(positions.reshape(total, CELLS)))
+
+    row = pltpu.VMEM((1, hidden), f32)
     inputs = (
-        positions.reshape(total, CELLS), momenta.reshape(total, CELLS),
-        layer_one.T, bias_one.reshape(1, hidden), layer_two, bias_two.reshape(1, hidden), readout.reshape(1, hidden),
-        jnp.asarray(modes), jnp.asarray(modes.T), wavevectors,
+        layer_one.T, bias_one.reshape(1, hidden), bias_two.reshape(1, hidden), readout.reshape(1, hidden),
+        momenta.reshape(total, CELLS), layer_two, jnp.asarray(modes), jnp.asarray(modes.T), wavevectors,
     )
-    rounded, q, p, one_t, bias_one, two, bias_two, readout, modes, modes_t, wavevectors = call(
-        load_kernel,
-        out_shape=(narrow,) + tuple(shape(x.shape, x.dtype) for x in inputs),
-        in_specs=[HBM] * len(inputs), out_specs=(VMEM,) * (len(inputs) + 1),
-        scratch_shapes=[pltpu.SemaphoreType.DMA((len(inputs),))],
-    )(*map(in_hbm, inputs))
-
     (
-        forward, outer_forward, backward, two_t, wide, q_base, q_map, p_base, pushed, cosine, finish, half
+        forward, outer_forward, backward, two_t, wide, q_base, q_map, p_base, pushed, cosine, finish, half,
+        two, modes, modes_t, wavevectors
     ) = call(
         functools.partial(setup_kernel, coords, beads),
         out_shape=(
             shape((hidden, width), bf16), shape((hidden, width), bf16), shape((width, hidden), bf16),
             shape((hidden, hidden), bf16), shape((2, hidden, CELLS), f32),
             field, square, field, field, field, shape((total, 2 * CELLS), f32), shape((8, CELLS), f32),
-        ),
-        in_specs=[HBM] * 3 + [VMEM] * 9, out_specs=(VMEM,) * 12,
+        ) + tuple(shape(x.shape, x.dtype) for x in inputs[5:]),
+        in_specs=[HBM] * 12 + [VMEM], out_specs=(VMEM,) * 16,
         scratch_shapes=[
             pltpu.VMEM((width, hidden), f32), pltpu.SMEM((coords,), f32), pltpu.SMEM((1,), f32),
-            pltpu.SMEM((1,), f32), pltpu.SemaphoreType.DMA((3,)),
+            pltpu.SMEM((1,), f32), pltpu.VMEM(inputs[0].shape, bf16), row, row, row,
+            pltpu.VMEM((total, CELLS), f32), pltpu.SemaphoreType.DMA((12,)),
         ],
-    )(
-        in_hbm(masses), step_size, cycle_frequency, one_t, bias_one, two, bias_two, readout, q, p, modes, modes_t
-    )
+    )(in_hbm(masses), step_size, cycle_frequency, *map(in_hbm, inputs), q)
     layers = (backward, two, two_t, wide)
     stage = pltpu.VMEM((total, CELLS), f32)
 
@@ -366,7 +405,7 @@
         sent, kept, features = call(
             functools.partial(own_kernel, coords, beads, len(tied)),
             out_shape=(field, field, shape((width, beads * CELLS), bf16)),
-            in_specs=[VMEM] * (8 + len(tied)), out_specs=(VMEM,) * 3, scratch_shapes=[stage],
+            in_specs=[VMEM] * (8 + len(tied)), out_specs=(VMEM,) * 3, scratch_shapes=[pltpu.VMEM((3, total, CELLS), f32)],
         )(outer, plane, inner, forward, *layers, *tied)
         came = swap(sent, 1)
         kept = call(

time: 67.9 us -> 62.3 us (0.918)
  Pallas kernels: 23.5 us -> 17.8 us
    pallas_call x2, Pallas kernels: 6.99 us -> 4.51 us  [forces(): call(functools.partial(outer_kernel, coords, beads), out_shape=field, in_...]
    pallas_call x2, Pallas kernels: 7.81 us -> 5.33 us  [forces(): call(functools.partial(own_kernel, coords, beads, len(tied)), out_shape=(...]
  transfers between devices with their start and end apart: 13 -> 13, of which waited for: 7 -> 7; matrix products, arithmetic and copies ran while one was open for 1% -> 1% of each run, Pallas kernels for 17% -> 14%
where the time goes in v1:
time: 62.3 us; the launch traced here: 62.1 us
  waiting for transfers between devices  33.7 us (54%)
  Pallas kernels  17.8 us (29%)
  starting transfers between devices  7.5 us (12%)
  between operations  2.1 us (3%)
  other arithmetic  0.68 us (1%)
    ppermute x9, waiting for transfers between devices, swap(): lax.ppermute(value, 'space', [(i, i ^ distance) for i in range(lax.axis_s...  15.9 us
    ppermute x2, waiting for transfers between devices, neighbour_planes(): lax.ppermute(plane, 'space', [(i, (i - 2 * step[i]) % count) for i in ran...  12.3 us
    ppermute x2, starting transfers between devices, neighbour_planes(): lax.ppermute(plane, 'space', [(i, (i + step[i]) % count) for i in range(c...  6.32 us
    ppermute x2, waiting for transfers between devices, neighbour_planes(): lax.ppermute(plane, 'space', [(i, (i + step[i]) % count) for i in range(c...  5.56 us
    pallas_call x2, Pallas kernels, forces(): call(functools.partial(own_kernel, coords, beads, len(tied)), out_shape=(...  5.33 us
    pallas_call x2, Pallas kernels, forces(): call(functools.partial(outer_kernel, coords, beads), out_shape=field, in_...  4.51 us
    pallas_call x1, Pallas kernels, on_device(): call(functools.partial(setup_kernel, coords, beads), out_shape=(shape((hi...  2.62 us
    pallas_call x1, Pallas kernels, on_device(): call(functools.partial(push_kernel, share, order), out_shape=(field, fiel...  1.56 us
  transfers between devices with their start and end apart: 13, of which 7 were waited for; matrix products, arithmetic and copies ran while one was open for 1% of the time, Pallas kernels for 14%

profile of v1, /device:TPU:0, one launch (start us, length us, event | category | flops | bytes accessed | tf_op | source)
XLA Modules:
  0.0 62.1 jit_solution(17493377552436389890)
XLA Ops:
  0.6 0.9 %shard_map.148 = (bf16[240,128]{1,0:T(8,128)(2,1)S(1)}, f32[240,128]{1,0:T(8,128)S(1)}) custom-call(f32[240,128]{1,0:T(8,128)} %bitcast.20), custom_call_target="tpu_custom_call" | custom-call | tf_op jit(solution)/shard_map/pallas_call | solution.py:373
  1.6 5.5 %collective-permute-start.1 = (bf16[240,128]{1,0:T(8,128)(2,1)S(1)}, bf16[240,128]{1,0:T(8,128)(2,1)S(1)}, u32[]{:S(2)}, u32[]{:S(2)}) collective-permute-start(bf16[240,128]{1,0:T(8,128)(2,1)S(1)} %get-tuple-element.40.own_ref), channel_id=1, source_target_pairs={{0,15},{1,2},{2,1},{3,4},{4,3},{5,6},{6,5},{7,8},{8,7},{9,10},{10,... | collective-permute-start | bytes 184328 | tf_op jit(solution)/shard_map/ppermute | solution.py:329
  7.1 0.0 collective-permute-start.2
  8.4 2.6 %shard_map.149 = (bf16[256,432]{1,0:T(8,128)(2,1)S(1)}, bf16[256,432]{1,0:T(8,128)(2,1)S(1)}, bf16[432,256]{1,0:T(8,128)(2,1)S(1)}, bf16[256,256]{1,0:T(8,128)(2...) custom-call(f32[15]{0:T(128)} %masses_hbm.1, ...), custom_call_target="tpu_custom_call" | custom-call | tf_op jit(solution)/shard_map/pallas_call | solution.py:386
  11.0 0.0 collective-permute-done.1.outer_ref
  11.0 0.0 collective-permute-done.2.inner_ref
  11.0 2.7 %shard_map.150 = (f32[240,128]{1,0:T(8,128)S(1)}, f32[240,128]{1,0:T(8,128)S(1)}, bf16[432,2048]{1,0:T(8,128)(2,1)S(1)}) custom-call(bf16[240,128]{1,0:T(8,128)(2,1)S(1)} %collective-permute-done.1.outer_ref, bf16[240,128]{1,0:T(8,128)(2,1)S(1)} %get-tuple-element.40.own_ref, bf16[240,128]{1,0:T(8,128)(2,1)S(1)} %collective-permute-done.2.inner_ref, ...), custom_call_target="tpu_custom_call" | custom-call | tf_op jit(solution)/shard_map/pallas_call | solution.py:405
  13.7 0.6 collective-permute-start.3
  14.3 0.0 collective-permute-start
  14.3 6.9 %collective-permute-done.outer2_ref = bf16[240,128]{1,0:T(8,128)(2,1)S(1)} collective-permute-done((bf16[240,128]{1,0:T(8,128)(2,1)S(1)}, bf16[240,128]{1,0:T(8,128)(2,1)S(1)}, u32[]{:S(2)}, u32[]{:S(2)}) %collective-permute-start) | collective-permute-done | bytes 61472 | tf_op jit(solution)/shard_map/ppermute | solution.py:331
  21.2 2.3 %shard_map.151.kept_ref = f32[240,128]{1,0:T(8,128)S(1)} custom-call(bf16[240,128]{1,0:T(8,128)(2,1)S(1)} %collective-permute-done.outer2_ref, bf16[432,2048]{1,0:T(8,128)(2,1)S(1)} %get-tuple-element.46.features_ref, f32[240,128]{1,0:T(8,128)S(1)} %get-tuple-element.47.kept_in_ref, bf16[256,432]{1,0:T(8,128)(2,1)S(1)} %get-tuple-element.48.forward_ref, ...), custom_call_target="tpu_custom_call" | custom-call | tf_op jit(solution)/shard_map/pallas_call | solution.py:411
  23.5 0.0 collective-permute-done.3.came_ref
  23.5 1.0 %shard_map.152 = (f32[240,128]{1,0:T(8,128)}, bf16[240,128]{1,0:T(8,128)(2,1)S(1)}, f32[240,128]{1,0:T(8,128)S(1)}) custom-call(f32[240,128]{1,0:T(8,128)S(1)} %get-tuple-element.38.q_base_ref, f32[240,240]{1,0:T(8,128)S(1)} %get-tuple-element.39.q_map_ref, f32[240,128]{1,0:T(8,128)S(1)} %shard_map.151.kept_ref, f32[240,128]{1,0:T(8,128)S(1)} %collective-permute-done.3.came_ref), custom_call_target="tpu_custom_call" | custom-call | tf_op jit(solution)/shard_map/pallas_call | solution.py:418
  24.5 0.8 %collective-permute-start.5 = (bf16[240,128]{1,0:T(8,128)(2,1)S(1)}, bf16[240,128]{1,0:T(8,128)(2,1)S(1)}, u32[]{:S(2)}, u32[]{:S(2)}) collective-permute-start(bf16[240,128]{1,0:T(8,128)(2,1)S(1)} %get-tuple-element.63.own_ref), channel_id=1, source_target_pairs={{0,15},{1,2},{2,1},{3,4},{4,3},{5,6},{6,5},{7,8},{8,7},{9,10},{10,... | collective-permute-start | bytes 184328 | tf_op jit(solution)/shard_map/ppermute | solution.py:329
  25.3 0.0 collective-permute-start.6
  25.3 5.6 %collective-permute-done.5.outer_ref = bf16[240,128]{1,0:T(8,128)(2,1)S(1)} collective-permute-done((bf16[240,128]{1,0:T(8,128)(2,1)S(1)}, bf16[240,128]{1,0:T(8,128)(2,1)S(1)}, u32[]{:S(2)}, u32[]{:S(2)}) %collective-permute-start.5) | collective-permute-done | bytes 61472 | tf_op jit(solution)/shard_map/ppermute | solution.py:329
  30.9 0.0 collective-permute-done.6.inner_ref
  30.9 2.7 %shard_map.154 = (f32[240,128]{1,0:T(8,128)S(1)}, f32[240,128]{1,0:T(8,128)S(1)}, bf16[432,2048]{1,0:T(8,128)(2,1)S(1)}) custom-call(bf16[240,128]{1,0:T(8,128)(2,1)S(1)} %collective-permute-done.5.outer_ref, bf16[240,128]{1,0:T(8,128)(2,1)S(1)} %get-tuple-element.63.own_ref, bf16[240,128]{1,0:T(8,128)(2,1)S(1)} %collective-permute-done.6.inner_ref, ...), custom_call_target="tpu_custom_call" | custom-call | tf_op jit(solution)/shard_map/pallas_call | solution.py:405
  33.5 0.1 collective-permute-start.7
  33.6 0.2 collective-permute-start.4
  33.9 1.6 %shard_map.153 = (f32[240,128]{1,0:T(8,128)S(1)}, f32[240,128]{1,0:T(8,128)S(1)}, f32[240,240]{1,0:T(8,128)S(1)}, f32[2,16,256]{2,1,0:T(8,128)S(1)}, f32[2,128,256]{2,1,0:T(8,128)S(1)}) custom-call(f32[8,128]{1,0:T(8,128)S(1)} %get-tuple-element.51.half_ref, f32[240,128]{1,0:T(8,128)S(1)} %get-tuple-element.52.sum_ref, ...), custom_call_target="tpu_custom_call" | custom-call | tf_op jit(solution)/shard_map/pallas_call | solution.py:422
  35.4 5.3 %collective-permute-done.4.outer2_ref = bf16[240,128]{1,0:T(8,128)(2,1)S(1)} collective-permute-done((bf16[240,128]{1,0:T(8,128)(2,1)S(1)}, bf16[240,128]{1,0:T(8,128)(2,1)S(1)}, u32[]{:S(2)}, u32[]{:S(2)}) %collective-permute-start.4) | collective-permute-done | bytes 61472 | tf_op jit(solution)/shard_map/ppermute | solution.py:331
  40.8 2.2 %shard_map.155.kept_ref = f32[240,128]{1,0:T(8,128)S(1)} custom-call(bf16[240,128]{1,0:T(8,128)(2,1)S(1)} %collective-permute-done.4.outer2_ref, bf16[432,2048]{1,0:T(8,128)(2,1)S(1)} %get-tuple-element.64.features_ref, f32[240,128]{1,0:T(8,128)S(1)} %get-tuple-element.65.kept_in_ref, bf16[256,432]{1,0:T(8,128)(2,1)S(1)} %get-tuple-element.48.forward_ref, ...), custom_call_target="tpu_custom_call" | custom-call | tf_op jit(solution)/shard_map/pallas_call | solution.py:411
  43.0 0.0 collective-permute-done.7.came_ref
  43.0 0.4 shard_map.156
  43.4 0.1 collective-permute-start.8
  43.5 5.2 %collective-permute-done.8 = bf16[1,240,128]{2,1,0:T(8,128)(2,1)S(1)} collective-permute-done((bf16[1,240,128]{2,1,0:T(8,128)(2,1)S(1)}, bf16[1,240,128]{2,1,0:T(8,128)(2,1)S(1)}, u32[]{:S(2)}, u32[]{:S(2)}) %collective-permute-start.8) | collective-permute-done | bytes 61472 | tf_op jit(solution)/shard_map/ppermute | solution.py:323
  48.7 0.1 collective-permute-start.9
  48.8 0.1 collective-permute-start.10
  48.9 4.7 %collective-permute-done.9 = bf16[2,240,128]{2,1,0:T(8,128)(2,1)S(1)} collective-permute-done((bf16[2,240,128]{2,1,0:T(8,128)(2,1)S(1)}, bf16[2,240,128]{2,1,0:T(8,128)(2,1)S(1)}, u32[]{:S(2)}, u32[]{:S(2)}) %collective-permute-start.9) | collective-permute-done | bytes 122912 | tf_op jit(solution)/shard_map/ppermute | solution.py:323
  53.6 0.0 collective-permute-start.11
  53.7 0.0 collective-permute-done.10
  53.8 4.7 %collective-permute-done.11 = bf16[2,240,128]{2,1,0:T(8,128)(2,1)S(1)} collective-permute-done((bf16[2,240,128]{2,1,0:T(8,128)(2,1)S(1)}, bf16[2,240,128]{2,1,0:T(8,128)(2,1)S(1)}, u32[]{:S(2)}, u32[]{:S(2)}) %collective-permute-start.11) | collective-permute-done | bytes 122912 | tf_op jit(solution)/shard_map/ppermute | solution.py:323
  58.6 0.1 collective-permute-start.12
  58.7 0.7 %sub.3 = f32[240,128]{1,0:T(8,128)} subtract(f32[240,128]{1,0:T(8,128)S(1)} %get-tuple-element.60, f32[240,128]{1,0:T(8,128)S(1)} %get-tuple-element.67) | non-fusion elementwise | flops 30720 | bytes 368640 | tf_op jit(solution)/shard_map/sub | solution.py:430
  59.3 1.2 %collective-permute-done.12 = bf16[8,240,128]{2,1,0:T(8,128)(2,1)S(1)} collective-permute-done((bf16[8,240,128]{2,1,0:T(8,128)(2,1)S(1)}, bf16[8,240,128]{2,1,0:T(8,128)(2,1)S(1)}, u32[]{:S(2)}, u32[]{:S(2)}) %collective-permute-start.12) | collective-permute-done | bytes 491552 | tf_op jit(solution)/shard_map/ppermute | solution.py:323
  60.5 0.1 constant_dynamic-update-slice_fusion.5.velocity_ref
  60.6 1.5 %shard_map.157 = f32[480,256]{1,0:T(8,128)} custom-call(bf16[16,240,128]{2,1,0:T(8,128)(2,1)S(1)} %constant_dynamic-update-slice_fusion.5.velocity_ref, f32[2,16,256]{2,1,0:T(8,128)S(1)} %get-tuple-element.69.planes_ref, f32[2,128,256]{2,1,0:T(8,128)S(1)} %get-tuple-element.70.cells_ref), custom_call_target="tpu_custom_call" | custom-call | tf_op jit(solution)/shard_map/pallas_call | solution.py:431
  (6 shorter events, 0.2 us)
Async XLA Ops:
  1.6 9.5 %collective-permute-start.1 = (bf16[240,128]{1,0:T(8,128)(2,1)S(1)}, bf16[240,128]{1,0:T(8,128)(2,1)S(1)}, u32[]{:S(2)}, u32[]{:S(2)}) collective-permute-start(bf16[240,128]{1,0:T(8,128)(2,1)S(1)} %get-tuple-element.40.own_ref), channel_id=1, source_target_pairs={{0,15},{1,2},{2,1},{3,4},{4,3},{5,6},{6,5},{7,8},{8,7},{9,10},{10,... | collective-permute-start | bytes 184328 | tf_op jit(solution)/shard_map/ppermute | solution.py:329
  7.1 3.9 %collective-permute-start.2 = (bf16[240,128]{1,0:T(8,128)(2,1)S(1)}, bf16[240,128]{1,0:T(8,128)(2,1)S(1)}, u32[]{:S(2)}, u32[]{:S(2)}) collective-permute-start(bf16[240,128]{1,0:T(8,128)(2,1)S(1)} %get-tuple-element.40.own_ref), channel_id=1, source_target_pairs={{0,1},{1,0},{2,3},{3,2},{4,5},{5,4},{6,7},{7,6},{8,9},{9,8},{10,11... | collective-permute-start | bytes 184328 | tf_op jit(solution)/shard_map/ppermute | solution.py:323
  13.7 9.8 %collective-permute-start.3 = (f32[240,128]{1,0:T(8,128)S(1)}, f32[240,128]{1,0:T(8,128)S(1)}, u32[]{:S(2)}, u32[]{:S(2)}) collective-permute-start(f32[240,128]{1,0:T(8,128)S(1)} %get-tuple-element.49), channel_id=1, source_target_pairs={{0,1},{1,0},{2,3},{3,2},{4,5},{5,4},{6,7},{7,6},{8,9},{9,8},{10,11... | collective-permute-start | bytes 368648 | tf_op jit(solution)/shard_map/ppermute | solution.py:323
  14.3 6.9 %collective-permute-start = (bf16[240,128]{1,0:T(8,128)(2,1)S(1)}, bf16[240,128]{1,0:T(8,128)(2,1)S(1)}, u32[]{:S(2)}, u32[]{:S(2)}) collective-permute-start(bf16[240,128]{1,0:T(8,128)(2,1)S(1)} %get-tuple-element.40.own_ref), channel_id=1, source_target_pairs={{0,2},{1,15},{2,4},{3,1},{4,6},{5,3},{6,8},{7,5},{8,10},{9,7},{10,... | collective-permute-start | bytes 184328 | tf_op jit(solution)/shard_map/ppermute | solution.py:331
  24.5 6.3 %collective-permute-start.5 = (bf16[240,128]{1,0:T(8,128)(2,1)S(1)}, bf16[240,128]{1,0:T(8,128)(2,1)S(1)}, u32[]{:S(2)}, u32[]{:S(2)}) collective-permute-start(bf16[240,128]{1,0:T(8,128)(2,1)S(1)} %get-tuple-element.63.own_ref), channel_id=1, source_target_pairs={{0,15},{1,2},{2,1},{3,4},{4,3},{5,6},{6,5},{7,8},{8,7},{9,10},{10,... | collective-permute-start | bytes 184328 | tf_op jit(solution)/shard_map/ppermute | solution.py:329
  25.3 5.6 %collective-permute-start.6 = (bf16[240,128]{1,0:T(8,128)(2,1)S(1)}, bf16[240,128]{1,0:T(8,128)(2,1)S(1)}, u32[]{:S(2)}, u32[]{:S(2)}) collective-permute-start(bf16[240,128]{1,0:T(8,128)(2,1)S(1)} %get-tuple-element.63.own_ref), channel_id=1, source_target_pairs={{0,1},{1,0},{2,3},{3,2},{4,5},{5,4},{6,7},{7,6},{8,9},{9,8},{10,11... | collective-permute-start | bytes 184328 | tf_op jit(solution)/shard_map/ppermute | solution.py:323
  33.5 9.5 %collective-permute-start.7 = (f32[240,128]{1,0:T(8,128)S(1)}, f32[240,128]{1,0:T(8,128)S(1)}, u32[]{:S(2)}, u32[]{:S(2)}) collective-permute-start(f32[240,128]{1,0:T(8,128)S(1)} %get-tuple-element.66), channel_id=1, source_target_pairs={{0,1},{1,0},{2,3},{3,2},{4,5},{5,4},{6,7},{7,6},{8,9},{9,8},{10,11... | collective-permute-start | bytes 368648 | tf_op jit(solution)/shard_map/ppermute | solution.py:323
  33.6 7.2 %collective-permute-start.4 = (bf16[240,128]{1,0:T(8,128)(2,1)S(1)}, bf16[240,128]{1,0:T(8,128)(2,1)S(1)}, u32[]{:S(2)}, u32[]{:S(2)}) collective-permute-start(bf16[240,128]{1,0:T(8,128)(2,1)S(1)} %get-tuple-element.63.own_ref), channel_id=1, source_target_pairs={{0,2},{1,15},{2,4},{3,1},{4,6},{5,3},{6,8},{7,5},{8,10},{9,7},{10,... | collective-permute-start | bytes 184328 | tf_op jit(solution)/shard_map/ppermute | solution.py:331
  43.4 5.3 %collective-permute-start.8 = (bf16[1,240,128]{2,1,0:T(8,128)(2,1)S(1)}, bf16[1,240,128]{2,1,0:T(8,128)(2,1)S(1)}, u32[]{:S(2)}, u32[]{:S(2)}) collective-permute-start(bf16[1,240,128]{2,1,0:T(8,128)(2,1)S(1)} %bitcast.16), channel_id=1, source_target_pairs={{0,8},{1,9},{2,10},{3,11},{4,12},{5,13},{6,14},{7,15},{8,0},{9,1},... | collective-permute-start | bytes 184328 | tf_op jit(solution)/shard_map/ppermute | solution.py:323
  48.7 4.9 %collective-permute-start.9 = (bf16[2,240,128]{2,1,0:T(8,128)(2,1)S(1)}, bf16[2,240,128]{2,1,0:T(8,128)(2,1)S(1)}, u32[]{:S(2)}, u32[]{:S(2)}) collective-permute-start(bf16[2,240,128]{2,1,0:T(8,128)(2,1)S(1)} %pad_maximum_fusion), channel_id=1, source_target_pairs={{0,2},{1,3},{2,0},{3,1},{4,6},{5,7},{6,4},{7,5},{8,10},{9,11},{10,... | collective-permute-start | bytes 368648 | tf_op jit(solution)/shard_map/ppermute | solution.py:323
  48.8 4.9 %collective-permute-start.10 = (bf16[2,240,128]{2,1,0:T(8,128)(2,1)S(1)}, bf16[2,240,128]{2,1,0:T(8,128)(2,1)S(1)}, u32[]{:S(2)}, u32[]{:S(2)}) collective-permute-start(bf16[2,240,128]{2,1,0:T(8,128)(2,1)S(1)} %pad_maximum_fusion), channel_id=1, source_target_pairs={{0,4},{1,5},{2,6},{3,7},{4,0},{5,1},{6,2},{7,3},{8,12},{9,13},{10,... | collective-permute-start | bytes 368648 | tf_op jit(solution)/shard_map/ppermute | solution.py:323
  53.6 4.9 %collective-permute-start.11 = (bf16[2,240,128]{2,1,0:T(8,128)(2,1)S(1)}, bf16[2,240,128]{2,1,0:T(8,128)(2,1)S(1)}, u32[]{:S(2)}, u32[]{:S(2)}) collective-permute-start(bf16[2,240,128]{2,1,0:T(8,128)(2,1)S(1)} %collective-permute-done.9), channel_id=1, source_target_pairs={{0,4},{1,5},{2,6},{3,7},{4,0},{5,1},{6,2},{7,3},{8,12},{9,13},{10,... | collective-permute-start | bytes 368648 | tf_op jit(solution)/shard_map/ppermute | solution.py:323
  58.6 1.9 %collective-permute-start.12 = (bf16[8,240,128]{2,1,0:T(8,128)(2,1)S(1)}, bf16[8,240,128]{2,1,0:T(8,128)(2,1)S(1)}, u32[]{:S(2)}, u32[]{:S(2)}) collective-permute-start(bf16[8,240,128]{2,1,0:T(8,128)(2,1)S(1)} %get-tuple-element.74), channel_id=1, source_target_pairs={{0,1},{1,0},{2,3},{3,2},{4,5},{5,4},{6,7},{7,6},{8,9},{9,8},{10,11... | collective-permute-start | bytes 1474568 | tf_op jit(solution)/shard_map/ppermute | solution.py:323

commit v2 on v1

--- a/solution.py
+++ b/solution.py
@@ -19,7 +19,6 @@
 SIZES = (8,8,)
 SKEW = 1
 SHIFTS = [(b, d) for b in (-1, 0, 1) for d in (-1, 0, 1)]
-HIGHEST = lax.Precision.HIGHEST
 TWO_PI = 6.283185307179586
 VMEM = pl.BlockSpec(memory_space=pltpu.VMEM)
 SMEM = pl.BlockSpec(memory_space=pltpu.SMEM)
@@ -29,7 +28,21 @@
 
 call = functools.partial(pl.pallas_call, compiler_params=pltpu.CompilerParams(vmem_limit_bytes=16 << 20))
 dot = functools.partial(jnp.dot, preferred_element_type=jnp.float32)
-exact_dot = functools.partial(jnp.dot, precision=HIGHEST, preferred_element_type=jnp.float32)
+
+
+def split(values):
+    high = values.astype(bf16)
+    return high, (values - high.astype(f32)).astype(bf16)
+
+
+def left_terms(values):
+    high, low = split(values)
+    return jnp.concatenate([high, high, low], axis=1)
+
+
+def close_dot(left, values):
+    high, low = split(values)
+    return dot(left, jnp.concatenate([high, low, high]))
 
 
 def in_hbm(value):
@@ -56,31 +69,32 @@
     return lax.broadcasted_iota(jnp.int32, (rows, CELLS), 1) % NZ
 
 
-def round_kernel(q_hbm, rounded_ref, q_ref, semaphore):
-    copy = pltpu.make_async_copy(q_hbm, q_ref, semaphore)
-    copy.start()
-    copy.wait()
-    rounded_ref[...] = q_ref[...].astype(bf16)
+def round_kernel(*refs):
+    count = (len(refs) - 2) // 2
+    sources, rounded_ref, targets, semaphores = refs[:count], refs[count], refs[count + 1 : -1], refs[-1]
+    copies = [pltpu.make_async_copy(a, b, semaphores.at[i]) for i, (a, b) in enumerate(zip(sources, targets))]
+    for copy in copies:
+        copy.start()
+    copies[0].wait()
+    rounded_ref[...] = targets[0][...].astype(bf16)
+    for copy in copies[1:]:
+        copy.wait()
 
 
 def setup_kernel(
-    coords, beads, masses_hbm, step_hbm, cycle_hbm, one_hbm, bias_one_hbm, bias_two_hbm, readout_hbm, p_hbm,
-    two_hbm, modes_hbm, modes_t_hbm, vectors_hbm, q_ref,
+    coords, beads, masses_hbm, step_hbm, cycle_hbm, p_hbm, modes_hbm, modes_t_hbm, vectors_hbm,
+    q_ref, one_ref, bias_one_ref, bias_two_ref, readout_ref, two_ref,
     forward_ref, outer_forward_ref, backward_ref, two_t_ref, wide_ref,
     q_base_ref, q_map_ref, p_base_ref, pushed_ref, cosine_ref, finish_ref, half_ref,
-    two_ref, modes_ref, modes_t_ref, vectors_ref,
-    rows, masses_ref, step_ref, cycle_ref, one_ref, bias_one_ref, bias_two_ref, readout_ref, p_ref, semaphores
+    modes_ref, modes_t_ref, vectors_ref, rows, masses_ref, step_ref, cycle_ref, p_ref, semaphores
 ):
     moves = (
-        (one_hbm, one_ref), (bias_one_hbm, bias_one_ref), (bias_two_hbm, bias_two_ref), (readout_hbm, readout_ref),
-        (two_hbm, two_ref), (masses_hbm, masses_ref), (step_hbm, step_ref), (cycle_hbm, cycle_ref),
-        (p_hbm, p_ref), (modes_hbm, modes_ref), (modes_t_hbm, modes_t_ref), (vectors_hbm, vectors_ref),
+        (masses_hbm, masses_ref), (step_hbm, step_ref), (cycle_hbm, cycle_ref), (p_hbm, p_ref),
+        (modes_hbm, modes_ref), (modes_t_hbm, modes_t_ref), (vectors_hbm, vectors_ref),
     )
     copies = [pltpu.make_async_copy(a, b, semaphores.at[i]) for i, (a, b) in enumerate(moves)]
     for copy in copies:
         copy.start()
-    for copy in copies[:5]:
-        copy.wait()
     is_odd = lax.axis_index("space") % 2 == 1
     hidden = one_ref.shape[1]
     rows[: one_ref.shape[0], :] = one_ref[...].astype(f32)
@@ -112,8 +126,9 @@
     for i in range(2):
         wide_ref[i] = jnp.broadcast_to(columns[:, i : i + 1], (hidden, CELLS))
 
-    for copy in copies[5:]:
+    for copy in copies:
         copy.wait()
+    total = coords * beads
     order = lax.broadcasted_iota(jnp.int32, (beads, CELLS), 0).astype(f32)
     mass = jnp.concatenate([jnp.full((beads, CELLS), masses_ref[c], f32) for c in range(coords)])
     step = step_ref[0]
@@ -126,16 +141,17 @@
         jnp.concatenate([term] * coords) for term in (jnp.cos(phase), step * ratio, frequency * sine)
     )
     drift, spring = drift / mass, mass * spring
-    mode = exact_dot(modes_t_ref[...], jnp.concatenate([q_ref[...], p_ref[...]], axis=1))
+    mode = close_dot(modes_t_ref[...], jnp.concatenate([q_ref[...], p_ref[...]], axis=1))
     mode_q, mode_p = mode[:, :CELLS], mode[:, CELLS:]
     moved = cosine * mode_q + drift * mode_p
     pushed = cosine * mode_p - spring * mode_q
-    base = exact_dot(modes_ref[...], jnp.concatenate([moved, pushed], axis=1))
+    base = close_dot(modes_ref[...], jnp.concatenate([moved, pushed], axis=1))
     q_base_ref[...] = base[:, :CELLS]
     p_base_ref[...] = base[:, CELLS:]
     pushed_ref[...] = pushed
     cosine_ref[...] = cosine
-    q_map_ref[...] = exact_dot(modes_ref[...], (half * drift[:, :1]) * modes_t_ref[...])
+    modes_t = modes_t_ref[:, :total].astype(f32) + modes_t_ref[:, 2 * total :].astype(f32)
+    q_map_ref[...] = left_terms(close_dot(modes_ref[...], (half * drift[:, :1]) * modes_t))
     finish_ref[...] = jnp.concatenate([half / mass, 1.0 / mass], axis=1)
     half_ref[...] = jnp.full(half_ref.shape, half, f32)
 
@@ -252,20 +268,23 @@
 
 def move_kernel(q_base_ref, q_map_ref, kept_ref, came_ref, q_out, rounded_out, sum_out):
     sums = kept_ref[...] + came_ref[...]
+    q = q_base_ref[...] - close_dot(q_map_ref[...], sums)
+    rounded_out[...] = q.astype(bf16)
+    q_out[...] = q
     sum_out[...] = sums
-    q = q_base_ref[...] - exact_dot(q_map_ref[...], sums)
-    q_out[...] = q
-    rounded_out[...] = q.astype(bf16)
 
 
 def push_kernel(
-    share, planes_at, half_ref, sum_ref, p_base_ref, pushed_ref, cosine_ref, finish_ref, modes_ref, modes_t_ref,
-    vectors_ref, p_out, velocity_out, velocity_map_out, planes_out, cells_out
+    share, planes_at, half_ref, q_ref, sum_ref, p_base_ref, pushed_ref, cosine_ref, finish_ref, modes_ref,
+    modes_t_ref, vectors_ref, q_out, p_out, velocity_out, velocity_map_out, planes_out, cells_out
 ):
-    kick = cosine_ref[...] * exact_dot(modes_t_ref[...], half_ref[0:1, :] * sum_ref[...])
-    p_out[...] = p_base_ref[...] - exact_dot(modes_ref[...], kick)
+    total = modes_ref.shape[0]
+    q_out[...] = q_ref[...]
+    kick = cosine_ref[...] * close_dot(modes_t_ref[...], half_ref[0:1, :] * sum_ref[...])
+    p_out[...] = p_base_ref[...] - close_dot(modes_ref[...], kick)
     velocity_out[...] = (pushed_ref[...] - kick) * finish_ref[:, CELLS:]
-    velocity_map_out[...] = finish_ref[:, :1] * modes_t_ref[...]
+    modes_t = modes_t_ref[:, :total].astype(f32) + modes_t_ref[:, 2 * total :].astype(f32)
+    velocity_map_out[...] = left_terms(finish_ref[:, :1] * modes_t)
     extent_x = len(planes_at)
     whole = extent_x * CELLS
     here = lax.axis_index("space")
@@ -284,28 +303,44 @@
 
 def finish_kernel(half_ref, velocity_ref, map_ref, kept_ref, came_ref, velocity_out, kick_out):
     sums = kept_ref[...] + came_ref[...]
-    velocity_out[...] = (velocity_ref[...] - exact_dot(map_ref[...], sums)).astype(bf16)
+    velocity_out[...] = (velocity_ref[...] - close_dot(map_ref[...], sums)).astype(bf16)
     kick_out[...] = half_ref[0:1, :] * sums
 
 
-def project_kernel(scale, velocity_ref, planes_ref, cells_ref, out_ref):
+def projected(velocity_ref, planes_ref, cells_ref, first, part):
+    cos_cell, sin_cell = cells_ref[0], cells_ref[1]
+
+    def trig(i):
+        cos_plane, sin_plane = (planes_ref[t, first + i : first + i + 1, :] for t in range(2))
+        if part == 0:
+            return (cos_plane * cos_cell - sin_plane * sin_cell).astype(bf16)
+        return (sin_plane * cos_cell + cos_plane * sin_cell).astype(bf16)
+
+    total = 0.0
+    for i in range(0, velocity_ref.shape[0] - 1, 2):
+        block = jnp.concatenate([velocity_ref[i], velocity_ref[i + 1]], axis=1)
+        total += dot(block, jnp.concatenate([trig(i), trig(i + 1)]))
+    if velocity_ref.shape[0] % 2:
+        total += dot(velocity_ref[velocity_ref.shape[0] - 1], trig(velocity_ref.shape[0] - 1))
+    return total
+
+
+def near_project_kernel(velocity_ref, planes_ref, cells_ref, out_ref):
+    fields = velocity_ref.shape[1]
+    for part in range(2):
+        out_ref[part * fields : (part + 1) * fields, :] = projected(velocity_ref, planes_ref, cells_ref, 0, part)
+
+
+def project_kernel(scale, near_ref, velocity_ref, planes_ref, cells_ref, out_hbm, result, semaphores):
     count, fields, _ = velocity_ref.shape
-    cos_cell, sin_cell = cells_ref[0], cells_ref[1]
-
-    def trig(i):
-        cos_plane, sin_plane = planes_ref[0, i : i + 1, :], planes_ref[1, i : i + 1, :]
-        cosine = cos_plane * cos_cell - sin_plane * sin_cell
-        sine = sin_plane * cos_cell + cos_plane * sin_cell
-        return cosine.astype(bf16), sine.astype(bf16)
-
-    cos_sum = sin_sum = 0.0
-    for i in range(0, count, 2):
-        (cos_0, sin_0), (cos_1, sin_1) = trig(i), trig(i + 1)
-        block = jnp.concatenate([velocity_ref[i], velocity_ref[i + 1]], axis=1)
-        cos_sum += dot(block, jnp.concatenate([cos_0, cos_1]))
-        sin_sum += dot(block, jnp.concatenate([sin_0, sin_1]))
-    out_ref[:fields, :] = cos_sum * scale
-    out_ref[fields:, :] = sin_sum * scale
+    copies = []
+    for part in range(2):
+        rows = slice(part * fields, (part + 1) * fields)
+        result[rows, :] = (near_ref[rows, :] + projected(velocity_ref, planes_ref, cells_ref, count, part)) * scale
+        copies.append(pltpu.make_async_copy(result.at[rows, :], out_hbm.at[rows, :], semaphores.at[part]))
+        copies[-1].start()
+    for copy in copies:
+        copy.wait()
 
 
 def mode_matrix(coords, beads):
@@ -319,6 +354,12 @@
     return modes.astype(np.float32)
 
 
+def constant_terms(matrix):
+    high = matrix.astype(jnp.bfloat16)
+    low = (matrix - high.astype(np.float32)).astype(jnp.bfloat16)
+    return jnp.asarray(np.concatenate([high, high, low], axis=1))
+
+
 def swap(value, distance):
     return lax.ppermute(value, "space", [(i, i ^ distance) for i in range(lax.axis_size("space"))])
 
@@ -344,13 +385,13 @@
 
 def gather_planes(velocity):
     held, distance = velocity[None], lax.axis_size("space") // 2
-    while distance:
+    while distance > 1:
         if distance == 4:
             near, far = swap(held, 2), swap(held, 4)
             held, distance = jnp.concatenate([held, near, far, swap(near, 4)]), 1
         else:
             held, distance = jnp.concatenate([held, swap(held, distance)]), distance // 2
-    return held
+    return held, swap(held, 1)
 
 
 def on_device(
@@ -364,39 +405,39 @@
     hidden = layer_one.shape[0]
     width = 27 * PAD
     field, narrow = shape((total, CELLS), f32), shape((total, CELLS), bf16)
-    square = shape((total, total), f32)
+    square = shape((total, 3 * total), bf16)
 
     modes = mode_matrix(coords, beads)
     share = wavevectors.shape[1] // devices
     if share % CELLS:
         wavevectors = lax.dynamic_slice_in_dim(wavevectors, lax.axis_index("space") * share, share, 1)
-    rounded, q = call(
-        round_kernel, out_shape=(narrow, field), in_specs=[HBM], out_specs=(VMEM,) * 2,
-        scratch_shapes=[pltpu.SemaphoreType.DMA],
-    )(in_hbm(positions.reshape(total, CELLS)))
-
-    row = pltpu.VMEM((1, hidden), f32)
     inputs = (
-        layer_one.T, bias_one.reshape(1, hidden), bias_two.reshape(1, hidden), readout.reshape(1, hidden),
-        momenta.reshape(total, CELLS), layer_two, jnp.asarray(modes), jnp.asarray(modes.T), wavevectors,
+        positions.reshape(total, CELLS), layer_one.T, bias_one.reshape(1, hidden), bias_two.reshape(1, hidden),
+        readout.reshape(1, hidden), layer_two,
     )
+    rounded, *brought = call(
+        round_kernel, out_shape=(narrow,) + tuple(shape(x.shape, x.dtype) for x in inputs),
+        in_specs=[HBM] * 6, out_specs=(VMEM,) * 7, scratch_shapes=[pltpu.SemaphoreType.DMA((6,))],
+    )(*map(in_hbm, inputs))
+    two = brought[-1]
+
+    inputs = (momenta.reshape(total, CELLS), constant_terms(modes), constant_terms(modes.T), wavevectors)
     (
         forward, outer_forward, backward, two_t, wide, q_base, q_map, p_base, pushed, cosine, finish, half,
-        two, modes, modes_t, wavevectors
+        modes, modes_t, wavevectors
     ) = call(
         functools.partial(setup_kernel, coords, beads),
         out_shape=(
             shape((hidden, width), bf16), shape((hidden, width), bf16), shape((width, hidden), bf16),
             shape((hidden, hidden), bf16), shape((2, hidden, CELLS), f32),
             field, square, field, field, field, shape((total, 2 * CELLS), f32), shape((8, CELLS), f32),
-        ) + tuple(shape(x.shape, x.dtype) for x in inputs[5:]),
-        in_specs=[HBM] * 12 + [VMEM], out_specs=(VMEM,) * 16,
+        ) + tuple(shape(x.shape, x.dtype) for x in inputs[1:]),
+        in_specs=[HBM] * 7 + [VMEM] * 6, out_specs=(VMEM,) * 15,
         scratch_shapes=[
             pltpu.VMEM((width, hidden), f32), pltpu.SMEM((coords,), f32), pltpu.SMEM((1,), f32),
-            pltpu.SMEM((1,), f32), pltpu.VMEM(inputs[0].shape, bf16), row, row, row,
-            pltpu.VMEM((total, CELLS), f32), pltpu.SemaphoreType.DMA((12,)),
+            pltpu.SMEM((1,), f32), pltpu.VMEM((total, CELLS), f32), pltpu.SemaphoreType.DMA((7,)),
         ],
-    )(in_hbm(masses), step_size, cycle_frequency, *map(in_hbm, inputs), q)
+    )(in_hbm(masses), step_size, cycle_frequency, *map(in_hbm, inputs), *brought)
     layers = (backward, two, two_t, wide)
     stage = pltpu.VMEM((total, CELLS), f32)
 
@@ -415,23 +456,29 @@
         )(outer2, features, kept, outer_forward, *layers)
         return kept, came
 
-    q_new, rounded, sums = call(
+    q_moved, rounded, sums = call(
         move_kernel, out_shape=(field, narrow, field), in_specs=[VMEM] * 4, out_specs=(VMEM,) * 3,
     )(q_base, q_map, *forces(rounded))
     order = gather_order(devices)
-    p_mid, velocity_base, velocity_map, across, along = call(
+    q_new, p_mid, velocity_base, velocity_map, across, along = call(
         functools.partial(push_kernel, share, order),
-        out_shape=(field, field, square, shape((2, devices, share), f32), shape((2, CELLS, share), f32)),
-        in_specs=[VMEM] * 9, out_specs=(VMEM,) * 5,
-    )(half, sums, p_base, pushed, cosine, finish, modes, modes_t, wavevectors)
+        out_shape=(
+            field, field, field, square, shape((2, devices, share), f32), shape((2, CELLS, share), f32),
+        ),
+        in_specs=[VMEM] * 10, out_specs=(VMEM,) * 6,
+    )(half, q_moved, sums, p_base, pushed, cosine, finish, modes, modes_t, wavevectors)
     velocity, kick = call(
         finish_kernel, out_shape=(narrow, field), in_specs=[VMEM] * 5, out_specs=(VMEM,) * 2,
     )(half, velocity_base, velocity_map, *forces(rounded))
     p_new = p_mid - kick
+    held, last = gather_planes(velocity)
+    spectrum = shape((2 * total, share), f32)
+    near = call(near_project_kernel, out_shape=spectrum, in_specs=[VMEM] * 3, out_specs=VMEM)(held, across, along)
     spectrum = call(
         functools.partial(project_kernel, 1.0 / math.sqrt(devices * CELLS)),
-        out_shape=shape((2 * total, share), f32), in_specs=[VMEM] * 3, out_specs=VMEM,
-    )(gather_planes(velocity), across, along)
+        out_shape=spectrum, in_specs=[VMEM] * 4, out_specs=HBM,
+        scratch_shapes=[pltpu.VMEM((2 * total, share), f32), pltpu.SemaphoreType.DMA((2,))],
+    )(near, last, across, along)
     return q_new.reshape(positions.shape), p_new.reshape(momenta.shape), spectrum.T
 
 

time: 62.3 us -> 61.1 us (0.981)
  waiting for transfers between devices: 33.7 us -> 32.9 us
  Pallas kernels: 17.8 us -> 17.1 us
    pallas_call x1, Pallas kernels: 1.03 us -> 0.25 us  [on_device(): call(move_kernel, out_shape=(field, narrow, field), in_specs=[VMEM] * 4,...]
    pallas_call x1 -> x2, Pallas kernels: 0.92 us -> 1.63 us  [the longest x1 1.17 us: on_device(): call(round_kernel, out_shape=(narrow,) + tuple((shape(x.shape, x.dtype) f...]
  transfers between devices with their start and end apart: 13 -> 13, of which waited for: 7 -> 8; matrix products, arithmetic and copies ran while one was open for 1% -> 1% of each run, Pallas kernels for 14% -> 15%
where the time goes in v2:
time: 61.1 us; the launch traced here: 61 us
  waiting for transfers between devices  32.9 us (54%)
  Pallas kernels  17.1 us (28%)
  starting transfers between devices  7.92 us (13%)
  between operations  2.26 us (4%)
  other arithmetic  0.68 us (1%)
    ppermute x9, waiting for transfers between devices, swap(): lax.ppermute(value, 'space', [(i, i ^ distance) for i in range(lax.axis_s...  15.5 us
    ppermute x2, waiting for transfers between devices, neighbour_planes(): lax.ppermute(plane, 'space', [(i, (i - 2 * step[i]) % count) for i in ran...  12.2 us
    ppermute x2, starting transfers between devices, neighbour_planes(): lax.ppermute(plane, 'space', [(i, (i + step[i]) % count) for i in range(c...  6.73 us
    pallas_call x2, Pallas kernels, forces(): call(functools.partial(own_kernel, coords, beads, len(tied)), out_shape=(...  5.31 us
    ppermute x2, waiting for transfers between devices, neighbour_planes(): lax.ppermute(plane, 'space', [(i, (i + step[i]) % count) for i in range(c...  5.21 us
    pallas_call x2, Pallas kernels, forces(): call(functools.partial(outer_kernel, coords, beads), out_shape=field, in_...  4.5 us
    pallas_call x1, Pallas kernels, on_device(): call(functools.partial(setup_kernel, coords, beads), out_shape=(shape((hi...  2.28 us
    pallas_call x1, Pallas kernels, on_device(): call(functools.partial(push_kernel, share, order), out_shape=(field, fiel...  1.63 us
  transfers between devices with their start and end apart: 13, of which 8 were waited for; matrix products, arithmetic and copies ran while one was open for 1% of the time, Pallas kernels for 15%

profile of v2, /device:TPU:0, one launch (start us, length us, event | category | flops | bytes accessed | tf_op | source)
XLA Modules:
  0.0 61.0 jit_solution(7749299951587001554)
XLA Ops:
  0.6 1.2 %shard_map.148 = (bf16[240,128]{1,0:T(8,128)(2,1)S(1)}, f32[240,128]{1,0:T(8,128)S(1)}, bf16[405,256]{1,0:T(8,128)(2,1)S(1)}, f32[1,256]{1,0:T(1,128)S(1)}, f32[...) custom-call(f32[240,128]{1,0:T(8,128)} %bitcast.19, bf16[405,256]{1,0:T(8,128)(2,1)} %bitcast.18, ...), custom_call_target="tpu_custom_call" | custom-call | tf_op jit(solution)/shard_map/pallas_call | solution.py:418
  1.8 5.5 %collective-permute-start.1 = (bf16[240,128]{1,0:T(8,128)(2,1)S(1)}, bf16[240,128]{1,0:T(8,128)(2,1)S(1)}, u32[]{:S(2)}, u32[]{:S(2)}) collective-permute-start(bf16[240,128]{1,0:T(8,128)(2,1)S(1)} %get-tuple-element.51.own_ref), channel_id=1, source_target_pairs={{0,15},{1,2},{2,1},{3,4},{4,3},{5,6},{6,5},{7,8},{8,7},{9,10},{10,... | collective-permute-start | bytes 184328 | tf_op jit(solution)/shard_map/ppermute | solution.py:370
  7.3 0.0 collective-permute-start.2
  8.6 2.3 %shard_map.149 = (bf16[256,432]{1,0:T(8,128)(2,1)S(1)}, bf16[256,432]{1,0:T(8,128)(2,1)S(1)}, bf16[432,256]{1,0:T(8,128)(2,1)S(1)}, bf16[256,256]{1,0:T(8,128)(2...) custom-call(f32[15]{0:T(128)} %masses_hbm.1, ...), custom_call_target="tpu_custom_call" | custom-call | tf_op jit(solution)/shard_map/pallas_call | solution.py:428
  10.9 0.0 collective-permute-done.1.outer_ref
  10.9 0.0 collective-permute-done.2.inner_ref
  11.0 2.7 %shard_map.150 = (f32[240,128]{1,0:T(8,128)S(1)}, f32[240,128]{1,0:T(8,128)S(1)}, bf16[432,2048]{1,0:T(8,128)(2,1)S(1)}) custom-call(bf16[240,128]{1,0:T(8,128)(2,1)S(1)} %collective-permute-done.1.outer_ref, bf16[240,128]{1,0:T(8,128)(2,1)S(1)} %get-tuple-element.51.own_ref, bf16[240,128]{1,0:T(8,128)(2,1)S(1)} %collective-permute-done.2.inner_ref, ...), custom_call_target="tpu_custom_call" | custom-call | tf_op jit(solution)/shard_map/pallas_call | solution.py:446
  13.6 0.6 collective-permute-start.3
  14.2 0.0 collective-permute-start
  14.2 6.9 %collective-permute-done.outer2_ref = bf16[240,128]{1,0:T(8,128)(2,1)S(1)} collective-permute-done((bf16[240,128]{1,0:T(8,128)(2,1)S(1)}, bf16[240,128]{1,0:T(8,128)(2,1)S(1)}, u32[]{:S(2)}, u32[]{:S(2)}) %collective-permute-start) | collective-permute-done | bytes 61472 | tf_op jit(solution)/shard_map/ppermute | solution.py:372
  21.1 2.2 %shard_map.151.kept_ref = f32[240,128]{1,0:T(8,128)S(1)} custom-call(bf16[240,128]{1,0:T(8,128)(2,1)S(1)} %collective-permute-done.outer2_ref, bf16[432,2048]{1,0:T(8,128)(2,1)S(1)} %get-tuple-element.56.features_ref, f32[240,128]{1,0:T(8,128)S(1)} %get-tuple-element.57.kept_in_ref, bf16[256,432]{1,0:T(8,128)(2,1)S(1)} %get-tuple-element.58.forward_ref, ...), custom_call_target="tpu_custom_call" | custom-call | tf_op jit(solution)/shard_map/pallas_call | solution.py:452
  23.4 0.0 collective-permute-done.3.came_ref
  23.4 0.2 shard_map.152
  23.6 1.2 %collective-permute-start.5 = (bf16[240,128]{1,0:T(8,128)(2,1)S(1)}, bf16[240,128]{1,0:T(8,128)(2,1)S(1)}, u32[]{:S(2)}, u32[]{:S(2)}) collective-permute-start(bf16[240,128]{1,0:T(8,128)(2,1)S(1)} %get-tuple-element.73.own_ref), channel_id=1, source_target_pairs={{0,15},{1,2},{2,1},{3,4},{4,3},{5,6},{6,5},{7,8},{8,7},{9,10},{10,... | collective-permute-start | bytes 184328 | tf_op jit(solution)/shard_map/ppermute | solution.py:370
  24.8 0.0 collective-permute-start.6
  24.8 5.2 %collective-permute-done.5.outer_ref = bf16[240,128]{1,0:T(8,128)(2,1)S(1)} collective-permute-done((bf16[240,128]{1,0:T(8,128)(2,1)S(1)}, bf16[240,128]{1,0:T(8,128)(2,1)S(1)}, u32[]{:S(2)}, u32[]{:S(2)}) %collective-permute-start.5) | collective-permute-done | bytes 61472 | tf_op jit(solution)/shard_map/ppermute | solution.py:370
  30.1 0.0 collective-permute-done.6.inner_ref
  30.1 2.7 %shard_map.154 = (f32[240,128]{1,0:T(8,128)S(1)}, f32[240,128]{1,0:T(8,128)S(1)}, bf16[432,2048]{1,0:T(8,128)(2,1)S(1)}) custom-call(bf16[240,128]{1,0:T(8,128)(2,1)S(1)} %collective-permute-done.5.outer_ref, bf16[240,128]{1,0:T(8,128)(2,1)S(1)} %get-tuple-element.73.own_ref, bf16[240,128]{1,0:T(8,128)(2,1)S(1)} %collective-permute-done.6.inner_ref, ...), custom_call_target="tpu_custom_call" | custom-call | tf_op jit(solution)/shard_map/pallas_call | solution.py:446
  32.7 0.1 collective-permute-start.7
  32.8 0.2 collective-permute-start.4
  33.0 1.6 %shard_map.153 = (f32[240,128]{1,0:T(8,128)}, f32[240,128]{1,0:T(8,128)S(1)}, f32[240,128]{1,0:T(8,128)S(1)}, bf16[240,720]{1,0:T(8,128)(2,1)S(1)}, f32[2,16,256...) custom-call(f32[8,128]{1,0:T(8,128)S(1)} %get-tuple-element.48.half_ref, f32[240,128]{1,0:T(8,128)S(1)} %get-tuple-element.60.q_ref, ...), custom_call_target="tpu_custom_call" | custom-call | tf_op jit(solution)/shard_map/pallas_call | solution.py:463
  34.7 5.3 %collective-permute-done.4.outer2_ref = bf16[240,128]{1,0:T(8,128)(2,1)S(1)} collective-permute-done((bf16[240,128]{1,0:T(8,128)(2,1)S(1)}, bf16[240,128]{1,0:T(8,128)(2,1)S(1)}, u32[]{:S(2)}, u32[]{:S(2)}) %collective-permute-start.4) | collective-permute-done | bytes 61472 | tf_op jit(solution)/shard_map/ppermute | solution.py:372
  40.0 2.3 %shard_map.155.kept_ref = f32[240,128]{1,0:T(8,128)S(1)} custom-call(bf16[240,128]{1,0:T(8,128)(2,1)S(1)} %collective-permute-done.4.outer2_ref, bf16[432,2048]{1,0:T(8,128)(2,1)S(1)} %get-tuple-element.74.features_ref, f32[240,128]{1,0:T(8,128)S(1)} %get-tuple-element.75.kept_in_ref, bf16[256,432]{1,0:T(8,128)(2,1)S(1)} %get-tuple-element.58.forward_ref, ...), custom_call_target="tpu_custom_call" | custom-call | tf_op jit(solution)/shard_map/pallas_call | solution.py:452
  42.2 0.0 collective-permute-done.7.came_ref
  42.2 0.3 shard_map.156
  42.5 0.1 collective-permute-start.8
  42.6 5.2 %collective-permute-done.8 = bf16[1,240,128]{2,1,0:T(8,128)(2,1)S(1)} collective-permute-done((bf16[1,240,128]{2,1,0:T(8,128)(2,1)S(1)}, bf16[1,240,128]{2,1,0:T(8,128)(2,1)S(1)}, u32[]{:S(2)}, u32[]{:S(2)}) %collective-permute-start.8) | collective-permute-done | bytes 61472 | tf_op jit(solution)/shard_map/ppermute | solution.py:364
  47.8 0.1 collective-permute-start.9
  47.9 0.1 collective-permute-start.10
  48.0 4.8 %collective-permute-done.9 = bf16[2,240,128]{2,1,0:T(8,128)(2,1)S(1)} collective-permute-done((bf16[2,240,128]{2,1,0:T(8,128)(2,1)S(1)}, bf16[2,240,128]{2,1,0:T(8,128)(2,1)S(1)}, u32[]{:S(2)}, u32[]{:S(2)}) %collective-permute-start.9) | collective-permute-done | bytes 122912 | tf_op jit(solution)/shard_map/ppermute | solution.py:364
  52.7 0.0 collective-permute-start.11
  52.7 0.2 collective-permute-done.10
  52.9 4.7 %collective-permute-done.11 = bf16[2,240,128]{2,1,0:T(8,128)(2,1)S(1)} collective-permute-done((bf16[2,240,128]{2,1,0:T(8,128)(2,1)S(1)}, bf16[2,240,128]{2,1,0:T(8,128)(2,1)S(1)}, u32[]{:S(2)}, u32[]{:S(2)}) %collective-permute-start.11) | collective-permute-done | bytes 122912 | tf_op jit(solution)/shard_map/ppermute | solution.py:364
  57.6 0.1 collective-permute-start.12
  57.7 0.7 %sub.3 = f32[240,128]{1,0:T(8,128)} subtract(f32[240,128]{1,0:T(8,128)S(1)} %get-tuple-element.70, f32[240,128]{1,0:T(8,128)S(1)} %get-tuple-element.77) | non-fusion elementwise | flops 30720 | bytes 368640 | tf_op jit(solution)/shard_map/sub | solution.py:473
  58.4 0.5 shard_map.157.near_ref
  58.8 0.7 %collective-permute-done.12.velocity_ref = bf16[8,240,128]{2,1,0:T(8,128)(2,1)S(1)} collective-permute-done((bf16[8,240,128]{2,1,0:T(8,128)(2,1)S(1)}, bf16[8,240,128]{2,1,0:T(8,128)(2,1)S(1)}, u32[]{:S(2)}, u32[]{:S(2)}) %collective-permute-start.12) | collective-permute-done | bytes 491552 | tf_op jit(solution)/shard_map/ppermute | solution.py:364
  59.5 1.3 %shard_map.158 = f32[480,256]{1,0:T(8,128)} custom-call(f32[480,256]{1,0:T(8,128)S(1)} %shard_map.157.near_ref, bf16[8,240,128]{2,1,0:T(8,128)(2,1)S(1)} %collective-permute-done.12.velocity_ref, f32[2,16,256]{2,1,0:T(8,128)S(1)} %get-tuple-element.79.planes_ref, f32[2,128,256]{2,1,0:T(8,128)S(1)} %get-tuple-element.80.cells_ref), custom_call_target="tpu_custom_call" | custom-call | tf_op jit(solution)/shard_map/pallas_call | solution.py:477
  (6 shorter events, 0.1 us)
Async XLA Ops:
  1.8 9.1 %collective-permute-start.1 = (bf16[240,128]{1,0:T(8,128)(2,1)S(1)}, bf16[240,128]{1,0:T(8,128)(2,1)S(1)}, u32[]{:S(2)}, u32[]{:S(2)}) collective-permute-start(bf16[240,128]{1,0:T(8,128)(2,1)S(1)} %get-tuple-element.51.own_ref), channel_id=1, source_target_pairs={{0,15},{1,2},{2,1},{3,4},{4,3},{5,6},{6,5},{7,8},{8,7},{9,10},{10,... | collective-permute-start | bytes 184328 | tf_op jit(solution)/shard_map/ppermute | solution.py:370
  7.3 3.6 %collective-permute-start.2 = (bf16[240,128]{1,0:T(8,128)(2,1)S(1)}, bf16[240,128]{1,0:T(8,128)(2,1)S(1)}, u32[]{:S(2)}, u32[]{:S(2)}) collective-permute-start(bf16[240,128]{1,0:T(8,128)(2,1)S(1)} %get-tuple-element.51.own_ref), channel_id=1, source_target_pairs={{0,1},{1,0},{2,3},{3,2},{4,5},{5,4},{6,7},{7,6},{8,9},{9,8},{10,11... | collective-permute-start | bytes 184328 | tf_op jit(solution)/shard_map/ppermute | solution.py:364
  13.6 9.8 %collective-permute-start.3 = (f32[240,128]{1,0:T(8,128)S(1)}, f32[240,128]{1,0:T(8,128)S(1)}, u32[]{:S(2)}, u32[]{:S(2)}) collective-permute-start(f32[240,128]{1,0:T(8,128)S(1)} %get-tuple-element.59), channel_id=1, source_target_pairs={{0,1},{1,0},{2,3},{3,2},{4,5},{5,4},{6,7},{7,6},{8,9},{9,8},{10,11... | collective-permute-start | bytes 368648 | tf_op jit(solution)/shard_map/ppermute | solution.py:364
  14.2 6.9 %collective-permute-start = (bf16[240,128]{1,0:T(8,128)(2,1)S(1)}, bf16[240,128]{1,0:T(8,128)(2,1)S(1)}, u32[]{:S(2)}, u32[]{:S(2)}) collective-permute-start(bf16[240,128]{1,0:T(8,128)(2,1)S(1)} %get-tuple-element.51.own_ref), channel_id=1, source_target_pairs={{0,2},{1,15},{2,4},{3,1},{4,6},{5,3},{6,8},{7,5},{8,10},{9,7},{10,... | collective-permute-start | bytes 184328 | tf_op jit(solution)/shard_map/ppermute | solution.py:372
  23.6 6.4 %collective-permute-start.5 = (bf16[240,128]{1,0:T(8,128)(2,1)S(1)}, bf16[240,128]{1,0:T(8,128)(2,1)S(1)}, u32[]{:S(2)}, u32[]{:S(2)}) collective-permute-start(bf16[240,128]{1,0:T(8,128)(2,1)S(1)} %get-tuple-element.73.own_ref), channel_id=1, source_target_pairs={{0,15},{1,2},{2,1},{3,4},{4,3},{5,6},{6,5},{7,8},{8,7},{9,10},{10,... | collective-permute-start | bytes 184328 | tf_op jit(solution)/shard_map/ppermute | solution.py:370
  24.8 5.2 %collective-permute-start.6 = (bf16[240,128]{1,0:T(8,128)(2,1)S(1)}, bf16[240,128]{1,0:T(8,128)(2,1)S(1)}, u32[]{:S(2)}, u32[]{:S(2)}) collective-permute-start(bf16[240,128]{1,0:T(8,128)(2,1)S(1)} %get-tuple-element.73.own_ref), channel_id=1, source_target_pairs={{0,1},{1,0},{2,3},{3,2},{4,5},{5,4},{6,7},{7,6},{8,9},{9,8},{10,11... | collective-permute-start | bytes 184328 | tf_op jit(solution)/shard_map/ppermute | solution.py:364
  32.7 9.5 %collective-permute-start.7 = (f32[240,128]{1,0:T(8,128)S(1)}, f32[240,128]{1,0:T(8,128)S(1)}, u32[]{:S(2)}, u32[]{:S(2)}) collective-permute-start(f32[240,128]{1,0:T(8,128)S(1)} %get-tuple-element.76), channel_id=1, source_target_pairs={{0,1},{1,0},{2,3},{3,2},{4,5},{5,4},{6,7},{7,6},{8,9},{9,8},{10,11... | collective-permute-start | bytes 368648 | tf_op jit(solution)/shard_map/ppermute | solution.py:364
  32.8 7.2 %collective-permute-start.4 = (bf16[240,128]{1,0:T(8,128)(2,1)S(1)}, bf16[240,128]{1,0:T(8,128)(2,1)S(1)}, u32[]{:S(2)}, u32[]{:S(2)}) collective-permute-start(bf16[240,128]{1,0:T(8,128)(2,1)S(1)} %get-tuple-element.73.own_ref), channel_id=1, source_target_pairs={{0,2},{1,15},{2,4},{3,1},{4,6},{5,3},{6,8},{7,5},{8,10},{9,7},{10,... | collective-permute-start | bytes 184328 | tf_op jit(solution)/shard_map/ppermute | solution.py:372
  42.5 5.3 %collective-permute-start.8 = (bf16[1,240,128]{2,1,0:T(8,128)(2,1)S(1)}, bf16[1,240,128]{2,1,0:T(8,128)(2,1)S(1)}, u32[]{:S(2)}, u32[]{:S(2)}) collective-permute-start(bf16[1,240,128]{2,1,0:T(8,128)(2,1)S(1)} %bitcast.15), channel_id=1, source_target_pairs={{0,8},{1,9},{2,10},{3,11},{4,12},{5,13},{6,14},{7,15},{8,0},{9,1},... | collective-permute-start | bytes 184328 | tf_op jit(solution)/shard_map/ppermute | solution.py:364
  47.8 4.9 %collective-permute-start.9 = (bf16[2,240,128]{2,1,0:T(8,128)(2,1)S(1)}, bf16[2,240,128]{2,1,0:T(8,128)(2,1)S(1)}, u32[]{:S(2)}, u32[]{:S(2)}) collective-permute-start(bf16[2,240,128]{2,1,0:T(8,128)(2,1)S(1)} %pad_maximum_fusion), channel_id=1, source_target_pairs={{0,2},{1,3},{2,0},{3,1},{4,6},{5,7},{6,4},{7,5},{8,10},{9,11},{10,... | collective-permute-start | bytes 368648 | tf_op jit(solution)/shard_map/ppermute | solution.py:364
  47.9 5.0 %collective-permute-start.10 = (bf16[2,240,128]{2,1,0:T(8,128)(2,1)S(1)}, bf16[2,240,128]{2,1,0:T(8,128)(2,1)S(1)}, u32[]{:S(2)}, u32[]{:S(2)}) collective-permute-start(bf16[2,240,128]{2,1,0:T(8,128)(2,1)S(1)} %pad_maximum_fusion), channel_id=1, source_target_pairs={{0,4},{1,5},{2,6},{3,7},{4,0},{5,1},{6,2},{7,3},{8,12},{9,13},{10,... | collective-permute-start | bytes 368648 | tf_op jit(solution)/shard_map/ppermute | solution.py:364
  52.7 4.9 %collective-permute-start.11 = (bf16[2,240,128]{2,1,0:T(8,128)(2,1)S(1)}, bf16[2,240,128]{2,1,0:T(8,128)(2,1)S(1)}, u32[]{:S(2)}, u32[]{:S(2)}) collective-permute-start(bf16[2,240,128]{2,1,0:T(8,128)(2,1)S(1)} %collective-permute-done.9), channel_id=1, source_target_pairs={{0,4},{1,5},{2,6},{3,7},{4,0},{5,1},{6,2},{7,3},{8,12},{9,13},{10,... | collective-permute-start | bytes 368648 | tf_op jit(solution)/shard_map/ppermute | solution.py:364
  57.6 1.9 %collective-permute-start.12 = (bf16[8,240,128]{2,1,0:T(8,128)(2,1)S(1)}, bf16[8,240,128]{2,1,0:T(8,128)(2,1)S(1)}, u32[]{:S(2)}, u32[]{:S(2)}) collective-permute-start(bf16[8,240,128]{2,1,0:T(8,128)(2,1)S(1)} %constant_dynamic-update-slice_fusion.velocity_ref), channel_id=1, source_target_pairs={{0,1},{1,0},{2,3},{3,2},{4,5},{5,4},{6,7},{7,6},{8,9},{9,8},{10,11... | collective-permute-start | bytes 1474568 | tf_op jit(solution)/shard_map/ppermute | solution.py:364

commit v3 on v2

--- a/solution.py
+++ b/solution.py
@@ -42,7 +42,8 @@
 
 def close_dot(left, values):
     high, low = split(values)
-    return dot(left, jnp.concatenate([high, low, high]))
+    rest = jnp.zeros((left.shape[1] // 3 - values.shape[0], values.shape[1]), bf16)
+    return dot(left, jnp.concatenate([high, rest, low, rest, high, rest]))
 
 
 def in_hbm(value):
@@ -82,15 +83,15 @@
 
 
 def setup_kernel(
-    coords, beads, masses_hbm, step_hbm, cycle_hbm, p_hbm, modes_hbm, modes_t_hbm, vectors_hbm,
+    coords, beads, masses_hbm, step_hbm, cycle_hbm, p_hbm, blocks_hbm, vectors_hbm,
     q_ref, one_ref, bias_one_ref, bias_two_ref, readout_ref, two_ref,
     forward_ref, outer_forward_ref, backward_ref, two_t_ref, wide_ref,
     q_base_ref, q_map_ref, p_base_ref, pushed_ref, cosine_ref, finish_ref, half_ref,
-    modes_ref, modes_t_ref, vectors_ref, rows, masses_ref, step_ref, cycle_ref, p_ref, semaphores
+    modes_ref, modes_t_ref, vectors_ref, rows, masses_ref, step_ref, cycle_ref, p_ref, blocks_ref, semaphores
 ):
     moves = (
-        (masses_hbm, masses_ref), (step_hbm, step_ref), (cycle_hbm, cycle_ref), (p_hbm, p_ref),
-        (modes_hbm, modes_ref), (modes_t_hbm, modes_t_ref), (vectors_hbm, vectors_ref),
+        (blocks_hbm, blocks_ref), (p_hbm, p_ref), (masses_hbm, masses_ref), (step_hbm, step_ref),
+        (cycle_hbm, cycle_ref), (vectors_hbm, vectors_ref),
     )
     copies = [pltpu.make_async_copy(a, b, semaphores.at[i]) for i, (a, b) in enumerate(moves)]
     for copy in copies:
@@ -126,9 +127,17 @@
     for i in range(2):
         wide_ref[i] = jnp.broadcast_to(columns[:, i : i + 1], (hidden, CELLS))
 
-    for copy in copies:
+    for copy in copies[:-1]:
         copy.wait()
-    total = coords * beads
+    depth = blocks_ref.shape[1]
+    column = lax.broadcasted_iota(jnp.int32, (beads, depth), 1) // beads
+    for matrix_ref, first in ((modes_ref, 0), (modes_t_ref, 2 * beads)):
+        high, low = blocks_ref[first : first + beads, :], blocks_ref[first + beads : first + 2 * beads, :]
+        for c in range(coords):
+            rows_at = slice(c * beads, (c + 1) * beads)
+            mine = jnp.where(column == c, high, 0.0).astype(bf16)
+            rest = jnp.where(column == c, low, 0.0).astype(bf16)
+            matrix_ref[rows_at, :] = jnp.concatenate([mine, mine, rest], axis=1)
     order = lax.broadcasted_iota(jnp.int32, (beads, CELLS), 0).astype(f32)
     mass = jnp.concatenate([jnp.full((beads, CELLS), masses_ref[c], f32) for c in range(coords)])
     step = step_ref[0]
@@ -150,10 +159,11 @@
     p_base_ref[...] = base[:, CELLS:]
     pushed_ref[...] = pushed
     cosine_ref[...] = cosine
-    modes_t = modes_t_ref[:, :total].astype(f32) + modes_t_ref[:, 2 * total :].astype(f32)
+    modes_t = modes_t_ref[:, :depth].astype(f32) + modes_t_ref[:, 2 * depth :].astype(f32)
     q_map_ref[...] = left_terms(close_dot(modes_ref[...], (half * drift[:, :1]) * modes_t))
     finish_ref[...] = jnp.concatenate([half / mass, 1.0 / mass], axis=1)
     half_ref[...] = jnp.full(half_ref.shape, half, f32)
+    copies[-1].wait()
 
 
 def put_features(coords, beads, chosen, stage, features, top):
@@ -215,7 +225,7 @@
 def own_kernel(
     coords, beads, tied, outer_ref, own_ref, inner_ref, forward_ref, backward_ref, two_ref, two_t_ref, wide_ref, *refs
 ):
-    sent_ref, kept_ref, features, stage = refs[tied:]
+    sent_ref, sums_ref, features, stage = refs[tied:]
     for place, ref in enumerate((outer_ref, own_ref, inner_ref)):
         stage[place] = ref[...].astype(f32)
 
@@ -228,19 +238,20 @@
         return (dot(forward_ref[...], features[:, columns_of(chosen)]),)
 
     def last(chosen, back):
-        return (dot(backward_ref[BLOCK:], back),)
+        sums = dot(backward_ref[BLOCK:], back)
+        sums_ref[:, columns_of(chosen)] = sums[:BLOCK]
+        return (sums,)
 
     def store(chosen, sums):
         for at, j in enumerate(chosen):
             rows = pl.ds(j, coords, stride=beads)
-            kept_ref[rows, :] = shifted_sum(sums[:BLOCK], at)[:coords]
             sent_ref[rows, :] = shifted_sum(sums[BLOCK:], at)[:coords]
 
     run_skewed(groups_of(beads), (put, first, *back_stages(two_ref, two_t_ref, wide_ref), last, store))
 
 
 def outer_kernel(
-    coords, beads, outer2_ref, features_ref, kept_in_ref, forward_ref, backward_ref, two_ref, two_t_ref, wide_ref,
+    coords, beads, outer2_ref, features_ref, sums_ref, forward_ref, backward_ref, two_ref, two_t_ref, wide_ref,
     kept_ref, features, stage
 ):
     extra = 2 * BLOCK - DEPTH
@@ -256,12 +267,12 @@
         return (near + dot(forward_ref[:, DEPTH:], features[:, columns_of(chosen)]),)
 
     def last(chosen, back):
-        return (dot(backward_ref[2 * BLOCK :], back),)
+        return (dot(backward_ref[2 * BLOCK :], back) + sums_ref[:, columns_of(chosen)],)
 
     def store(chosen, sums):
         for at, j in enumerate(chosen):
             rows = pl.ds(j, coords, stride=beads)
-            kept_ref[rows, :] = kept_in_ref[rows, :] + shifted_sum(sums, at)[:coords]
+            kept_ref[rows, :] = shifted_sum(sums, at)[:coords]
 
     run_skewed(groups_of(beads), (put, first, *back_stages(two_ref, two_t_ref, wide_ref), last, store))
 
@@ -278,12 +289,12 @@
     share, planes_at, half_ref, q_ref, sum_ref, p_base_ref, pushed_ref, cosine_ref, finish_ref, modes_ref,
     modes_t_ref, vectors_ref, q_out, p_out, velocity_out, velocity_map_out, planes_out, cells_out
 ):
-    total = modes_ref.shape[0]
+    depth = modes_ref.shape[1] // 3
     q_out[...] = q_ref[...]
     kick = cosine_ref[...] * close_dot(modes_t_ref[...], half_ref[0:1, :] * sum_ref[...])
     p_out[...] = p_base_ref[...] - close_dot(modes_ref[...], kick)
     velocity_out[...] = (pushed_ref[...] - kick) * finish_ref[:, CELLS:]
-    modes_t = modes_t_ref[:, :total].astype(f32) + modes_t_ref[:, 2 * total :].astype(f32)
+    modes_t = modes_t_ref[:, :depth].astype(f32) + modes_t_ref[:, 2 * depth :].astype(f32)
     velocity_map_out[...] = left_terms(finish_ref[:, :1] * modes_t)
     extent_x = len(planes_at)
     whole = extent_x * CELLS
@@ -343,21 +354,17 @@
         copy.wait()
 
 
-def mode_matrix(coords, beads):
+def mode_blocks(coords, beads):
     j = np.arange(beads)[:, None]
     k = np.arange(beads)[None, :]
     angles = 2.0 * np.pi * ((j * k) % beads) / beads
     edge = np.cos(angles) / math.sqrt(beads)
     inside = np.where(k < beads // 2, np.cos(angles), np.sin(angles)) * math.sqrt(2.0 / beads)
-    matrix = np.where((k == 0) | (k == beads // 2), edge, inside)
-    modes = np.einsum("ab,jk->ajbk", np.eye(coords), matrix).reshape(coords * beads, coords * beads)
-    return modes.astype(np.float32)
-
-
-def constant_terms(matrix):
-    high = matrix.astype(jnp.bfloat16)
-    low = (matrix - high.astype(np.float32)).astype(jnp.bfloat16)
-    return jnp.asarray(np.concatenate([high, high, low], axis=1))
+    matrix = np.where((k == 0) | (k == beads // 2), edge, inside).astype(np.float32)
+    high = matrix.astype(jnp.bfloat16).astype(np.float32)
+    low = (matrix - high).astype(jnp.bfloat16).astype(np.float32)
+    blocks = np.concatenate([np.tile(block, (1, coords)) for block in (high, low, high.T, low.T)])
+    return np.pad(blocks, ((0, 0), (0, -coords * beads % CELLS)))
 
 
 def swap(value, distance):
@@ -405,9 +412,8 @@
     hidden = layer_one.shape[0]
     width = 27 * PAD
     field, narrow = shape((total, CELLS), f32), shape((total, CELLS), bf16)
-    square = shape((total, 3 * total), bf16)
-
-    modes = mode_matrix(coords, beads)
+    square = shape((total, 3 * (total + -total % CELLS)), bf16)
+
     share = wavevectors.shape[1] // devices
     if share % CELLS:
         wavevectors = lax.dynamic_slice_in_dim(wavevectors, lax.axis_index("space") * share, share, 1)
@@ -421,7 +427,7 @@
     )(*map(in_hbm, inputs))
     two = brought[-1]
 
-    inputs = (momenta.reshape(total, CELLS), constant_terms(modes), constant_terms(modes.T), wavevectors)
+    inputs = (momenta.reshape(total, CELLS), jnp.asarray(mode_blocks(coords, beads)), wavevectors)
     (
         forward, outer_forward, backward, two_t, wide, q_base, q_map, p_base, pushed, cosine, finish, half,
         modes, modes_t, wavevectors
@@ -431,11 +437,13 @@
             shape((hidden, width), bf16), shape((hidden, width), bf16), shape((width, hidden), bf16),
             shape((hidden, hidden), bf16), shape((2, hidden, CELLS), f32),
             field, square, field, field, field, shape((total, 2 * CELLS), f32), shape((8, CELLS), f32),
-        ) + tuple(shape(x.shape, x.dtype) for x in inputs[1:]),
-        in_specs=[HBM] * 7 + [VMEM] * 6, out_specs=(VMEM,) * 15,
+            square, square, shape(wavevectors.shape, wavevectors.dtype),
+        ),
+        in_specs=[HBM] * 6 + [VMEM] * 6, out_specs=(VMEM,) * 15,
         scratch_shapes=[
             pltpu.VMEM((width, hidden), f32), pltpu.SMEM((coords,), f32), pltpu.SMEM((1,), f32),
-            pltpu.SMEM((1,), f32), pltpu.VMEM((total, CELLS), f32), pltpu.SemaphoreType.DMA((7,)),
+            pltpu.SMEM((1,), f32), pltpu.VMEM((total, CELLS), f32), pltpu.VMEM(inputs[1].shape, f32),
+            pltpu.SemaphoreType.DMA((6,)),
         ],
     )(in_hbm(masses), step_size, cycle_frequency, *map(in_hbm, inputs), *brought)
     layers = (backward, two, two_t, wide)
@@ -443,9 +451,9 @@
 
     def forces(plane, *tied):
         outer2, outer, inner = neighbour_planes(plane)
-        sent, kept, features = call(
+        sent, sums, features = call(
             functools.partial(own_kernel, coords, beads, len(tied)),
-            out_shape=(field, field, shape((width, beads * CELLS), bf16)),
+            out_shape=(field, shape((BLOCK, beads * CELLS), f32), shape((width, beads * CELLS), bf16)),
             in_specs=[VMEM] * (8 + len(tied)), out_specs=(VMEM,) * 3, scratch_shapes=[pltpu.VMEM((3, total, CELLS), f32)],
         )(outer, plane, inner, forward, *layers, *tied)
         came = swap(sent, 1)
@@ -453,7 +461,7 @@
             functools.partial(outer_kernel, coords, beads),
             out_shape=field, in_specs=[VMEM] * 8, out_specs=VMEM,
             scratch_shapes=[pltpu.VMEM((width - DEPTH, beads * CELLS), bf16), stage],
-        )(outer2, features, kept, outer_forward, *layers)
+        )(outer2, features, sums, outer_forward, *layers)
         return kept, came
 
     q_moved, rounded, sums = call(

time: 61.1 us -> 60.7 us (level)
  Pallas kernels: 17.1 us -> 16.4 us
  transfers between devices with their start and end apart: 13 -> 13, of which waited for: 8 -> 8; matrix products, arithmetic and copies ran while one was open for 1% -> 1% of each run, Pallas kernels for 15% -> 14%
where the time goes in v3:
time: 60.7 us; the launch traced here: 60.5 us
  waiting for transfers between devices  32.9 us (54%)
  Pallas kernels  16.4 us (27%)
  starting transfers between devices  8.18 us (13%)
  between operations  2.26 us (4%)
  other arithmetic  0.68 us (1%)
    ppermute x9, waiting for transfers between devices, swap(): lax.ppermute(value, 'space', [(i, i ^ distance) for i in range(lax.axis_s...  15.5 us
    ppermute x2, waiting for transfers between devices, neighbour_planes(): lax.ppermute(plane, 'space', [(i, (i - 2 * step[i]) % count) for i in ran...  12.5 us
    ppermute x2, starting transfers between devices, neighbour_planes(): lax.ppermute(plane, 'space', [(i, (i + step[i]) % count) for i in range(c...  6.99 us
    pallas_call x2, Pallas kernels, forces(): call(functools.partial(own_kernel, coords, beads, len(tied)), out_shape=(...  5.05 us
    ppermute x2, waiting for transfers between devices, neighbour_planes(): lax.ppermute(plane, 'space', [(i, (i + step[i]) % count) for i in range(c...  4.95 us
    pallas_call x2, Pallas kernels, forces(): call(functools.partial(outer_kernel, coords, beads), out_shape=field, in_...  4.57 us
    pallas_call x1, Pallas kernels, on_device(): call(functools.partial(setup_kernel, coords, beads), out_shape=(shape((hi...  2.03 us
    pallas_call x1, Pallas kernels, on_device(): call(functools.partial(push_kernel, share, order), out_shape=(field, fiel...  1.35 us
  transfers between devices with their start and end apart: 13, of which 8 were waited for; matrix products, arithmetic and copies ran while one was open for 1% of the time, Pallas kernels for 14%

profile of v3, /device:TPU:0, one launch (start us, length us, event | category | flops | bytes accessed | tf_op | source)
XLA Modules:
  0.0 60.5 jit_solution(1423113913113545051)
XLA Ops:
  0.6 1.2 %shard_map.139 = (bf16[240,128]{1,0:T(8,128)(2,1)S(1)}, f32[240,128]{1,0:T(8,128)S(1)}, bf16[405,256]{1,0:T(8,128)(2,1)S(1)}, f32[1,256]{1,0:T(1,128)S(1)}, f32[...) custom-call(f32[240,128]{1,0:T(8,128)} %bitcast.20, bf16[405,256]{1,0:T(8,128)(2,1)} %bitcast.18, ...), custom_call_target="tpu_custom_call" | custom-call | tf_op jit(solution)/shard_map/pallas_call | solution.py:424
  1.8 5.5 %collective-permute-start.1 = (bf16[240,128]{1,0:T(8,128)(2,1)S(1)}, bf16[240,128]{1,0:T(8,128)(2,1)S(1)}, u32[]{:S(2)}, u32[]{:S(2)}) collective-permute-start(bf16[240,128]{1,0:T(8,128)(2,1)S(1)} %get-tuple-element.51.own_ref), channel_id=1, source_target_pairs={{0,15},{1,2},{2,1},{3,4},{4,3},{5,6},{6,5},{7,8},{8,7},{9,10},{10,... | collective-permute-start | bytes 184328 | tf_op jit(solution)/shard_map/ppermute | solution.py:377
  7.3 0.0 collective-permute-start.2
  8.6 2.0 %shard_map.140 = (bf16[256,432]{1,0:T(8,128)(2,1)S(1)}, bf16[256,432]{1,0:T(8,128)(2,1)S(1)}, bf16[432,256]{1,0:T(8,128)(2,1)S(1)}, bf16[256,256]{1,0:T(8,128)(2...) custom-call(f32[15]{0:T(128)} %masses_hbm.1, ...), custom_call_target="tpu_custom_call" | custom-call | tf_op jit(solution)/shard_map/pallas_call | solution.py:434
  10.7 0.0 collective-permute-done.1.outer_ref
  10.7 0.0 collective-permute-done.2.inner_ref
  10.7 2.5 %shard_map.141 = (f32[240,128]{1,0:T(8,128)S(1)}, f32[144,2048]{1,0:T(8,128)S(1)}, bf16[432,2048]{1,0:T(8,128)(2,1)S(1)}) custom-call(bf16[240,128]{1,0:T(8,128)(2,1)S(1)} %collective-permute-done.1.outer_ref, bf16[240,128]{1,0:T(8,128)(2,1)S(1)} %get-tuple-element.51.own_ref, bf16[240,128]{1,0:T(8,128)(2,1)S(1)} %collective-permute-done.2.inner_ref, ...), custom_call_target="tpu_custom_call" | custom-call | tf_op jit(solution)/shard_map/pallas_call | solution.py:454
  13.2 0.6 collective-permute-start.3
  13.8 0.0 collective-permute-start
  13.8 6.9 %collective-permute-done.outer2_ref = bf16[240,128]{1,0:T(8,128)(2,1)S(1)} collective-permute-done((bf16[240,128]{1,0:T(8,128)(2,1)S(1)}, bf16[240,128]{1,0:T(8,128)(2,1)S(1)}, u32[]{:S(2)}, u32[]{:S(2)}) %collective-permute-start) | collective-permute-done | bytes 61472 | tf_op jit(solution)/shard_map/ppermute | solution.py:379
  20.7 2.3 %shard_map.142.kept_ref = f32[240,128]{1,0:T(8,128)S(1)} custom-call(bf16[240,128]{1,0:T(8,128)(2,1)S(1)} %collective-permute-done.outer2_ref, bf16[432,2048]{1,0:T(8,128)(2,1)S(1)} %get-tuple-element.56.features_ref, f32[144,2048]{1,0:T(8,128)S(1)} %get-tuple-element.57.sums_ref, bf16[256,432]{1,0:T(8,128)(2,1)S(1)} %get-tuple-element.58.forward_ref, ...), custom_call_target="tpu_custom_call" | custom-call | tf_op jit(solution)/shard_map/pallas_call | solution.py:460
  23.0 0.0 collective-permute-done.3.came_ref
  23.0 0.3 shard_map.143
  23.3 1.5 %collective-permute-start.5 = (bf16[240,128]{1,0:T(8,128)(2,1)S(1)}, bf16[240,128]{1,0:T(8,128)(2,1)S(1)}, u32[]{:S(2)}, u32[]{:S(2)}) collective-permute-start(bf16[240,128]{1,0:T(8,128)(2,1)S(1)} %get-tuple-element.73.own_ref), channel_id=1, source_target_pairs={{0,15},{1,2},{2,1},{3,4},{4,3},{5,6},{6,5},{7,8},{8,7},{9,10},{10,... | collective-permute-start | bytes 184328 | tf_op jit(solution)/shard_map/ppermute | solution.py:377
  24.8 0.0 collective-permute-start.6
  24.8 4.9 %collective-permute-done.5.outer_ref = bf16[240,128]{1,0:T(8,128)(2,1)S(1)} collective-permute-done((bf16[240,128]{1,0:T(8,128)(2,1)S(1)}, bf16[240,128]{1,0:T(8,128)(2,1)S(1)}, u32[]{:S(2)}, u32[]{:S(2)}) %collective-permute-start.5) | collective-permute-done | bytes 61472 | tf_op jit(solution)/shard_map/ppermute | solution.py:377
  29.7 0.0 collective-permute-done.6.inner_ref
  29.7 2.5 %shard_map.145 = (f32[240,128]{1,0:T(8,128)S(1)}, f32[144,2048]{1,0:T(8,128)S(1)}, bf16[432,2048]{1,0:T(8,128)(2,1)S(1)}) custom-call(bf16[240,128]{1,0:T(8,128)(2,1)S(1)} %collective-permute-done.5.outer_ref, bf16[240,128]{1,0:T(8,128)(2,1)S(1)} %get-tuple-element.73.own_ref, bf16[240,128]{1,0:T(8,128)(2,1)S(1)} %collective-permute-done.6.inner_ref, ...), custom_call_target="tpu_custom_call" | custom-call | tf_op jit(solution)/shard_map/pallas_call | solution.py:454
  32.3 0.1 collective-permute-start.7
  32.3 0.2 collective-permute-start.4
  32.6 1.3 %shard_map.144 = (f32[240,128]{1,0:T(8,128)}, f32[240,128]{1,0:T(8,128)S(1)}, f32[240,128]{1,0:T(8,128)S(1)}, bf16[240,768]{1,0:T(8,128)(2,1)S(1)}, f32[2,16,256...) custom-call(f32[8,128]{1,0:T(8,128)S(1)} %get-tuple-element.48.half_ref, f32[240,128]{1,0:T(8,128)S(1)} %get-tuple-element.60.q_ref, ...), custom_call_target="tpu_custom_call" | custom-call | tf_op jit(solution)/shard_map/pallas_call | solution.py:471
  33.9 5.6 %collective-permute-done.4.outer2_ref = bf16[240,128]{1,0:T(8,128)(2,1)S(1)} collective-permute-done((bf16[240,128]{1,0:T(8,128)(2,1)S(1)}, bf16[240,128]{1,0:T(8,128)(2,1)S(1)}, u32[]{:S(2)}, u32[]{:S(2)}) %collective-permute-start.4) | collective-permute-done | bytes 61472 | tf_op jit(solution)/shard_map/ppermute | solution.py:379
  39.5 2.3 %shard_map.146.kept_ref = f32[240,128]{1,0:T(8,128)S(1)} custom-call(bf16[240,128]{1,0:T(8,128)(2,1)S(1)} %collective-permute-done.4.outer2_ref, bf16[432,2048]{1,0:T(8,128)(2,1)S(1)} %get-tuple-element.74.features_ref, f32[144,2048]{1,0:T(8,128)S(1)} %get-tuple-element.75.sums_ref, bf16[256,432]{1,0:T(8,128)(2,1)S(1)} %get-tuple-element.58.forward_ref, ...), custom_call_target="tpu_custom_call" | custom-call | tf_op jit(solution)/shard_map/pallas_call | solution.py:460
  41.8 0.0 collective-permute-done.7.came_ref
  41.8 0.3 shard_map.147
  42.1 0.1 collective-permute-start.8
  42.1 5.2 %collective-permute-done.8 = bf16[1,240,128]{2,1,0:T(8,128)(2,1)S(1)} collective-permute-done((bf16[1,240,128]{2,1,0:T(8,128)(2,1)S(1)}, bf16[1,240,128]{2,1,0:T(8,128)(2,1)S(1)}, u32[]{:S(2)}, u32[]{:S(2)}) %collective-permute-start.8) | collective-permute-done | bytes 61472 | tf_op jit(solution)/shard_map/ppermute | solution.py:371
  47.4 0.1 collective-permute-start.9
  47.5 0.1 collective-permute-start.10
  47.5 4.8 %collective-permute-done.9 = bf16[2,240,128]{2,1,0:T(8,128)(2,1)S(1)} collective-permute-done((bf16[2,240,128]{2,1,0:T(8,128)(2,1)S(1)}, bf16[2,240,128]{2,1,0:T(8,128)(2,1)S(1)}, u32[]{:S(2)}, u32[]{:S(2)}) %collective-permute-start.9) | collective-permute-done | bytes 122912 | tf_op jit(solution)/shard_map/ppermute | solution.py:371
  52.3 0.0 collective-permute-start.11
  52.3 0.1 collective-permute-done.10
  52.4 4.8 %collective-permute-done.11 = bf16[2,240,128]{2,1,0:T(8,128)(2,1)S(1)} collective-permute-done((bf16[2,240,128]{2,1,0:T(8,128)(2,1)S(1)}, bf16[2,240,128]{2,1,0:T(8,128)(2,1)S(1)}, u32[]{:S(2)}, u32[]{:S(2)}) %collective-permute-start.11) | collective-permute-done | bytes 122912 | tf_op jit(solution)/shard_map/ppermute | solution.py:371
  57.2 0.1 collective-permute-start.12
  57.3 0.7 %sub.3 = f32[240,128]{1,0:T(8,128)} subtract(f32[240,128]{1,0:T(8,128)S(1)} %get-tuple-element.70, f32[240,128]{1,0:T(8,128)S(1)} %get-tuple-element.77) | non-fusion elementwise | flops 30720 | bytes 368640 | tf_op jit(solution)/shard_map/sub | solution.py:481
  57.9 0.5 shard_map.148.near_ref
  58.4 0.7 %collective-permute-done.12.velocity_ref = bf16[8,240,128]{2,1,0:T(8,128)(2,1)S(1)} collective-permute-done((bf16[8,240,128]{2,1,0:T(8,128)(2,1)S(1)}, bf16[8,240,128]{2,1,0:T(8,128)(2,1)S(1)}, u32[]{:S(2)}, u32[]{:S(2)}) %collective-permute-start.12) | collective-permute-done | bytes 491552 | tf_op jit(solution)/shard_map/ppermute | solution.py:371
  59.1 1.3 %shard_map.149 = f32[480,256]{1,0:T(8,128)} custom-call(f32[480,256]{1,0:T(8,128)S(1)} %shard_map.148.near_ref, bf16[8,240,128]{2,1,0:T(8,128)(2,1)S(1)} %collective-permute-done.12.velocity_ref, f32[2,16,256]{2,1,0:T(8,128)S(1)} %get-tuple-element.79.planes_ref, f32[2,128,256]{2,1,0:T(8,128)S(1)} %get-tuple-element.80.cells_ref), custom_call_target="tpu_custom_call" | custom-call | tf_op jit(solution)/shard_map/pallas_call | solution.py:485
  (6 shorter events, 0.1 us)
Async XLA Ops:
  1.8 8.9 %collective-permute-start.1 = (bf16[240,128]{1,0:T(8,128)(2,1)S(1)}, bf16[240,128]{1,0:T(8,128)(2,1)S(1)}, u32[]{:S(2)}, u32[]{:S(2)}) collective-permute-start(bf16[240,128]{1,0:T(8,128)(2,1)S(1)} %get-tuple-element.51.own_ref), channel_id=1, source_target_pairs={{0,15},{1,2},{2,1},{3,4},{4,3},{5,6},{6,5},{7,8},{8,7},{9,10},{10,... | collective-permute-start | bytes 184328 | tf_op jit(solution)/shard_map/ppermute | solution.py:377
  7.3 3.4 %collective-permute-start.2 = (bf16[240,128]{1,0:T(8,128)(2,1)S(1)}, bf16[240,128]{1,0:T(8,128)(2,1)S(1)}, u32[]{:S(2)}, u32[]{:S(2)}) collective-permute-start(bf16[240,128]{1,0:T(8,128)(2,1)S(1)} %get-tuple-element.51.own_ref), channel_id=1, source_target_pairs={{0,1},{1,0},{2,3},{3,2},{4,5},{5,4},{6,7},{7,6},{8,9},{9,8},{10,11... | collective-permute-start | bytes 184328 | tf_op jit(solution)/shard_map/ppermute | solution.py:371
  13.2 9.8 %collective-permute-start.3 = (f32[240,128]{1,0:T(8,128)S(1)}, f32[240,128]{1,0:T(8,128)S(1)}, u32[]{:S(2)}, u32[]{:S(2)}) collective-permute-start(f32[240,128]{1,0:T(8,128)S(1)} %get-tuple-element.59), channel_id=1, source_target_pairs={{0,1},{1,0},{2,3},{3,2},{4,5},{5,4},{6,7},{7,6},{8,9},{9,8},{10,11... | collective-permute-start | bytes 368648 | tf_op jit(solution)/shard_map/ppermute | solution.py:371
  13.8 6.9 %collective-permute-start = (bf16[240,128]{1,0:T(8,128)(2,1)S(1)}, bf16[240,128]{1,0:T(8,128)(2,1)S(1)}, u32[]{:S(2)}, u32[]{:S(2)}) collective-permute-start(bf16[240,128]{1,0:T(8,128)(2,1)S(1)} %get-tuple-element.51.own_ref), channel_id=1, source_target_pairs={{0,2},{1,15},{2,4},{3,1},{4,6},{5,3},{6,8},{7,5},{8,10},{9,7},{10,... | collective-permute-start | bytes 184328 | tf_op jit(solution)/shard_map/ppermute | solution.py:379
  23.3 6.4 %collective-permute-start.5 = (bf16[240,128]{1,0:T(8,128)(2,1)S(1)}, bf16[240,128]{1,0:T(8,128)(2,1)S(1)}, u32[]{:S(2)}, u32[]{:S(2)}) collective-permute-start(bf16[240,128]{1,0:T(8,128)(2,1)S(1)} %get-tuple-element.73.own_ref), channel_id=1, source_target_pairs={{0,15},{1,2},{2,1},{3,4},{4,3},{5,6},{6,5},{7,8},{8,7},{9,10},{10,... | collective-permute-start | bytes 184328 | tf_op jit(solution)/shard_map/ppermute | solution.py:377
  24.8 5.0 %collective-permute-start.6 = (bf16[240,128]{1,0:T(8,128)(2,1)S(1)}, bf16[240,128]{1,0:T(8,128)(2,1)S(1)}, u32[]{:S(2)}, u32[]{:S(2)}) collective-permute-start(bf16[240,128]{1,0:T(8,128)(2,1)S(1)} %get-tuple-element.73.own_ref), channel_id=1, source_target_pairs={{0,1},{1,0},{2,3},{3,2},{4,5},{5,4},{6,7},{7,6},{8,9},{9,8},{10,11... | collective-permute-start | bytes 184328 | tf_op jit(solution)/shard_map/ppermute | solution.py:371
  32.3 9.5 %collective-permute-start.7 = (f32[240,128]{1,0:T(8,128)S(1)}, f32[240,128]{1,0:T(8,128)S(1)}, u32[]{:S(2)}, u32[]{:S(2)}) collective-permute-start(f32[240,128]{1,0:T(8,128)S(1)} %get-tuple-element.76), channel_id=1, source_target_pairs={{0,1},{1,0},{2,3},{3,2},{4,5},{5,4},{6,7},{7,6},{8,9},{9,8},{10,11... | collective-permute-start | bytes 368648 | tf_op jit(solution)/shard_map/ppermute | solution.py:371
  32.3 7.2 %collective-permute-start.4 = (bf16[240,128]{1,0:T(8,128)(2,1)S(1)}, bf16[240,128]{1,0:T(8,128)(2,1)S(1)}, u32[]{:S(2)}, u32[]{:S(2)}) collective-permute-start(bf16[240,128]{1,0:T(8,128)(2,1)S(1)} %get-tuple-element.73.own_ref), channel_id=1, source_target_pairs={{0,2},{1,15},{2,4},{3,1},{4,6},{5,3},{6,8},{7,5},{8,10},{9,7},{10,... | collective-permute-start | bytes 184328 | tf_op jit(solution)/shard_map/ppermute | solution.py:379
  42.1 5.3 %collective-permute-start.8 = (bf16[1,240,128]{2,1,0:T(8,128)(2,1)S(1)}, bf16[1,240,128]{2,1,0:T(8,128)(2,1)S(1)}, u32[]{:S(2)}, u32[]{:S(2)}) collective-permute-start(bf16[1,240,128]{2,1,0:T(8,128)(2,1)S(1)} %bitcast.15), channel_id=1, source_target_pairs={{0,8},{1,9},{2,10},{3,11},{4,12},{5,13},{6,14},{7,15},{8,0},{9,1},... | collective-permute-start | bytes 184328 | tf_op jit(solution)/shard_map/ppermute | solution.py:371
  47.4 4.9 %collective-permute-start.9 = (bf16[2,240,128]{2,1,0:T(8,128)(2,1)S(1)}, bf16[2,240,128]{2,1,0:T(8,128)(2,1)S(1)}, u32[]{:S(2)}, u32[]{:S(2)}) collective-permute-start(bf16[2,240,128]{2,1,0:T(8,128)(2,1)S(1)} %pad_maximum_fusion), channel_id=1, source_target_pairs={{0,2},{1,3},{2,0},{3,1},{4,6},{5,7},{6,4},{7,5},{8,10},{9,11},{10,... | collective-permute-start | bytes 368648 | tf_op jit(solution)/shard_map/ppermute | solution.py:371
  47.5 4.9 %collective-permute-start.10 = (bf16[2,240,128]{2,1,0:T(8,128)(2,1)S(1)}, bf16[2,240,128]{2,1,0:T(8,128)(2,1)S(1)}, u32[]{:S(2)}, u32[]{:S(2)}) collective-permute-start(bf16[2,240,128]{2,1,0:T(8,128)(2,1)S(1)} %pad_maximum_fusion), channel_id=1, source_target_pairs={{0,4},{1,5},{2,6},{3,7},{4,0},{5,1},{6,2},{7,3},{8,12},{9,13},{10,... | collective-permute-start | bytes 368648 | tf_op jit(solution)/shard_map/ppermute | solution.py:371
  52.3 4.9 %collective-permute-start.11 = (bf16[2,240,128]{2,1,0:T(8,128)(2,1)S(1)}, bf16[2,240,128]{2,1,0:T(8,128)(2,1)S(1)}, u32[]{:S(2)}, u32[]{:S(2)}) collective-permute-start(bf16[2,240,128]{2,1,0:T(8,128)(2,1)S(1)} %collective-permute-done.9), channel_id=1, source_target_pairs={{0,4},{1,5},{2,6},{3,7},{4,0},{5,1},{6,2},{7,3},{8,12},{9,13},{10,... | collective-permute-start | bytes 368648 | tf_op jit(solution)/shard_map/ppermute | solution.py:371
  57.2 1.9 %collective-permute-start.12 = (bf16[8,240,128]{2,1,0:T(8,128)(2,1)S(1)}, bf16[8,240,128]{2,1,0:T(8,128)(2,1)S(1)}, u32[]{:S(2)}, u32[]{:S(2)}) collective-permute-start(bf16[8,240,128]{2,1,0:T(8,128)(2,1)S(1)} %constant_dynamic-update-slice_fusion.velocity_ref), channel_id=1, source_target_pairs={{0,1},{1,0},{2,3},{3,2},{4,5},{5,4},{6,7},{7,6},{8,9},{9,8},{10,11... | collective-permute-start | bytes 1474568 | tf_op jit(solution)/shard_map/ppermute | solution.py:371

commit v4 on v3

--- a/solution.py
+++ b/solution.py
@@ -83,19 +83,14 @@
 
 
 def setup_kernel(
-    coords, beads, masses_hbm, step_hbm, cycle_hbm, p_hbm, blocks_hbm, vectors_hbm,
-    q_ref, one_ref, bias_one_ref, bias_two_ref, readout_ref, two_ref,
+    coords, beads, step_ref, cycle_ref, vectors_hbm, q_ref, one_ref, bias_one_ref, bias_two_ref, readout_ref,
+    p_ref, masses_ref, blocks_ref, two_ref,
     forward_ref, outer_forward_ref, backward_ref, two_t_ref, wide_ref,
     q_base_ref, q_map_ref, p_base_ref, pushed_ref, cosine_ref, finish_ref, half_ref,
-    modes_ref, modes_t_ref, vectors_ref, rows, masses_ref, step_ref, cycle_ref, p_ref, blocks_ref, semaphores
+    modes_ref, modes_t_ref, vectors_ref, rows, semaphore
 ):
-    moves = (
-        (blocks_hbm, blocks_ref), (p_hbm, p_ref), (masses_hbm, masses_ref), (step_hbm, step_ref),
-        (cycle_hbm, cycle_ref), (vectors_hbm, vectors_ref),
-    )
-    copies = [pltpu.make_async_copy(a, b, semaphores.at[i]) for i, (a, b) in enumerate(moves)]
-    for copy in copies:
-        copy.start()
+    copy = pltpu.make_async_copy(vectors_hbm, vectors_ref, semaphore)
+    copy.start()
     is_odd = lax.axis_index("space") % 2 == 1
     hidden = one_ref.shape[1]
     rows[: one_ref.shape[0], :] = one_ref[...].astype(f32)
@@ -127,8 +122,6 @@
     for i in range(2):
         wide_ref[i] = jnp.broadcast_to(columns[:, i : i + 1], (hidden, CELLS))
 
-    for copy in copies[:-1]:
-        copy.wait()
     depth = blocks_ref.shape[1]
     column = lax.broadcasted_iota(jnp.int32, (beads, depth), 1) // beads
     for matrix_ref, first in ((modes_ref, 0), (modes_t_ref, 2 * beads)):
@@ -139,7 +132,7 @@
             rest = jnp.where(column == c, low, 0.0).astype(bf16)
             matrix_ref[rows_at, :] = jnp.concatenate([mine, mine, rest], axis=1)
     order = lax.broadcasted_iota(jnp.int32, (beads, CELLS), 0).astype(f32)
-    mass = jnp.concatenate([jnp.full((beads, CELLS), masses_ref[c], f32) for c in range(coords)])
+    mass = jnp.concatenate([jnp.broadcast_to(masses_ref[:, c : c + 1], (beads, CELLS)) for c in range(coords)])
     step = step_ref[0]
     half = 0.5 * step
     frequency = 2.0 * cycle_ref[0] * jnp.sin(order * (0.5 * TWO_PI / beads))
@@ -163,7 +156,7 @@
     q_map_ref[...] = left_terms(close_dot(modes_ref[...], (half * drift[:, :1]) * modes_t))
     finish_ref[...] = jnp.concatenate([half / mass, 1.0 / mass], axis=1)
     half_ref[...] = jnp.full(half_ref.shape, half, f32)
-    copies[-1].wait()
+    copy.wait()
 
 
 def put_features(coords, beads, chosen, stage, features, top):
@@ -419,15 +412,16 @@
         wavevectors = lax.dynamic_slice_in_dim(wavevectors, lax.axis_index("space") * share, share, 1)
     inputs = (
         positions.reshape(total, CELLS), layer_one.T, bias_one.reshape(1, hidden), bias_two.reshape(1, hidden),
-        readout.reshape(1, hidden), layer_two,
+        readout.reshape(1, hidden), momenta.reshape(total, CELLS), masses.reshape(1, coords),
+        jnp.asarray(mode_blocks(coords, beads)), layer_two,
     )
     rounded, *brought = call(
         round_kernel, out_shape=(narrow,) + tuple(shape(x.shape, x.dtype) for x in inputs),
-        in_specs=[HBM] * 6, out_specs=(VMEM,) * 7, scratch_shapes=[pltpu.SemaphoreType.DMA((6,))],
+        in_specs=[HBM] * len(inputs), out_specs=(VMEM,) * (len(inputs) + 1),
+        scratch_shapes=[pltpu.SemaphoreType.DMA((len(inputs),))],
     )(*map(in_hbm, inputs))
     two = brought[-1]
 
-    inputs = (momenta.reshape(total, CELLS), jnp.asarray(mode_blocks(coords, beads)), wavevectors)
     (
         forward, outer_forward, backward, two_t, wide, q_base, q_map, p_base, pushed, cosine, finish, half,
         modes, modes_t, wavevectors
@@ -439,13 +433,9 @@
             field, square, field, field, field, shape((total, 2 * CELLS), f32), shape((8, CELLS), f32),
             square, square, shape(wavevectors.shape, wavevectors.dtype),
         ),
-        in_specs=[HBM] * 6 + [VMEM] * 6, out_specs=(VMEM,) * 15,
-        scratch_shapes=[
-            pltpu.VMEM((width, hidden), f32), pltpu.SMEM((coords,), f32), pltpu.SMEM((1,), f32),
-            pltpu.SMEM((1,), f32), pltpu.VMEM((total, CELLS), f32), pltpu.VMEM(inputs[1].shape, f32),
-            pltpu.SemaphoreType.DMA((6,)),
-        ],
-    )(in_hbm(masses), step_size, cycle_frequency, *map(in_hbm, inputs), *brought)
+        in_specs=[SMEM, SMEM, HBM] + [VMEM] * len(brought), out_specs=(VMEM,) * 15,
+        scratch_shapes=[pltpu.VMEM((width, hidden), f32), pltpu.SemaphoreType.DMA],
+    )(step_size, cycle_frequency, in_hbm(wavevectors), *brought)
     layers = (backward, two, two_t, wide)
     stage = pltpu.VMEM((total, CELLS), f32)
 

time: 60.7 us -> 60.5 us (level)
  transfers between devices with their start and end apart: 13 -> 13, of which waited for: 8 -> 8; matrix products, arithmetic and copies ran while one was open for 1% -> 1% of each run, Pallas kernels for 14% -> 13%
where the time goes in v4:
time: 60.5 us; the launch traced here: 60.3 us
  waiting for transfers between devices  32.5 us (54%)
  Pallas kernels  16.1 us (27%)
  starting transfers between devices  8.62 us (14%)
  between operations  2.26 us (4%)
  other arithmetic  0.68 us (1%)
    ppermute x9, waiting for transfers between devices, swap(): lax.ppermute(value, 'space', [(i, i ^ distance) for i in range(lax.axis_s...  15.5 us
    ppermute x2, waiting for transfers between devices, neighbour_planes(): lax.ppermute(plane, 'space', [(i, (i - 2 * step[i]) % count) for i in ran...  12.5 us
    ppermute x2, starting transfers between devices, neighbour_planes(): lax.ppermute(plane, 'space', [(i, (i + step[i]) % count) for i in range(c...  7.45 us
    pallas_call x2, Pallas kernels, forces(): call(functools.partial(own_kernel, coords, beads, len(tied)), out_shape=(...  5.06 us
    pallas_call x2, Pallas kernels, forces(): call(functools.partial(outer_kernel, coords, beads), out_shape=field, in_...  4.56 us
    ppermute x2, waiting for transfers between devices, neighbour_planes(): lax.ppermute(plane, 'space', [(i, (i + step[i]) % count) for i in range(c...  4.5 us
    pallas_call x1, Pallas kernels, on_device(): call(functools.partial(setup_kernel, coords, beads), out_shape=(shape((hi...  1.58 us
    pallas_call x1, Pallas kernels, on_device(): call(functools.partial(push_kernel, share, order), out_shape=(field, fiel...  1.35 us
  transfers between devices with their start and end apart: 13, of which 8 were waited for; matrix products, arithmetic and copies ran while one was open for 1% of the time, Pallas kernels for 13%

profile of v4, /device:TPU:0, one launch (start us, length us, event | category | flops | bytes accessed | tf_op | source)
XLA Modules:
  0.0 60.3 jit_solution(1444423165728495968)
XLA Ops:
  0.6 1.3 %shard_map.139 = (bf16[240,128]{1,0:T(8,128)(2,1)S(1)}, f32[240,128]{1,0:T(8,128)S(1)}, bf16[405,256]{1,0:T(8,128)(2,1)S(1)}, f32[1,256]{1,0:T(1,128)S(1)}, f32[...) custom-call(f32[240,128]{1,0:T(8,128)} %bitcast.20, ...), custom_call_target="tpu_custom_call" | custom-call | tf_op jit(solution)/shard_map/pallas_call | solution.py:418
  1.9 5.5 %collective-permute-start.1 = (bf16[240,128]{1,0:T(8,128)(2,1)S(1)}, bf16[240,128]{1,0:T(8,128)(2,1)S(1)}, u32[]{:S(2)}, u32[]{:S(2)}) collective-permute-start(bf16[240,128]{1,0:T(8,128)(2,1)S(1)} %get-tuple-element.57.own_ref), channel_id=1, source_target_pairs={{0,15},{1,2},{2,1},{3,4},{4,3},{5,6},{6,5},{7,8},{8,7},{9,10},{10,... | collective-permute-start | bytes 184328 | tf_op jit(solution)/shard_map/ppermute | solution.py:370
  7.5 0.0 collective-permute-start.2
  8.8 1.6 %shard_map.140 = (bf16[256,432]{1,0:T(8,128)(2,1)S(1)}, bf16[256,432]{1,0:T(8,128)(2,1)S(1)}, bf16[432,256]{1,0:T(8,128)(2,1)S(1)}, bf16[256,256]{1,0:T(8,128)(2...) custom-call(f32[1]{0:T(128)S(6)} %copy.21.step_ref, ...), custom_call_target="tpu_custom_call" | custom-call | tf_op jit(solution)/shard_map/pallas_call | solution.py:428
  10.4 0.0 collective-permute-done.1.outer_ref
  10.4 0.0 collective-permute-done.2.inner_ref
  10.4 2.5 %shard_map.141 = (f32[240,128]{1,0:T(8,128)S(1)}, f32[144,2048]{1,0:T(8,128)S(1)}, bf16[432,2048]{1,0:T(8,128)(2,1)S(1)}) custom-call(bf16[240,128]{1,0:T(8,128)(2,1)S(1)} %collective-permute-done.1.outer_ref, bf16[240,128]{1,0:T(8,128)(2,1)S(1)} %get-tuple-element.57.own_ref, bf16[240,128]{1,0:T(8,128)(2,1)S(1)} %collective-permute-done.2.inner_ref, ...), custom_call_target="tpu_custom_call" | custom-call | tf_op jit(solution)/shard_map/pallas_call | solution.py:444
  12.9 0.6 collective-permute-start.3
  13.5 0.0 collective-permute-start
  13.5 6.9 %collective-permute-done.outer2_ref = bf16[240,128]{1,0:T(8,128)(2,1)S(1)} collective-permute-done((bf16[240,128]{1,0:T(8,128)(2,1)S(1)}, bf16[240,128]{1,0:T(8,128)(2,1)S(1)}, u32[]{:S(2)}, u32[]{:S(2)}) %collective-permute-start) | collective-permute-done | bytes 61472 | tf_op jit(solution)/shard_map/ppermute | solution.py:372
  20.4 2.3 %shard_map.142.kept_ref = f32[240,128]{1,0:T(8,128)S(1)} custom-call(bf16[240,128]{1,0:T(8,128)(2,1)S(1)} %collective-permute-done.outer2_ref, bf16[432,2048]{1,0:T(8,128)(2,1)S(1)} %get-tuple-element.62.features_ref, f32[144,2048]{1,0:T(8,128)S(1)} %get-tuple-element.63.sums_ref, bf16[256,432]{1,0:T(8,128)(2,1)S(1)} %get-tuple-element.64.forward_ref, ...), custom_call_target="tpu_custom_call" | custom-call | tf_op jit(solution)/shard_map/pallas_call | solution.py:450
  22.7 0.0 collective-permute-done.3.came_ref
  22.7 0.3 shard_map.143
  23.0 1.9 %collective-permute-start.5 = (bf16[240,128]{1,0:T(8,128)(2,1)S(1)}, bf16[240,128]{1,0:T(8,128)(2,1)S(1)}, u32[]{:S(2)}, u32[]{:S(2)}) collective-permute-start(bf16[240,128]{1,0:T(8,128)(2,1)S(1)} %get-tuple-element.79.own_ref), channel_id=1, source_target_pairs={{0,15},{1,2},{2,1},{3,4},{4,3},{5,6},{6,5},{7,8},{8,7},{9,10},{10,... | collective-permute-start | bytes 184328 | tf_op jit(solution)/shard_map/ppermute | solution.py:370
  24.9 0.0 collective-permute-start.6
  24.9 4.5 %collective-permute-done.5.outer_ref = bf16[240,128]{1,0:T(8,128)(2,1)S(1)} collective-permute-done((bf16[240,128]{1,0:T(8,128)(2,1)S(1)}, bf16[240,128]{1,0:T(8,128)(2,1)S(1)}, u32[]{:S(2)}, u32[]{:S(2)}) %collective-permute-start.5) | collective-permute-done | bytes 61472 | tf_op jit(solution)/shard_map/ppermute | solution.py:370
  29.4 0.0 collective-permute-done.6.inner_ref
  29.4 2.5 %shard_map.145 = (f32[240,128]{1,0:T(8,128)S(1)}, f32[144,2048]{1,0:T(8,128)S(1)}, bf16[432,2048]{1,0:T(8,128)(2,1)S(1)}) custom-call(bf16[240,128]{1,0:T(8,128)(2,1)S(1)} %collective-permute-done.5.outer_ref, bf16[240,128]{1,0:T(8,128)(2,1)S(1)} %get-tuple-element.79.own_ref, bf16[240,128]{1,0:T(8,128)(2,1)S(1)} %collective-permute-done.6.inner_ref, ...), custom_call_target="tpu_custom_call" | custom-call | tf_op jit(solution)/shard_map/pallas_call | solution.py:444
  31.9 0.1 collective-permute-start.7
  32.0 0.2 collective-permute-start.4
  32.3 1.4 %shard_map.144 = (f32[240,128]{1,0:T(8,128)}, f32[240,128]{1,0:T(8,128)S(1)}, f32[240,128]{1,0:T(8,128)S(1)}, bf16[240,768]{1,0:T(8,128)(2,1)S(1)}, f32[2,16,256...) custom-call(f32[8,128]{1,0:T(8,128)S(1)} %get-tuple-element.54.half_ref, f32[240,128]{1,0:T(8,128)S(1)} %get-tuple-element.66.q_ref, ...), custom_call_target="tpu_custom_call" | custom-call | tf_op jit(solution)/shard_map/pallas_call | solution.py:461
  33.6 5.6 %collective-permute-done.4.outer2_ref = bf16[240,128]{1,0:T(8,128)(2,1)S(1)} collective-permute-done((bf16[240,128]{1,0:T(8,128)(2,1)S(1)}, bf16[240,128]{1,0:T(8,128)(2,1)S(1)}, u32[]{:S(2)}, u32[]{:S(2)}) %collective-permute-start.4) | collective-permute-done | bytes 61472 | tf_op jit(solution)/shard_map/ppermute | solution.py:372
  39.2 2.3 %shard_map.146.kept_ref = f32[240,128]{1,0:T(8,128)S(1)} custom-call(bf16[240,128]{1,0:T(8,128)(2,1)S(1)} %collective-permute-done.4.outer2_ref, bf16[432,2048]{1,0:T(8,128)(2,1)S(1)} %get-tuple-element.80.features_ref, f32[144,2048]{1,0:T(8,128)S(1)} %get-tuple-element.81.sums_ref, bf16[256,432]{1,0:T(8,128)(2,1)S(1)} %get-tuple-element.64.forward_ref, ...), custom_call_target="tpu_custom_call" | custom-call | tf_op jit(solution)/shard_map/pallas_call | solution.py:450
  41.5 0.0 collective-permute-done.7.came_ref
  41.5 0.3 shard_map.147
  41.8 0.1 collective-permute-start.8
  41.8 5.2 %collective-permute-done.8 = bf16[1,240,128]{2,1,0:T(8,128)(2,1)S(1)} collective-permute-done((bf16[1,240,128]{2,1,0:T(8,128)(2,1)S(1)}, bf16[1,240,128]{2,1,0:T(8,128)(2,1)S(1)}, u32[]{:S(2)}, u32[]{:S(2)}) %collective-permute-start.8) | collective-permute-done | bytes 61472 | tf_op jit(solution)/shard_map/ppermute | solution.py:364
  47.1 0.1 collective-permute-start.9
  47.2 0.1 collective-permute-start.10
  47.2 4.8 %collective-permute-done.9 = bf16[2,240,128]{2,1,0:T(8,128)(2,1)S(1)} collective-permute-done((bf16[2,240,128]{2,1,0:T(8,128)(2,1)S(1)}, bf16[2,240,128]{2,1,0:T(8,128)(2,1)S(1)}, u32[]{:S(2)}, u32[]{:S(2)}) %collective-permute-start.9) | collective-permute-done | bytes 122912 | tf_op jit(solution)/shard_map/ppermute | solution.py:364
  52.0 0.0 collective-permute-start.11
  52.0 0.3 collective-permute-done.10
  52.4 4.5 %collective-permute-done.11 = bf16[2,240,128]{2,1,0:T(8,128)(2,1)S(1)} collective-permute-done((bf16[2,240,128]{2,1,0:T(8,128)(2,1)S(1)}, bf16[2,240,128]{2,1,0:T(8,128)(2,1)S(1)}, u32[]{:S(2)}, u32[]{:S(2)}) %collective-permute-start.11) | collective-permute-done | bytes 122912 | tf_op jit(solution)/shard_map/ppermute | solution.py:364
  56.9 0.1 collective-permute-start.12
  57.0 0.7 %sub.3 = f32[240,128]{1,0:T(8,128)} subtract(f32[240,128]{1,0:T(8,128)S(1)} %get-tuple-element.76, f32[240,128]{1,0:T(8,128)S(1)} %get-tuple-element.83) | non-fusion elementwise | flops 30720 | bytes 368640 | tf_op jit(solution)/shard_map/sub | solution.py:471
  57.6 0.5 shard_map.148.near_ref
  58.1 0.7 %collective-permute-done.12.velocity_ref = bf16[8,240,128]{2,1,0:T(8,128)(2,1)S(1)} collective-permute-done((bf16[8,240,128]{2,1,0:T(8,128)(2,1)S(1)}, bf16[8,240,128]{2,1,0:T(8,128)(2,1)S(1)}, u32[]{:S(2)}, u32[]{:S(2)}) %collective-permute-start.12) | collective-permute-done | bytes 491552 | tf_op jit(solution)/shard_map/ppermute | solution.py:364
  58.8 1.3 %shard_map.149 = f32[480,256]{1,0:T(8,128)} custom-call(f32[480,256]{1,0:T(8,128)S(1)} %shard_map.148.near_ref, bf16[8,240,128]{2,1,0:T(8,128)(2,1)S(1)} %collective-permute-done.12.velocity_ref, f32[2,16,256]{2,1,0:T(8,128)S(1)} %get-tuple-element.85.planes_ref, f32[2,128,256]{2,1,0:T(8,128)S(1)} %get-tuple-element.86.cells_ref), custom_call_target="tpu_custom_call" | custom-call | tf_op jit(solution)/shard_map/pallas_call | solution.py:475
  (6 shorter events, 0.1 us)
Async XLA Ops:
  1.9 8.4 %collective-permute-start.1 = (bf16[240,128]{1,0:T(8,128)(2,1)S(1)}, bf16[240,128]{1,0:T(8,128)(2,1)S(1)}, u32[]{:S(2)}, u32[]{:S(2)}) collective-permute-start(bf16[240,128]{1,0:T(8,128)(2,1)S(1)} %get-tuple-element.57.own_ref), channel_id=1, source_target_pairs={{0,15},{1,2},{2,1},{3,4},{4,3},{5,6},{6,5},{7,8},{8,7},{9,10},{10,... | collective-permute-start | bytes 184328 | tf_op jit(solution)/shard_map/ppermute | solution.py:370
  7.5 2.9 %collective-permute-start.2 = (bf16[240,128]{1,0:T(8,128)(2,1)S(1)}, bf16[240,128]{1,0:T(8,128)(2,1)S(1)}, u32[]{:S(2)}, u32[]{:S(2)}) collective-permute-start(bf16[240,128]{1,0:T(8,128)(2,1)S(1)} %get-tuple-element.57.own_ref), channel_id=1, source_target_pairs={{0,1},{1,0},{2,3},{3,2},{4,5},{5,4},{6,7},{7,6},{8,9},{9,8},{10,11... | collective-permute-start | bytes 184328 | tf_op jit(solution)/shard_map/ppermute | solution.py:364
  12.9 9.8 %collective-permute-start.3 = (f32[240,128]{1,0:T(8,128)S(1)}, f32[240,128]{1,0:T(8,128)S(1)}, u32[]{:S(2)}, u32[]{:S(2)}) collective-permute-start(f32[240,128]{1,0:T(8,128)S(1)} %get-tuple-element.65), channel_id=1, source_target_pairs={{0,1},{1,0},{2,3},{3,2},{4,5},{5,4},{6,7},{7,6},{8,9},{9,8},{10,11... | collective-permute-start | bytes 368648 | tf_op jit(solution)/shard_map/ppermute | solution.py:364
  13.5 6.9 %collective-permute-start = (bf16[240,128]{1,0:T(8,128)(2,1)S(1)}, bf16[240,128]{1,0:T(8,128)(2,1)S(1)}, u32[]{:S(2)}, u32[]{:S(2)}) collective-permute-start(bf16[240,128]{1,0:T(8,128)(2,1)S(1)} %get-tuple-element.57.own_ref), channel_id=1, source_target_pairs={{0,2},{1,15},{2,4},{3,1},{4,6},{5,3},{6,8},{7,5},{8,10},{9,7},{10,... | collective-permute-start | bytes 184328 | tf_op jit(solution)/shard_map/ppermute | solution.py:372
  23.0 6.4 %collective-permute-start.5 = (bf16[240,128]{1,0:T(8,128)(2,1)S(1)}, bf16[240,128]{1,0:T(8,128)(2,1)S(1)}, u32[]{:S(2)}, u32[]{:S(2)}) collective-permute-start(bf16[240,128]{1,0:T(8,128)(2,1)S(1)} %get-tuple-element.79.own_ref), channel_id=1, source_target_pairs={{0,15},{1,2},{2,1},{3,4},{4,3},{5,6},{6,5},{7,8},{8,7},{9,10},{10,... | collective-permute-start | bytes 184328 | tf_op jit(solution)/shard_map/ppermute | solution.py:370
  24.9 4.5 %collective-permute-start.6 = (bf16[240,128]{1,0:T(8,128)(2,1)S(1)}, bf16[240,128]{1,0:T(8,128)(2,1)S(1)}, u32[]{:S(2)}, u32[]{:S(2)}) collective-permute-start(bf16[240,128]{1,0:T(8,128)(2,1)S(1)} %get-tuple-element.79.own_ref), channel_id=1, source_target_pairs={{0,1},{1,0},{2,3},{3,2},{4,5},{5,4},{6,7},{7,6},{8,9},{9,8},{10,11... | collective-permute-start | bytes 184328 | tf_op jit(solution)/shard_map/ppermute | solution.py:364
  31.9 9.5 %collective-permute-start.7 = (f32[240,128]{1,0:T(8,128)S(1)}, f32[240,128]{1,0:T(8,128)S(1)}, u32[]{:S(2)}, u32[]{:S(2)}) collective-permute-start(f32[240,128]{1,0:T(8,128)S(1)} %get-tuple-element.82), channel_id=1, source_target_pairs={{0,1},{1,0},{2,3},{3,2},{4,5},{5,4},{6,7},{7,6},{8,9},{9,8},{10,11... | collective-permute-start | bytes 368648 | tf_op jit(solution)/shard_map/ppermute | solution.py:364
  32.0 7.2 %collective-permute-start.4 = (bf16[240,128]{1,0:T(8,128)(2,1)S(1)}, bf16[240,128]{1,0:T(8,128)(2,1)S(1)}, u32[]{:S(2)}, u32[]{:S(2)}) collective-permute-start(bf16[240,128]{1,0:T(8,128)(2,1)S(1)} %get-tuple-element.79.own_ref), channel_id=1, source_target_pairs={{0,2},{1,15},{2,4},{3,1},{4,6},{5,3},{6,8},{7,5},{8,10},{9,7},{10,... | collective-permute-start | bytes 184328 | tf_op jit(solution)/shard_map/ppermute | solution.py:372
  41.8 5.3 %collective-permute-start.8 = (bf16[1,240,128]{2,1,0:T(8,128)(2,1)S(1)}, bf16[1,240,128]{2,1,0:T(8,128)(2,1)S(1)}, u32[]{:S(2)}, u32[]{:S(2)}) collective-permute-start(bf16[1,240,128]{2,1,0:T(8,128)(2,1)S(1)} %bitcast.16), channel_id=1, source_target_pairs={{0,8},{1,9},{2,10},{3,11},{4,12},{5,13},{6,14},{7,15},{8,0},{9,1},... | collective-permute-start | bytes 184328 | tf_op jit(solution)/shard_map/ppermute | solution.py:364
  47.1 4.9 %collective-permute-start.9 = (bf16[2,240,128]{2,1,0:T(8,128)(2,1)S(1)}, bf16[2,240,128]{2,1,0:T(8,128)(2,1)S(1)}, u32[]{:S(2)}, u32[]{:S(2)}) collective-permute-start(bf16[2,240,128]{2,1,0:T(8,128)(2,1)S(1)} %pad_maximum_fusion), channel_id=1, source_target_pairs={{0,2},{1,3},{2,0},{3,1},{4,6},{5,7},{6,4},{7,5},{8,10},{9,11},{10,... | collective-permute-start | bytes 368648 | tf_op jit(solution)/shard_map/ppermute | solution.py:364
  47.2 5.2 %collective-permute-start.10 = (bf16[2,240,128]{2,1,0:T(8,128)(2,1)S(1)}, bf16[2,240,128]{2,1,0:T(8,128)(2,1)S(1)}, u32[]{:S(2)}, u32[]{:S(2)}) collective-permute-start(bf16[2,240,128]{2,1,0:T(8,128)(2,1)S(1)} %pad_maximum_fusion), channel_id=1, source_target_pairs={{0,4},{1,5},{2,6},{3,7},{4,0},{5,1},{6,2},{7,3},{8,12},{9,13},{10,... | collective-permute-start | bytes 368648 | tf_op jit(solution)/shard_map/ppermute | solution.py:364
  52.0 4.9 %collective-permute-start.11 = (bf16[2,240,128]{2,1,0:T(8,128)(2,1)S(1)}, bf16[2,240,128]{2,1,0:T(8,128)(2,1)S(1)}, u32[]{:S(2)}, u32[]{:S(2)}) collective-permute-start(bf16[2,240,128]{2,1,0:T(8,128)(2,1)S(1)} %collective-permute-done.9), channel_id=1, source_target_pairs={{0,4},{1,5},{2,6},{3,7},{4,0},{5,1},{6,2},{7,3},{8,12},{9,13},{10,... | collective-permute-start | bytes 368648 | tf_op jit(solution)/shard_map/ppermute | solution.py:364
  56.9 1.9 %collective-permute-start.12 = (bf16[8,240,128]{2,1,0:T(8,128)(2,1)S(1)}, bf16[8,240,128]{2,1,0:T(8,128)(2,1)S(1)}, u32[]{:S(2)}, u32[]{:S(2)}) collective-permute-start(bf16[8,240,128]{2,1,0:T(8,128)(2,1)S(1)} %constant_dynamic-update-slice_fusion.velocity_ref), channel_id=1, source_target_pairs={{0,1},{1,0},{2,3},{3,2},{4,5},{5,4},{6,7},{7,6},{8,9},{9,8},{10,11... | collective-permute-start | bytes 1474568 | tf_op jit(solution)/shard_map/ppermute | solution.py:364

commit v5 on v4

--- a/solution.py
+++ b/solution.py
@@ -374,23 +374,20 @@
 
 
 def gather_order(count):
-    order, distance = [0], count // 2
-    while distance:
-        if distance == 4:
-            order, distance = [i ^ d for d in (0, 2, 4, 6) for i in order], 1
-        else:
-            order, distance = [i ^ d for d in (0, distance) for i in order], distance // 2
-    return order
+    if count % 4:
+        return [0, 1]
+    far = list(range(4, count, 4))
+    return [i ^ j for j in (0, 1) for i in [0] + far + [2] + [d ^ 2 for d in far]]
 
 
 def gather_planes(velocity):
-    held, distance = velocity[None], lax.axis_size("space") // 2
-    while distance > 1:
-        if distance == 4:
-            near, far = swap(held, 2), swap(held, 4)
-            held, distance = jnp.concatenate([held, near, far, swap(near, 4)]), 1
-        else:
-            held, distance = jnp.concatenate([held, swap(held, distance)]), distance // 2
+    count = lax.axis_size("space")
+    if count % 4:
+        held = velocity[None]
+    else:
+        near = swap(velocity, 2)
+        far = [swap(velocity, distance) for distance in range(4, count, 4)]
+        held = jnp.stack([velocity] + far + [near] + [swap(x, 2) for x in far])
     return held, swap(held, 1)
 
 

time: 60.5 us -> 56.9 us (0.940)
  waiting for transfers between devices: 32.5 us -> 21.2 us
  starting transfers between devices: 8.62 us -> 16.3 us
    ppermute x9 -> x12, waiting for transfers between devices: 15.5 us -> 4.22 us  [swap(): lax.ppermute(value, 'space', [(i, i ^ distance) for i in range(lax.axis_s...]
    ppermute x9 -> x12, starting transfers between devices: 0.94 us -> 8.64 us  [swap(): lax.ppermute(value, 'space', [(i, i ^ distance) for i in range(lax.axis_s...]
  transfers between devices with their start and end apart: 13 -> 16, of which waited for: 8 -> 9; matrix products, arithmetic and copies ran while one was open for 1% -> 1% of each run, Pallas kernels for 13% -> 14%
where the time goes in v5:
time: 56.9 us; the launch traced here: 56.6 us
  waiting for transfers between devices  21.2 us (37%)
  starting transfers between devices  16.3 us (29%)
  Pallas kernels  16.1 us (28%)
  between operations  2.25 us (4%)
  other arithmetic  0.67 us (1%)
    ppermute x2, waiting for transfers between devices, neighbour_planes(): lax.ppermute(plane, 'space', [(i, (i - 2 * step[i]) % count) for i in ran...  12.5 us
    ppermute x12, starting transfers between devices, swap(): lax.ppermute(value, 'space', [(i, i ^ distance) for i in range(lax.axis_s...  8.64 us
    ppermute x2, starting transfers between devices, neighbour_planes(): lax.ppermute(plane, 'space', [(i, (i + step[i]) % count) for i in range(c...  7.44 us
    pallas_call x2, Pallas kernels, forces(): call(functools.partial(own_kernel, coords, beads, len(tied)), out_shape=(...  5.06 us
    pallas_call x2, Pallas kernels, forces(): call(functools.partial(outer_kernel, coords, beads), out_shape=field, in_...  4.56 us
    ppermute x2, waiting for transfers between devices, neighbour_planes(): lax.ppermute(plane, 'space', [(i, (i + step[i]) % count) for i in range(c...  4.5 us
    ppermute x12, waiting for transfers between devices, swap(): lax.ppermute(value, 'space', [(i, i ^ distance) for i in range(lax.axis_s...  4.22 us
    pallas_call x1, Pallas kernels, on_device(): call(functools.partial(setup_kernel, coords, beads), out_shape=(shape((hi...  1.58 us
  transfers between devices with their start and end apart: 16, of which 9 were waited for; matrix products, arithmetic and copies ran while one was open for 1% of the time, Pallas kernels for 14%

profile of v5, /device:TPU:0, one launch (start us, length us, event | category | flops | bytes accessed | tf_op | source)
XLA Modules:
  0.0 56.6 jit_solution(4526423101329523372)
XLA Ops:
  0.6 1.3 %shard_map.139 = (bf16[240,128]{1,0:T(8,128)(2,1)S(1)}, f32[240,128]{1,0:T(8,128)S(1)}, bf16[405,256]{1,0:T(8,128)(2,1)S(1)}, f32[1,256]{1,0:T(1,128)S(1)}, f32[...) custom-call(f32[240,128]{1,0:T(8,128)} %bitcast.32, ...), custom_call_target="tpu_custom_call" | custom-call | tf_op jit(solution)/shard_map/pallas_call | solution.py:415
  1.9 5.5 %collective-permute-start.1 = (bf16[240,128]{1,0:T(8,128)(2,1)S(1)}, bf16[240,128]{1,0:T(8,128)(2,1)S(1)}, u32[]{:S(2)}, u32[]{:S(2)}) collective-permute-start(bf16[240,128]{1,0:T(8,128)(2,1)S(1)} %get-tuple-element.57.own_ref), channel_id=1, source_target_pairs={{0,15},{1,2},{2,1},{3,4},{4,3},{5,6},{6,5},{7,8},{8,7},{9,10},{10,... | collective-permute-start | bytes 184328 | tf_op jit(solution)/shard_map/ppermute | solution.py:370
  7.5 0.0 collective-permute-start.2
  8.8 1.6 %shard_map.140 = (bf16[256,432]{1,0:T(8,128)(2,1)S(1)}, bf16[256,432]{1,0:T(8,128)(2,1)S(1)}, bf16[432,256]{1,0:T(8,128)(2,1)S(1)}, bf16[256,256]{1,0:T(8,128)(2...) custom-call(f32[1]{0:T(128)S(6)} %copy.24.step_ref, ...), custom_call_target="tpu_custom_call" | custom-call | tf_op jit(solution)/shard_map/pallas_call | solution.py:425
  10.4 0.0 collective-permute-done.1.outer_ref
  10.4 0.0 collective-permute-done.2.inner_ref
  10.4 2.5 %shard_map.141 = (f32[240,128]{1,0:T(8,128)S(1)}, f32[144,2048]{1,0:T(8,128)S(1)}, bf16[432,2048]{1,0:T(8,128)(2,1)S(1)}) custom-call(bf16[240,128]{1,0:T(8,128)(2,1)S(1)} %collective-permute-done.1.outer_ref, bf16[240,128]{1,0:T(8,128)(2,1)S(1)} %get-tuple-element.57.own_ref, bf16[240,128]{1,0:T(8,128)(2,1)S(1)} %collective-permute-done.2.inner_ref, ...), custom_call_target="tpu_custom_call" | custom-call | tf_op jit(solution)/shard_map/pallas_call | solution.py:441
  12.9 0.6 %collective-permute-start.3 = (f32[240,128]{1,0:T(8,128)S(1)}, f32[240,128]{1,0:T(8,128)S(1)}, u32[]{:S(2)}, u32[]{:S(2)}) collective-permute-start(f32[240,128]{1,0:T(8,128)S(1)} %get-tuple-element.65), channel_id=1, source_target_pairs={{0,1},{1,0},{2,3},{3,2},{4,5},{5,4},{6,7},{7,6},{8,9},{9,8},{10,11... | collective-permute-start | bytes 368648 | tf_op jit(solution)/shard_map/ppermute | solution.py:364
  13.5 0.0 collective-permute-start
  13.5 6.9 %collective-permute-done.outer2_ref = bf16[240,128]{1,0:T(8,128)(2,1)S(1)} collective-permute-done((bf16[240,128]{1,0:T(8,128)(2,1)S(1)}, bf16[240,128]{1,0:T(8,128)(2,1)S(1)}, u32[]{:S(2)}, u32[]{:S(2)}) %collective-permute-start) | collective-permute-done | bytes 61472 | tf_op jit(solution)/shard_map/ppermute | solution.py:372
  20.4 2.3 %shard_map.142.kept_ref = f32[240,128]{1,0:T(8,128)S(1)} custom-call(bf16[240,128]{1,0:T(8,128)(2,1)S(1)} %collective-permute-done.outer2_ref, bf16[432,2048]{1,0:T(8,128)(2,1)S(1)} %get-tuple-element.62.features_ref, f32[144,2048]{1,0:T(8,128)S(1)} %get-tuple-element.63.sums_ref, bf16[256,432]{1,0:T(8,128)(2,1)S(1)} %get-tuple-element.64.forward_ref, ...), custom_call_target="tpu_custom_call" | custom-call | tf_op jit(solution)/shard_map/pallas_call | solution.py:447
  22.7 0.0 collective-permute-done.3.came_ref
  22.7 0.3 shard_map.143
  23.0 1.9 %collective-permute-start.5 = (bf16[240,128]{1,0:T(8,128)(2,1)S(1)}, bf16[240,128]{1,0:T(8,128)(2,1)S(1)}, u32[]{:S(2)}, u32[]{:S(2)}) collective-permute-start(bf16[240,128]{1,0:T(8,128)(2,1)S(1)} %get-tuple-element.79.own_ref), channel_id=1, source_target_pairs={{0,15},{1,2},{2,1},{3,4},{4,3},{5,6},{6,5},{7,8},{8,7},{9,10},{10,... | collective-permute-start | bytes 184328 | tf_op jit(solution)/shard_map/ppermute | solution.py:370
  24.9 0.0 collective-permute-start.6
  24.9 4.5 %collective-permute-done.5.outer_ref = bf16[240,128]{1,0:T(8,128)(2,1)S(1)} collective-permute-done((bf16[240,128]{1,0:T(8,128)(2,1)S(1)}, bf16[240,128]{1,0:T(8,128)(2,1)S(1)}, u32[]{:S(2)}, u32[]{:S(2)}) %collective-permute-start.5) | collective-permute-done | bytes 61472 | tf_op jit(solution)/shard_map/ppermute | solution.py:370
  29.4 0.0 collective-permute-done.6.inner_ref
  29.4 2.5 %shard_map.145 = (f32[240,128]{1,0:T(8,128)S(1)}, f32[144,2048]{1,0:T(8,128)S(1)}, bf16[432,2048]{1,0:T(8,128)(2,1)S(1)}) custom-call(bf16[240,128]{1,0:T(8,128)(2,1)S(1)} %collective-permute-done.5.outer_ref, bf16[240,128]{1,0:T(8,128)(2,1)S(1)} %get-tuple-element.79.own_ref, bf16[240,128]{1,0:T(8,128)(2,1)S(1)} %collective-permute-done.6.inner_ref, ...), custom_call_target="tpu_custom_call" | custom-call | tf_op jit(solution)/shard_map/pallas_call | solution.py:441
  32.0 0.1 collective-permute-start.7
  32.0 0.2 collective-permute-start.4
  32.3 1.4 %shard_map.144 = (f32[240,128]{1,0:T(8,128)}, f32[240,128]{1,0:T(8,128)S(1)}, f32[240,128]{1,0:T(8,128)S(1)}, bf16[240,768]{1,0:T(8,128)(2,1)S(1)}, f32[2,16,256...) custom-call(f32[8,128]{1,0:T(8,128)S(1)} %get-tuple-element.54.half_ref, f32[240,128]{1,0:T(8,128)S(1)} %get-tuple-element.66.q_ref, ...), custom_call_target="tpu_custom_call" | custom-call | tf_op jit(solution)/shard_map/pallas_call | solution.py:458
  33.6 5.6 %collective-permute-done.4.outer2_ref = bf16[240,128]{1,0:T(8,128)(2,1)S(1)} collective-permute-done((bf16[240,128]{1,0:T(8,128)(2,1)S(1)}, bf16[240,128]{1,0:T(8,128)(2,1)S(1)}, u32[]{:S(2)}, u32[]{:S(2)}) %collective-permute-start.4) | collective-permute-done | bytes 61472 | tf_op jit(solution)/shard_map/ppermute | solution.py:372
  39.2 2.3 %shard_map.146.kept_ref = f32[240,128]{1,0:T(8,128)S(1)} custom-call(bf16[240,128]{1,0:T(8,128)(2,1)S(1)} %collective-permute-done.4.outer2_ref, bf16[432,2048]{1,0:T(8,128)(2,1)S(1)} %get-tuple-element.80.features_ref, f32[144,2048]{1,0:T(8,128)S(1)} %get-tuple-element.81.sums_ref, bf16[256,432]{1,0:T(8,128)(2,1)S(1)} %get-tuple-element.64.forward_ref, ...), custom_call_target="tpu_custom_call" | custom-call | tf_op jit(solution)/shard_map/pallas_call | solution.py:447
  41.5 0.0 collective-permute-done.7.came_ref
  41.5 0.3 shard_map.147
  41.8 0.1 collective-permute-start.8
  41.8 0.1 collective-permute-start.9
  41.9 4.3 %collective-permute-start.10 = (bf16[240,128]{1,0:T(8,128)(2,1)S(1)}, bf16[240,128]{1,0:T(8,128)(2,1)S(1)}, u32[]{:S(2)}, u32[]{:S(2)}) collective-permute-start(bf16[240,128]{1,0:T(8,128)(2,1)S(1)} %get-tuple-element.84), channel_id=1, source_target_pairs={{0,12},{1,13},{2,14},{3,15},{4,8},{5,9},{6,10},{7,11},{8,4},{9,5},... | collective-permute-start | bytes 184328 | tf_op jit(solution)/shard_map/ppermute | solution.py:364
  46.2 0.0 collective-permute-start.11
  46.2 0.0 collective-permute-done.8
  46.2 2.0 %collective-permute-start.12 = (bf16[240,128]{1,0:T(8,128)(2,1)S(1)}, bf16[240,128]{1,0:T(8,128)(2,1)S(1)}, u32[]{:S(2)}, u32[]{:S(2)}) collective-permute-start(bf16[240,128]{1,0:T(8,128)(2,1)S(1)} %collective-permute-done.8), channel_id=1, source_target_pairs={{0,2},{1,3},{2,0},{3,1},{4,6},{5,7},{6,4},{7,5},{8,10},{9,11},{10,... | collective-permute-start | bytes 184328 | tf_op jit(solution)/shard_map/ppermute | solution.py:364
  48.3 0.0 collective-permute-done.9
  48.3 0.1 collective-permute-start.13
  48.4 0.7 %collective-permute-done.10 = bf16[240,128]{1,0:T(8,128)(2,1)S(1)} collective-permute-done((bf16[240,128]{1,0:T(8,128)(2,1)S(1)}, bf16[240,128]{1,0:T(8,128)(2,1)S(1)}, u32[]{:S(2)}, u32[]{:S(2)}) %collective-permute-start.10) | collective-permute-done | bytes 61472 | tf_op jit(solution)/shard_map/ppermute | solution.py:364
  49.1 1.4 %collective-permute-start.14 = (bf16[240,128]{1,0:T(8,128)(2,1)S(1)}, bf16[240,128]{1,0:T(8,128)(2,1)S(1)}, u32[]{:S(2)}, u32[]{:S(2)}) collective-permute-start(bf16[240,128]{1,0:T(8,128)(2,1)S(1)} %collective-permute-done.10), channel_id=1, source_target_pairs={{0,2},{1,3},{2,0},{3,1},{4,6},{5,7},{6,4},{7,5},{8,10},{9,11},{10,... | collective-permute-start | bytes 184328 | tf_op jit(solution)/shard_map/ppermute | solution.py:364
  50.5 0.3 collective-permute-done.11
  50.8 0.9 %collective-permute-done.12 = bf16[240,128]{1,0:T(8,128)(2,1)S(1)} collective-permute-done((bf16[240,128]{1,0:T(8,128)(2,1)S(1)}, bf16[240,128]{1,0:T(8,128)(2,1)S(1)}, u32[]{:S(2)}, u32[]{:S(2)}) %collective-permute-start.12) | collective-permute-done | bytes 61472 | tf_op jit(solution)/shard_map/ppermute | solution.py:364
  51.8 0.8 %collective-permute-done.13 = bf16[240,128]{1,0:T(8,128)(2,1)S(1)} collective-permute-done((bf16[240,128]{1,0:T(8,128)(2,1)S(1)}, bf16[240,128]{1,0:T(8,128)(2,1)S(1)}, u32[]{:S(2)}, u32[]{:S(2)}) %collective-permute-start.13) | collective-permute-done | bytes 61472 | tf_op jit(solution)/shard_map/ppermute | solution.py:364
  52.6 0.7 %collective-permute-done.14 = bf16[240,128]{1,0:T(8,128)(2,1)S(1)} collective-permute-done((bf16[240,128]{1,0:T(8,128)(2,1)S(1)}, bf16[240,128]{1,0:T(8,128)(2,1)S(1)}, u32[]{:S(2)}, u32[]{:S(2)}) %collective-permute-start.14) | collective-permute-done | bytes 61472 | tf_op jit(solution)/shard_map/ppermute | solution.py:364
  53.3 0.1 collective-permute-start.15
  53.4 0.7 %sub.3 = f32[240,128]{1,0:T(8,128)} subtract(f32[240,128]{1,0:T(8,128)S(1)} %get-tuple-element.76, f32[240,128]{1,0:T(8,128)S(1)} %get-tuple-element.83) | non-fusion elementwise | flops 30720 | bytes 368640 | tf_op jit(solution)/shard_map/sub | solution.py:468
  54.0 0.5 shard_map.148.near_ref
  54.5 0.7 %collective-permute-done.15.velocity_ref = bf16[8,240,128]{2,1,0:T(8,128)(2,1)S(1)} collective-permute-done((bf16[8,240,128]{2,1,0:T(8,128)(2,1)S(1)}, bf16[8,240,128]{2,1,0:T(8,128)(2,1)S(1)}, u32[]{:S(2)}, u32[]{:S(2)}) %collective-permute-start.15) | collective-permute-done | bytes 491552 | tf_op jit(solution)/shard_map/ppermute | solution.py:364
  55.2 1.3 %shard_map.149 = f32[480,256]{1,0:T(8,128)} custom-call(f32[480,256]{1,0:T(8,128)S(1)} %shard_map.148.near_ref, bf16[8,240,128]{2,1,0:T(8,128)(2,1)S(1)} %collective-permute-done.15.velocity_ref, f32[2,16,256]{2,1,0:T(8,128)S(1)} %get-tuple-element.85.planes_ref, f32[2,128,256]{2,1,0:T(8,128)S(1)} %get-tuple-element.86.cells_ref), custom_call_target="tpu_custom_call" | custom-call | tf_op jit(solution)/shard_map/pallas_call | solution.py:472
  (8 shorter events, 0.1 us)
Async XLA Ops:
  1.9 8.4 %collective-permute-start.1 = (bf16[240,128]{1,0:T(8,128)(2,1)S(1)}, bf16[240,128]{1,0:T(8,128)(2,1)S(1)}, u32[]{:S(2)}, u32[]{:S(2)}) collective-permute-start(bf16[240,128]{1,0:T(8,128)(2,1)S(1)} %get-tuple-element.57.own_ref), channel_id=1, source_target_pairs={{0,15},{1,2},{2,1},{3,4},{4,3},{5,6},{6,5},{7,8},{8,7},{9,10},{10,... | collective-permute-start | bytes 184328 | tf_op jit(solution)/shard_map/ppermute | solution.py:370
  7.5 2.9 %collective-permute-start.2 = (bf16[240,128]{1,0:T(8,128)(2,1)S(1)}, bf16[240,128]{1,0:T(8,128)(2,1)S(1)}, u32[]{:S(2)}, u32[]{:S(2)}) collective-permute-start(bf16[240,128]{1,0:T(8,128)(2,1)S(1)} %get-tuple-element.57.own_ref), channel_id=1, source_target_pairs={{0,1},{1,0},{2,3},{3,2},{4,5},{5,4},{6,7},{7,6},{8,9},{9,8},{10,11... | collective-permute-start | bytes 184328 | tf_op jit(solution)/shard_map/ppermute | solution.py:364
  12.9 9.8 %collective-permute-start.3 = (f32[240,128]{1,0:T(8,128)S(1)}, f32[240,128]{1,0:T(8,128)S(1)}, u32[]{:S(2)}, u32[]{:S(2)}) collective-permute-start(f32[240,128]{1,0:T(8,128)S(1)} %get-tuple-element.65), channel_id=1, source_target_pairs={{0,1},{1,0},{2,3},{3,2},{4,5},{5,4},{6,7},{7,6},{8,9},{9,8},{10,11... | collective-permute-start | bytes 368648 | tf_op jit(solution)/shard_map/ppermute | solution.py:364
  13.5 6.9 %collective-permute-start = (bf16[240,128]{1,0:T(8,128)(2,1)S(1)}, bf16[240,128]{1,0:T(8,128)(2,1)S(1)}, u32[]{:S(2)}, u32[]{:S(2)}) collective-permute-start(bf16[240,128]{1,0:T(8,128)(2,1)S(1)} %get-tuple-element.57.own_ref), channel_id=1, source_target_pairs={{0,2},{1,15},{2,4},{3,1},{4,6},{5,3},{6,8},{7,5},{8,10},{9,7},{10,... | collective-permute-start | bytes 184328 | tf_op jit(solution)/shard_map/ppermute | solution.py:372
  23.0 6.4 %collective-permute-start.5 = (bf16[240,128]{1,0:T(8,128)(2,1)S(1)}, bf16[240,128]{1,0:T(8,128)(2,1)S(1)}, u32[]{:S(2)}, u32[]{:S(2)}) collective-permute-start(bf16[240,128]{1,0:T(8,128)(2,1)S(1)} %get-tuple-element.79.own_ref), channel_id=1, source_target_pairs={{0,15},{1,2},{2,1},{3,4},{4,3},{5,6},{6,5},{7,8},{8,7},{9,10},{10,... | collective-permute-start | bytes 184328 | tf_op jit(solution)/shard_map/ppermute | solution.py:370
  24.9 4.5 %collective-permute-start.6 = (bf16[240,128]{1,0:T(8,128)(2,1)S(1)}, bf16[240,128]{1,0:T(8,128)(2,1)S(1)}, u32[]{:S(2)}, u32[]{:S(2)}) collective-permute-start(bf16[240,128]{1,0:T(8,128)(2,1)S(1)} %get-tuple-element.79.own_ref), channel_id=1, source_target_pairs={{0,1},{1,0},{2,3},{3,2},{4,5},{5,4},{6,7},{7,6},{8,9},{9,8},{10,11... | collective-permute-start | bytes 184328 | tf_op jit(solution)/shard_map/ppermute | solution.py:364
  32.0 9.5 %collective-permute-start.7 = (f32[240,128]{1,0:T(8,128)S(1)}, f32[240,128]{1,0:T(8,128)S(1)}, u32[]{:S(2)}, u32[]{:S(2)}) collective-permute-start(f32[240,128]{1,0:T(8,128)S(1)} %get-tuple-element.82), channel_id=1, source_target_pairs={{0,1},{1,0},{2,3},{3,2},{4,5},{5,4},{6,7},{7,6},{8,9},{9,8},{10,11... | collective-permute-start | bytes 368648 | tf_op jit(solution)/shard_map/ppermute | solution.py:364
  32.0 7.2 %collective-permute-start.4 = (bf16[240,128]{1,0:T(8,128)(2,1)S(1)}, bf16[240,128]{1,0:T(8,128)(2,1)S(1)}, u32[]{:S(2)}, u32[]{:S(2)}) collective-permute-start(bf16[240,128]{1,0:T(8,128)(2,1)S(1)} %get-tuple-element.79.own_ref), channel_id=1, source_target_pairs={{0,2},{1,15},{2,4},{3,1},{4,6},{5,3},{6,8},{7,5},{8,10},{9,7},{10,... | collective-permute-start | bytes 184328 | tf_op jit(solution)/shard_map/ppermute | solution.py:372
  41.8 4.5 %collective-permute-start.8 = (bf16[240,128]{1,0:T(8,128)(2,1)S(1)}, bf16[240,128]{1,0:T(8,128)(2,1)S(1)}, u32[]{:S(2)}, u32[]{:S(2)}) collective-permute-start(bf16[240,128]{1,0:T(8,128)(2,1)S(1)} %get-tuple-element.84), channel_id=1, source_target_pairs={{0,4},{1,5},{2,6},{3,7},{4,0},{5,1},{6,2},{7,3},{8,12},{9,13},{10,... | collective-permute-start | bytes 184328 | tf_op jit(solution)/shard_map/ppermute | solution.py:364
  41.8 6.4 %collective-permute-start.9 = (bf16[240,128]{1,0:T(8,128)(2,1)S(1)}, bf16[240,128]{1,0:T(8,128)(2,1)S(1)}, u32[]{:S(2)}, u32[]{:S(2)}) collective-permute-start(bf16[240,128]{1,0:T(8,128)(2,1)S(1)} %get-tuple-element.84), channel_id=1, source_target_pairs={{0,8},{1,9},{2,10},{3,11},{4,12},{5,13},{6,14},{7,15},{8,0},{9,1},... | collective-permute-start | bytes 184328 | tf_op jit(solution)/shard_map/ppermute | solution.py:364
  41.9 7.1 %collective-permute-start.10 = (bf16[240,128]{1,0:T(8,128)(2,1)S(1)}, bf16[240,128]{1,0:T(8,128)(2,1)S(1)}, u32[]{:S(2)}, u32[]{:S(2)}) collective-permute-start(bf16[240,128]{1,0:T(8,128)(2,1)S(1)} %get-tuple-element.84), channel_id=1, source_target_pairs={{0,12},{1,13},{2,14},{3,15},{4,8},{5,9},{6,10},{7,11},{8,4},{9,5},... | collective-permute-start | bytes 184328 | tf_op jit(solution)/shard_map/ppermute | solution.py:364
  46.2 4.6 %collective-permute-start.11 = (bf16[240,128]{1,0:T(8,128)(2,1)S(1)}, bf16[240,128]{1,0:T(8,128)(2,1)S(1)}, u32[]{:S(2)}, u32[]{:S(2)}) collective-permute-start(bf16[240,128]{1,0:T(8,128)(2,1)S(1)} %get-tuple-element.84), channel_id=1, source_target_pairs={{0,2},{1,3},{2,0},{3,1},{4,6},{5,7},{6,4},{7,5},{8,10},{9,11},{10,... | collective-permute-start | bytes 184328 | tf_op jit(solution)/shard_map/ppermute | solution.py:364
  46.2 5.5 %collective-permute-start.12 = (bf16[240,128]{1,0:T(8,128)(2,1)S(1)}, bf16[240,128]{1,0:T(8,128)(2,1)S(1)}, u32[]{:S(2)}, u32[]{:S(2)}) collective-permute-start(bf16[240,128]{1,0:T(8,128)(2,1)S(1)} %collective-permute-done.8), channel_id=1, source_target_pairs={{0,2},{1,3},{2,0},{3,1},{4,6},{5,7},{6,4},{7,5},{8,10},{9,11},{10,... | collective-permute-start | bytes 184328 | tf_op jit(solution)/shard_map/ppermute | solution.py:364
  48.3 4.3 %collective-permute-start.13 = (bf16[240,128]{1,0:T(8,128)(2,1)S(1)}, bf16[240,128]{1,0:T(8,128)(2,1)S(1)}, u32[]{:S(2)}, u32[]{:S(2)}) collective-permute-start(bf16[240,128]{1,0:T(8,128)(2,1)S(1)} %collective-permute-done.9), channel_id=1, source_target_pairs={{0,2},{1,3},{2,0},{3,1},{4,6},{5,7},{6,4},{7,5},{8,10},{9,11},{10,... | collective-permute-start | bytes 184328 | tf_op jit(solution)/shard_map/ppermute | solution.py:364
  49.1 4.2 %collective-permute-start.14 = (bf16[240,128]{1,0:T(8,128)(2,1)S(1)}, bf16[240,128]{1,0:T(8,128)(2,1)S(1)}, u32[]{:S(2)}, u32[]{:S(2)}) collective-permute-start(bf16[240,128]{1,0:T(8,128)(2,1)S(1)} %collective-permute-done.10), channel_id=1, source_target_pairs={{0,2},{1,3},{2,0},{3,1},{4,6},{5,7},{6,4},{7,5},{8,10},{9,11},{10,... | collective-permute-start | bytes 184328 | tf_op jit(solution)/shard_map/ppermute | solution.py:364
  53.3 1.9 %collective-permute-start.15 = (bf16[8,240,128]{2,1,0:T(8,128)(2,1)S(1)}, bf16[8,240,128]{2,1,0:T(8,128)(2,1)S(1)}, u32[]{:S(2)}, u32[]{:S(2)}) collective-permute-start(bf16[8,240,128]{2,1,0:T(8,128)(2,1)S(1)} %bitcast_dynamic-update-slice_fusion.velocity_ref), channel_id=1, source_target_pairs={{0,1},{1,0},{2,3},{3,2},{4,5},{5,4},{6,7},{7,6},{8,9},{9,8},{10,11... | collective-permute-start | bytes 1474568 | tf_op jit(solution)/shard_map/ppermute | solution.py:364

commit v6 on v5

--- a/solution.py
+++ b/solution.py
@@ -280,7 +280,7 @@
 
 def push_kernel(
     share, planes_at, half_ref, q_ref, sum_ref, p_base_ref, pushed_ref, cosine_ref, finish_ref, modes_ref,
-    modes_t_ref, vectors_ref, q_out, p_out, velocity_out, velocity_map_out, planes_out, cells_out
+    modes_t_ref, vectors_ref, q_out, p_out, velocity_out, velocity_map_out, planes_out, cells_out, trig_out
 ):
     depth = modes_ref.shape[1] // 3
     q_out[...] = q_ref[...]
@@ -303,6 +303,10 @@
         angle = TWO_PI * (numerator & (whole - 1)).astype(f32) / whole
         out[0] = jnp.cos(angle)
         out[1] = jnp.sin(angle)
+    half = extent_x // 2
+    for i in range(half):
+        for part in range(2):
+            trig_out[part, i * CELLS : (i + 1) * CELLS, :] = plane_trig(planes_out, cells_out, part, half + i)
 
 
 def finish_kernel(half_ref, velocity_ref, map_ref, kept_ref, came_ref, velocity_out, kick_out):
@@ -311,36 +315,37 @@
     kick_out[...] = half_ref[0:1, :] * sums
 
 
-def projected(velocity_ref, planes_ref, cells_ref, first, part):
-    cos_cell, sin_cell = cells_ref[0], cells_ref[1]
-
-    def trig(i):
-        cos_plane, sin_plane = (planes_ref[t, first + i : first + i + 1, :] for t in range(2))
-        if part == 0:
-            return (cos_plane * cos_cell - sin_plane * sin_cell).astype(bf16)
-        return (sin_plane * cos_cell + cos_plane * sin_cell).astype(bf16)
-
+def projected(velocity_ref, trig):
+    count = velocity_ref.shape[0]
     total = 0.0
-    for i in range(0, velocity_ref.shape[0] - 1, 2):
+    for i in range(0, count - 1, 2):
         block = jnp.concatenate([velocity_ref[i], velocity_ref[i + 1]], axis=1)
         total += dot(block, jnp.concatenate([trig(i), trig(i + 1)]))
-    if velocity_ref.shape[0] % 2:
-        total += dot(velocity_ref[velocity_ref.shape[0] - 1], trig(velocity_ref.shape[0] - 1))
-    return total
-
-
-def near_project_kernel(velocity_ref, planes_ref, cells_ref, out_ref):
+    return total + dot(velocity_ref[count - 1], trig(count - 1)) if count % 2 else total
+
+
+def plane_trig(planes_ref, cells_ref, part, i):
+    cos_plane, sin_plane = (planes_ref[t, i : i + 1, :] for t in range(2))
+    if part == 0:
+        return (cos_plane * cells_ref[0] - sin_plane * cells_ref[1]).astype(bf16)
+    return (sin_plane * cells_ref[0] + cos_plane * cells_ref[1]).astype(bf16)
+
+
+def near_project_kernel(own_ref, other_ref, planes_ref, cells_ref, trig_ref, out_ref):
+    fields = own_ref.shape[1]
+    for part in range(2):
+        own = projected(own_ref, functools.partial(plane_trig, planes_ref, cells_ref, part))
+        other = projected(other_ref, lambda i: trig_ref[part, i * CELLS : (i + 1) * CELLS, :])
+        out_ref[part * fields : (part + 1) * fields, :] = own + other
+
+
+def project_kernel(scale, first, near_ref, velocity_ref, trig_ref, out_hbm, result, semaphores):
     fields = velocity_ref.shape[1]
-    for part in range(2):
-        out_ref[part * fields : (part + 1) * fields, :] = projected(velocity_ref, planes_ref, cells_ref, 0, part)
-
-
-def project_kernel(scale, near_ref, velocity_ref, planes_ref, cells_ref, out_hbm, result, semaphores):
-    count, fields, _ = velocity_ref.shape
     copies = []
     for part in range(2):
         rows = slice(part * fields, (part + 1) * fields)
-        result[rows, :] = (near_ref[rows, :] + projected(velocity_ref, planes_ref, cells_ref, count, part)) * scale
+        last = projected(velocity_ref, lambda i: trig_ref[part, (first + i) * CELLS : (first + i + 1) * CELLS, :])
+        result[rows, :] = (near_ref[rows, :] + last) * scale
         copies.append(pltpu.make_async_copy(result.at[rows, :], out_hbm.at[rows, :], semaphores.at[part]))
         copies[-1].start()
     for copy in copies:
@@ -382,13 +387,16 @@
 
 def gather_planes(velocity):
     count = lax.axis_size("space")
-    if count % 4:
-        held = velocity[None]
-    else:
+    first, second = [velocity], []
+    if count % 4 == 0:
         near = swap(velocity, 2)
         far = [swap(velocity, distance) for distance in range(4, count, 4)]
-        held = jnp.stack([velocity] + far + [near] + [swap(x, 2) for x in far])
-    return held, swap(held, 1)
+        first = first + far + [near]
+        second = [swap(x, 2) for x in far]
+    if not second:
+        first, second = first[:-1], first[-1:]
+    others = swap(jnp.stack(first), 1) if first else None
+    return jnp.stack(first + second), others, swap(jnp.stack(second), 1)
 
 
 def on_device(
@@ -397,7 +405,7 @@
 ):
     coords, beads, planes, cells = positions.shape
     devices = lax.axis_size("space")
-    assert planes == 1 and cells == CELLS and devices & (devices - 1) == 0 and devices > 1
+    assert planes == 1 and cells == CELLS and devices & (devices - 1) == 0 and devices > 2
     total = coords * beads
     hidden = layer_one.shape[0]
     width = 27 * PAD
@@ -412,11 +420,12 @@
         readout.reshape(1, hidden), momenta.reshape(total, CELLS), masses.reshape(1, coords),
         jnp.asarray(mode_blocks(coords, beads)), layer_two,
     )
-    rounded, *brought = call(
-        round_kernel, out_shape=(narrow,) + tuple(shape(x.shape, x.dtype) for x in inputs),
-        in_specs=[HBM] * len(inputs), out_specs=(VMEM,) * (len(inputs) + 1),
-        scratch_shapes=[pltpu.SemaphoreType.DMA((len(inputs),))],
-    )(*map(in_hbm, inputs))
+    rounded, q = call(
+        round_kernel, out_shape=(narrow, field), in_specs=[HBM], out_specs=(VMEM,) * 2,
+        scratch_shapes=[pltpu.SemaphoreType.DMA((1,))],
+        cost_estimate=pl.CostEstimate(flops=10**10, bytes_accessed=10**8, transcendentals=0),
+    )(in_hbm(inputs[0]))
+    brought = (q, *inputs[1:])
     two = brought[-1]
 
     (
@@ -455,25 +464,28 @@
         move_kernel, out_shape=(field, narrow, field), in_specs=[VMEM] * 4, out_specs=(VMEM,) * 3,
     )(q_base, q_map, *forces(rounded))
     order = gather_order(devices)
-    q_new, p_mid, velocity_base, velocity_map, across, along = call(
+    q_new, p_mid, velocity_base, velocity_map, across, along, trig = call(
         functools.partial(push_kernel, share, order),
         out_shape=(
             field, field, field, square, shape((2, devices, share), f32), shape((2, CELLS, share), f32),
+            shape((2, devices // 2 * CELLS, share), bf16),
         ),
-        in_specs=[VMEM] * 10, out_specs=(VMEM,) * 6,
+        in_specs=[VMEM] * 10, out_specs=(VMEM,) * 7,
     )(half, q_moved, sums, p_base, pushed, cosine, finish, modes, modes_t, wavevectors)
     velocity, kick = call(
         finish_kernel, out_shape=(narrow, field), in_specs=[VMEM] * 5, out_specs=(VMEM,) * 2,
     )(half, velocity_base, velocity_map, *forces(rounded))
     p_new = p_mid - kick
-    held, last = gather_planes(velocity)
+    held, others, last = gather_planes(velocity)
     spectrum = shape((2 * total, share), f32)
-    near = call(near_project_kernel, out_shape=spectrum, in_specs=[VMEM] * 3, out_specs=VMEM)(held, across, along)
+    near = call(near_project_kernel, out_shape=spectrum, in_specs=[VMEM] * 5, out_specs=VMEM)(
+        held, others, across, along, trig
+    )
     spectrum = call(
-        functools.partial(project_kernel, 1.0 / math.sqrt(devices * CELLS)),
-        out_shape=spectrum, in_specs=[VMEM] * 4, out_specs=HBM,
+        functools.partial(project_kernel, 1.0 / math.sqrt(devices * CELLS), others.shape[0]),
+        out_shape=spectrum, in_specs=[VMEM] * 3, out_specs=HBM,
         scratch_shapes=[pltpu.VMEM((2 * total, share), f32), pltpu.SemaphoreType.DMA((2,))],
-    )(near, last, across, along)
+    )(near, last, trig)
     return q_new.reshape(positions.shape), p_new.reshape(momenta.shape), spectrum.T
 
 

time: 56.9 us -> 56.7 us (level)
  waiting for transfers between devices: 21.2 us -> 20.2 us
  starting transfers between devices: 16.3 us -> 16.9 us
    ppermute x12 -> x13, waiting for transfers between devices: 4.22 us -> 3.36 us  [swap(): lax.ppermute(value, 'space', [(i, i ^ distance) for i in range(lax.axis_s...]
    ppermute x12 -> x13, starting transfers between devices: 8.64 us -> 9.33 us  [swap(): lax.ppermute(value, 'space', [(i, i ^ distance) for i in range(lax.axis_s...]
  transfers between devices with their start and end apart: 16 -> 17, of which waited for: 9 -> 7; matrix products, arithmetic and copies ran while one was open for 1% -> 1% of each run, Pallas kernels for 14% -> 15%
where the time goes in v6:
time: 56.7 us; the launch traced here: 56.5 us
  waiting for transfers between devices  20.2 us (36%)
  starting transfers between devices  16.9 us (30%)
  Pallas kernels  16 us (28%)
  between operations  2.42 us (4%)
  other arithmetic  0.69 us (1%)
    ppermute x2, waiting for transfers between devices, neighbour_planes(): lax.ppermute(plane, 'space', [(i, (i - 2 * step[i]) % count) for i in ran...  12.3 us
    ppermute x13, starting transfers between devices, swap(): lax.ppermute(value, 'space', [(i, i ^ distance) for i in range(lax.axis_s...  9.33 us
    ppermute x2, starting transfers between devices, neighbour_planes(): lax.ppermute(plane, 'space', [(i, (i + step[i]) % count) for i in range(c...  7.37 us
    pallas_call x2, Pallas kernels, forces(): call(functools.partial(own_kernel, coords, beads, len(tied)), out_shape=(...  5.07 us
    pallas_call x2, Pallas kernels, forces(): call(functools.partial(outer_kernel, coords, beads), out_shape=field, in_...  4.58 us
    ppermute x2, waiting for transfers between devices, neighbour_planes(): lax.ppermute(plane, 'space', [(i, (i + step[i]) % count) for i in range(c...  4.58 us
    ppermute x13, waiting for transfers between devices, swap(): lax.ppermute(value, 'space', [(i, i ^ distance) for i in range(lax.axis_s...  3.36 us
    pallas_call x1, Pallas kernels, on_device(): call(functools.partial(setup_kernel, coords, beads), out_shape=(shape((hi...  1.58 us
  transfers between devices with their start and end apart: 17, of which 7 were waited for; matrix products, arithmetic and copies ran while one was open for 1% of the time, Pallas kernels for 15%

profile of v6, /device:TPU:0, one launch (start us, length us, event | category | flops | bytes accessed | tf_op | source)
XLA Modules:
  0.0 56.5 jit_solution(14810300660429395000)
XLA Ops:
  0.7 0.0 copy-start.3
  0.7 1.0 %shard_map.139 = (bf16[240,128]{1,0:T(8,128)(2,1)S(1)}, f32[240,128]{1,0:T(8,128)S(1)}) custom-call(f32[240,128]{1,0:T(8,128)} %bitcast.46), custom_call_target="tpu_custom_call" | custom-call | flops 10000000000 | bytes 100000000 | tf_op jit(solution)/shard_map/pallas_call | solution.py:423
  1.8 5.5 %collective-permute-start.1 = (bf16[240,128]{1,0:T(8,128)(2,1)S(1)}, bf16[240,128]{1,0:T(8,128)(2,1)S(1)}, u32[]{:S(2)}, u32[]{:S(2)}) collective-permute-start(bf16[240,128]{1,0:T(8,128)(2,1)S(1)} %get-tuple-element.42.own_ref), channel_id=1, source_target_pairs={{0,15},{1,2},{2,1},{3,4},{4,3},{5,6},{6,5},{7,8},{8,7},{9,10},{10,... | collective-permute-start | bytes 184328 | tf_op jit(solution)/shard_map/ppermute | solution.py:375
  7.3 0.0 collective-permute-start.2
  8.6 0.0 copy-done
  8.7 1.6 %shard_map.140 = (bf16[256,432]{1,0:T(8,128)(2,1)S(1)}, bf16[256,432]{1,0:T(8,128)(2,1)S(1)}, bf16[432,256]{1,0:T(8,128)(2,1)S(1)}, bf16[256,256]{1,0:T(8,128)(2...) custom-call(f32[1]{0:T(128)S(6)} %copy.28.step_ref, ...), custom_call_target="tpu_custom_call" | custom-call | tf_op jit(solution)/shard_map/pallas_call | solution.py:434
  10.3 0.0 collective-permute-done.1.outer_ref
  10.3 0.0 collective-permute-done.2.inner_ref
  10.3 2.5 %shard_map.141 = (f32[240,128]{1,0:T(8,128)S(1)}, f32[144,2048]{1,0:T(8,128)S(1)}, bf16[432,2048]{1,0:T(8,128)(2,1)S(1)}) custom-call(bf16[240,128]{1,0:T(8,128)(2,1)S(1)} %collective-permute-done.1.outer_ref, bf16[240,128]{1,0:T(8,128)(2,1)S(1)} %get-tuple-element.42.own_ref, bf16[240,128]{1,0:T(8,128)(2,1)S(1)} %collective-permute-done.2.inner_ref, ...), custom_call_target="tpu_custom_call" | custom-call | tf_op jit(solution)/shard_map/pallas_call | solution.py:450
  12.8 0.6 %collective-permute-start.3 = (f32[240,128]{1,0:T(8,128)S(1)}, f32[240,128]{1,0:T(8,128)S(1)}, u32[]{:S(2)}, u32[]{:S(2)}) collective-permute-start(f32[240,128]{1,0:T(8,128)S(1)} %get-tuple-element.50), channel_id=1, source_target_pairs={{0,1},{1,0},{2,3},{3,2},{4,5},{5,4},{6,7},{7,6},{8,9},{9,8},{10,11... | collective-permute-start | bytes 368648 | tf_op jit(solution)/shard_map/ppermute | solution.py:369
  13.4 0.0 collective-permute-start
  13.4 6.9 %collective-permute-done.outer2_ref = bf16[240,128]{1,0:T(8,128)(2,1)S(1)} collective-permute-done((bf16[240,128]{1,0:T(8,128)(2,1)S(1)}, bf16[240,128]{1,0:T(8,128)(2,1)S(1)}, u32[]{:S(2)}, u32[]{:S(2)}) %collective-permute-start) | collective-permute-done | bytes 61472 | tf_op jit(solution)/shard_map/ppermute | solution.py:377
  20.3 2.3 %shard_map.142.kept_ref = f32[240,128]{1,0:T(8,128)S(1)} custom-call(bf16[240,128]{1,0:T(8,128)(2,1)S(1)} %collective-permute-done.outer2_ref, bf16[432,2048]{1,0:T(8,128)(2,1)S(1)} %get-tuple-element.47.features_ref, f32[144,2048]{1,0:T(8,128)S(1)} %get-tuple-element.48.sums_ref, bf16[256,432]{1,0:T(8,128)(2,1)S(1)} %get-tuple-element.49.forward_ref, ...), custom_call_target="tpu_custom_call" | custom-call | tf_op jit(solution)/shard_map/pallas_call | solution.py:456
  22.6 0.0 collective-permute-done.3.came_ref
  22.6 0.3 shard_map.143
  22.9 1.8 %collective-permute-start.5 = (bf16[240,128]{1,0:T(8,128)(2,1)S(1)}, bf16[240,128]{1,0:T(8,128)(2,1)S(1)}, u32[]{:S(2)}, u32[]{:S(2)}) collective-permute-start(bf16[240,128]{1,0:T(8,128)(2,1)S(1)} %get-tuple-element.64.own_ref), channel_id=1, source_target_pairs={{0,15},{1,2},{2,1},{3,4},{4,3},{5,6},{6,5},{7,8},{8,7},{9,10},{10,... | collective-permute-start | bytes 184328 | tf_op jit(solution)/shard_map/ppermute | solution.py:375
  24.7 0.0 collective-permute-start.6
  24.7 4.6 %collective-permute-done.5.outer_ref = bf16[240,128]{1,0:T(8,128)(2,1)S(1)} collective-permute-done((bf16[240,128]{1,0:T(8,128)(2,1)S(1)}, bf16[240,128]{1,0:T(8,128)(2,1)S(1)}, u32[]{:S(2)}, u32[]{:S(2)}) %collective-permute-start.5) | collective-permute-done | bytes 61472 | tf_op jit(solution)/shard_map/ppermute | solution.py:375
  29.3 0.0 collective-permute-done.6.inner_ref
  29.3 2.5 %shard_map.145 = (f32[240,128]{1,0:T(8,128)S(1)}, f32[144,2048]{1,0:T(8,128)S(1)}, bf16[432,2048]{1,0:T(8,128)(2,1)S(1)}) custom-call(bf16[240,128]{1,0:T(8,128)(2,1)S(1)} %collective-permute-done.5.outer_ref, bf16[240,128]{1,0:T(8,128)(2,1)S(1)} %get-tuple-element.64.own_ref, bf16[240,128]{1,0:T(8,128)(2,1)S(1)} %collective-permute-done.6.inner_ref, ...), custom_call_target="tpu_custom_call" | custom-call | tf_op jit(solution)/shard_map/pallas_call | solution.py:450
  31.9 0.1 collective-permute-start.7
  31.9 0.2 collective-permute-start.4
  32.2 1.5 %shard_map.144 = (f32[240,128]{1,0:T(8,128)}, f32[240,128]{1,0:T(8,128)S(1)}, f32[240,128]{1,0:T(8,128)S(1)}, bf16[240,768]{1,0:T(8,128)(2,1)S(1)}, f32[2,16,256...) custom-call(f32[8,128]{1,0:T(8,128)S(1)} %get-tuple-element.39.half_ref, ...), custom_call_target="tpu_custom_call" | custom-call | tf_op jit(solution)/shard_map/pallas_call | solution.py:467
  33.7 5.4 %collective-permute-done.4.outer2_ref = bf16[240,128]{1,0:T(8,128)(2,1)S(1)} collective-permute-done((bf16[240,128]{1,0:T(8,128)(2,1)S(1)}, bf16[240,128]{1,0:T(8,128)(2,1)S(1)}, u32[]{:S(2)}, u32[]{:S(2)}) %collective-permute-start.4) | collective-permute-done | bytes 61472 | tf_op jit(solution)/shard_map/ppermute | solution.py:377
  39.1 2.3 %shard_map.146.kept_ref = f32[240,128]{1,0:T(8,128)S(1)} custom-call(bf16[240,128]{1,0:T(8,128)(2,1)S(1)} %collective-permute-done.4.outer2_ref, bf16[432,2048]{1,0:T(8,128)(2,1)S(1)} %get-tuple-element.65.features_ref, f32[144,2048]{1,0:T(8,128)S(1)} %get-tuple-element.66.sums_ref, bf16[256,432]{1,0:T(8,128)(2,1)S(1)} %get-tuple-element.49.forward_ref, ...), custom_call_target="tpu_custom_call" | custom-call | tf_op jit(solution)/shard_map/pallas_call | solution.py:456
  41.4 0.0 collective-permute-done.7.came_ref
  41.4 0.3 shard_map.147
  41.7 0.1 collective-permute-start.8
  41.7 0.1 collective-permute-start.9
  41.8 4.3 %collective-permute-start.10 = (bf16[240,128]{1,0:T(8,128)(2,1)S(1)}, bf16[240,128]{1,0:T(8,128)(2,1)S(1)}, u32[]{:S(2)}, u32[]{:S(2)}) collective-permute-start(bf16[240,128]{1,0:T(8,128)(2,1)S(1)} %get-tuple-element.69), channel_id=1, source_target_pairs={{0,12},{1,13},{2,14},{3,15},{4,8},{5,9},{6,10},{7,11},{8,4},{9,5},... | collective-permute-start | bytes 184328 | tf_op jit(solution)/shard_map/ppermute | solution.py:369
  46.1 0.1 collective-permute-start.11
  46.2 0.7 %sub.3 = f32[240,128]{1,0:T(8,128)} subtract(f32[240,128]{1,0:T(8,128)S(1)} %get-tuple-element.61, f32[240,128]{1,0:T(8,128)S(1)} %get-tuple-element.68) | non-fusion elementwise | flops 30720 | bytes 368640 | tf_op jit(solution)/shard_map/sub | solution.py:478
  46.9 0.0 collective-permute-done.8
  46.9 2.0 %collective-permute-start.12 = (bf16[240,128]{1,0:T(8,128)(2,1)S(1)}, bf16[240,128]{1,0:T(8,128)(2,1)S(1)}, u32[]{:S(2)}, u32[]{:S(2)}) collective-permute-start(bf16[240,128]{1,0:T(8,128)(2,1)S(1)} %collective-permute-done.8), channel_id=1, source_target_pairs={{0,2},{1,3},{2,0},{3,1},{4,6},{5,7},{6,4},{7,5},{8,10},{9,11},{10,... | collective-permute-start | bytes 184328 | tf_op jit(solution)/shard_map/ppermute | solution.py:369
  48.9 0.0 collective-permute-done.9
  48.9 0.1 collective-permute-start.13
  49.0 0.0 collective-permute-done.10
  49.0 2.0 %collective-permute-start.14 = (bf16[240,128]{1,0:T(8,128)(2,1)S(1)}, bf16[240,128]{1,0:T(8,128)(2,1)S(1)}, u32[]{:S(2)}, u32[]{:S(2)}) collective-permute-start(bf16[240,128]{1,0:T(8,128)(2,1)S(1)} %collective-permute-done.10), channel_id=1, source_target_pairs={{0,2},{1,3},{2,0},{3,1},{4,6},{5,7},{6,4},{7,5},{8,10},{9,11},{10,... | collective-permute-start | bytes 184328 | tf_op jit(solution)/shard_map/ppermute | solution.py:369
  51.0 0.0 collective-permute-done.11
  51.0 0.1 collective-permute-start.15
  51.1 0.6 %collective-permute-done.12 = bf16[240,128]{1,0:T(8,128)(2,1)S(1)} collective-permute-done((bf16[240,128]{1,0:T(8,128)(2,1)S(1)}, bf16[240,128]{1,0:T(8,128)(2,1)S(1)}, u32[]{:S(2)}, u32[]{:S(2)}) %collective-permute-start.12) | collective-permute-done | bytes 61472 | tf_op jit(solution)/shard_map/ppermute | solution.py:369
  51.7 1.4 %collective-permute-done.13 = bf16[240,128]{1,0:T(8,128)(2,1)S(1)} collective-permute-done((bf16[240,128]{1,0:T(8,128)(2,1)S(1)}, bf16[240,128]{1,0:T(8,128)(2,1)S(1)}, u32[]{:S(2)}, u32[]{:S(2)}) %collective-permute-start.13) | collective-permute-done | bytes 61472 | tf_op jit(solution)/shard_map/ppermute | solution.py:369
  53.1 0.7 %collective-permute-done.14 = bf16[240,128]{1,0:T(8,128)(2,1)S(1)} collective-permute-done((bf16[240,128]{1,0:T(8,128)(2,1)S(1)}, bf16[240,128]{1,0:T(8,128)(2,1)S(1)}, u32[]{:S(2)}, u32[]{:S(2)}) %collective-permute-start.14) | collective-permute-done | bytes 61472 | tf_op jit(solution)/shard_map/ppermute | solution.py:369
  53.8 0.1 collective-permute-start.16
  53.9 0.0 collective-permute-done.15.other_ref
  54.0 0.7 %shard_map.148.near_ref = f32[480,256]{1,0:T(8,128)S(1)} custom-call(bf16[8,240,128]{2,1,0:T(8,128)(2,1)S(1)} %constant_dynamic-update-slice_fusion.own_ref, bf16[5,240,128]{2,1,0:T(8,128)(2,1)S(1)} %collective-permute-done.15.other_ref, f32[2,16,256]{2,1,0:T(8,128)S(1)} %get-tuple-element.70.planes_ref, f32[2,128,256]{2,1,0:T(8,128)S(1)} %get-tuple-element.71.cells_ref, ...), custom_call_target="tpu_custom_call" | custom-call | tf_op jit(solution)/shard_map/pallas_call | solution.py:481
  54.6 0.7 %collective-permute-done.16.velocity_ref = bf16[3,240,128]{2,1,0:T(8,128)(2,1)S(1)} collective-permute-done((bf16[3,240,128]{2,1,0:T(8,128)(2,1)S(1)}, bf16[3,240,128]{2,1,0:T(8,128)(2,1)S(1)}, u32[]{:S(2)}, u32[]{:S(2)}) %collective-permute-start.16) | collective-permute-done | bytes 184352 | tf_op jit(solution)/shard_map/ppermute | solution.py:369
  55.3 1.1 %shard_map.149 = f32[480,256]{1,0:T(8,128)} custom-call(f32[480,256]{1,0:T(8,128)S(1)} %shard_map.148.near_ref, bf16[3,240,128]{2,1,0:T(8,128)(2,1)S(1)} %collective-permute-done.16.velocity_ref, bf16[2,1024,256]{2,1,0:T(8,128)(2,1)S(1)} %get-tuple-element.72.trig_ref), custom_call_target="tpu_custom_call" | custom-call | tf_op jit(solution)/shard_map/pallas_call | solution.py:484
  (23 shorter events, 0.2 us)
Async XLA Ops:
  0.6 8.0 %copy-start = (bf16[256,256]{1,0:T(8,128)(2,1)S(1)}, bf16[256,256]{1,0:T(8,128)(2,1)}, u32[]{:S(2)}) copy-start(bf16[256,256]{1,0:T(8,128)(2,1)} %two_ref.9) | copy-start | bytes 393220
  0.6 8.0 %copy-start.1 = (bf16[256,405]{0,1:T(8,128)(2,1)S(1)}, bf16[256,405]{0,1:T(8,128)(2,1)}, u32[]{:S(2)}) copy-start(bf16[256,405]{0,1:T(8,128)(2,1)} %param.17) | copy-start | bytes 622084
  0.7 8.0 %copy-start.2 = (f32[15,16,1,128]{3,2,1,0:T(1,128)S(1)}, f32[15,16,1,128]{3,2,1,0:T(1,128)}, u32[]{:S(2)}) copy-start(f32[15,16,1,128]{3,2,1,0:T(1,128)} %param.13) | copy-start | bytes 368644
  0.7 8.0 %copy-start.3 = (f32[64,256]{1,0:T(8,128)S(1)}, f32[64,256]{1,0:T(8,128)}, u32[]{:S(2)}) copy-start(f32[64,256]{1,0:T(8,128)} %constant.2.clone.blocks_ref) | copy-start | bytes 196612
  0.7 8.0 %copy-start.4 = (f32[256]{0:T(256)S(1)}, f32[256]{0:T(256)}, u32[]{:S(2)}) copy-start(f32[256]{0:T(256)} %param.18) | copy-start | bytes 3076
  0.7 8.0 %copy-start.5 = (f32[256]{0:T(256)S(1)}, f32[256]{0:T(256)}, u32[]{:S(2)}) copy-start(f32[256]{0:T(256)} %param.20) | copy-start | bytes 3076
  0.7 8.0 %copy-start.6 = (f32[256]{0:T(256)S(1)}, f32[256]{0:T(256)}, u32[]{:S(2)}) copy-start(f32[256]{0:T(256)} %param.21) | copy-start | bytes 3076
  0.7 8.0 %copy-start.7 = (f32[15]{0:T(128)S(1)}, f32[15]{0:T(128)}, u32[]{:S(2)}) copy-start(f32[15]{0:T(128)} %param.14) | copy-start | bytes 184
  1.8 8.5 %collective-permute-start.1 = (bf16[240,128]{1,0:T(8,128)(2,1)S(1)}, bf16[240,128]{1,0:T(8,128)(2,1)S(1)}, u32[]{:S(2)}, u32[]{:S(2)}) collective-permute-start(bf16[240,128]{1,0:T(8,128)(2,1)S(1)} %get-tuple-element.42.own_ref), channel_id=1, source_target_pairs={{0,15},{1,2},{2,1},{3,4},{4,3},{5,6},{6,5},{7,8},{8,7},{9,10},{10,... | collective-permute-start | bytes 184328 | tf_op jit(solution)/shard_map/ppermute | solution.py:375
  7.3 3.0 %collective-permute-start.2 = (bf16[240,128]{1,0:T(8,128)(2,1)S(1)}, bf16[240,128]{1,0:T(8,128)(2,1)S(1)}, u32[]{:S(2)}, u32[]{:S(2)}) collective-permute-start(bf16[240,128]{1,0:T(8,128)(2,1)S(1)} %get-tuple-element.42.own_ref), channel_id=1, source_target_pairs={{0,1},{1,0},{2,3},{3,2},{4,5},{5,4},{6,7},{7,6},{8,9},{9,8},{10,11... | collective-permute-start | bytes 184328 | tf_op jit(solution)/shard_map/ppermute | solution.py:369
  12.8 9.8 %collective-permute-start.3 = (f32[240,128]{1,0:T(8,128)S(1)}, f32[240,128]{1,0:T(8,128)S(1)}, u32[]{:S(2)}, u32[]{:S(2)}) collective-permute-start(f32[240,128]{1,0:T(8,128)S(1)} %get-tuple-element.50), channel_id=1, source_target_pairs={{0,1},{1,0},{2,3},{3,2},{4,5},{5,4},{6,7},{7,6},{8,9},{9,8},{10,11... | collective-permute-start | bytes 368648 | tf_op jit(solution)/shard_map/ppermute | solution.py:369
  13.4 6.9 %collective-permute-start = (bf16[240,128]{1,0:T(8,128)(2,1)S(1)}, bf16[240,128]{1,0:T(8,128)(2,1)S(1)}, u32[]{:S(2)}, u32[]{:S(2)}) collective-permute-start(bf16[240,128]{1,0:T(8,128)(2,1)S(1)} %get-tuple-element.42.own_ref), channel_id=1, source_target_pairs={{0,2},{1,15},{2,4},{3,1},{4,6},{5,3},{6,8},{7,5},{8,10},{9,7},{10,... | collective-permute-start | bytes 184328 | tf_op jit(solution)/shard_map/ppermute | solution.py:377
  22.9 6.4 %collective-permute-start.5 = (bf16[240,128]{1,0:T(8,128)(2,1)S(1)}, bf16[240,128]{1,0:T(8,128)(2,1)S(1)}, u32[]{:S(2)}, u32[]{:S(2)}) collective-permute-start(bf16[240,128]{1,0:T(8,128)(2,1)S(1)} %get-tuple-element.64.own_ref), channel_id=1, source_target_pairs={{0,15},{1,2},{2,1},{3,4},{4,3},{5,6},{6,5},{7,8},{8,7},{9,10},{10,... | collective-permute-start | bytes 184328 | tf_op jit(solution)/shard_map/ppermute | solution.py:375
  24.7 4.6 %collective-permute-start.6 = (bf16[240,128]{1,0:T(8,128)(2,1)S(1)}, bf16[240,128]{1,0:T(8,128)(2,1)S(1)}, u32[]{:S(2)}, u32[]{:S(2)}) collective-permute-start(bf16[240,128]{1,0:T(8,128)(2,1)S(1)} %get-tuple-element.64.own_ref), channel_id=1, source_target_pairs={{0,1},{1,0},{2,3},{3,2},{4,5},{5,4},{6,7},{7,6},{8,9},{9,8},{10,11... | collective-permute-start | bytes 184328 | tf_op jit(solution)/shard_map/ppermute | solution.py:369
  31.9 9.5 %collective-permute-start.7 = (f32[240,128]{1,0:T(8,128)S(1)}, f32[240,128]{1,0:T(8,128)S(1)}, u32[]{:S(2)}, u32[]{:S(2)}) collective-permute-start(f32[240,128]{1,0:T(8,128)S(1)} %get-tuple-element.67), channel_id=1, source_target_pairs={{0,1},{1,0},{2,3},{3,2},{4,5},{5,4},{6,7},{7,6},{8,9},{9,8},{10,11... | collective-permute-start | bytes 368648 | tf_op jit(solution)/shard_map/ppermute | solution.py:369
  31.9 7.2 %collective-permute-start.4 = (bf16[240,128]{1,0:T(8,128)(2,1)S(1)}, bf16[240,128]{1,0:T(8,128)(2,1)S(1)}, u32[]{:S(2)}, u32[]{:S(2)}) collective-permute-start(bf16[240,128]{1,0:T(8,128)(2,1)S(1)} %get-tuple-element.64.own_ref), channel_id=1, source_target_pairs={{0,2},{1,15},{2,4},{3,1},{4,6},{5,3},{6,8},{7,5},{8,10},{9,7},{10,... | collective-permute-start | bytes 184328 | tf_op jit(solution)/shard_map/ppermute | solution.py:377
  41.7 5.2 %collective-permute-start.8 = (bf16[240,128]{1,0:T(8,128)(2,1)S(1)}, bf16[240,128]{1,0:T(8,128)(2,1)S(1)}, u32[]{:S(2)}, u32[]{:S(2)}) collective-permute-start(bf16[240,128]{1,0:T(8,128)(2,1)S(1)} %get-tuple-element.69), channel_id=1, source_target_pairs={{0,4},{1,5},{2,6},{3,7},{4,0},{5,1},{6,2},{7,3},{8,12},{9,13},{10,... | collective-permute-start | bytes 184328 | tf_op jit(solution)/shard_map/ppermute | solution.py:369
  41.7 7.1 %collective-permute-start.9 = (bf16[240,128]{1,0:T(8,128)(2,1)S(1)}, bf16[240,128]{1,0:T(8,128)(2,1)S(1)}, u32[]{:S(2)}, u32[]{:S(2)}) collective-permute-start(bf16[240,128]{1,0:T(8,128)(2,1)S(1)} %get-tuple-element.69), channel_id=1, source_target_pairs={{0,8},{1,9},{2,10},{3,11},{4,12},{5,13},{6,14},{7,15},{8,0},{9,1},... | collective-permute-start | bytes 184328 | tf_op jit(solution)/shard_map/ppermute | solution.py:369
  41.8 7.1 %collective-permute-start.10 = (bf16[240,128]{1,0:T(8,128)(2,1)S(1)}, bf16[240,128]{1,0:T(8,128)(2,1)S(1)}, u32[]{:S(2)}, u32[]{:S(2)}) collective-permute-start(bf16[240,128]{1,0:T(8,128)(2,1)S(1)} %get-tuple-element.69), channel_id=1, source_target_pairs={{0,12},{1,13},{2,14},{3,15},{4,8},{5,9},{6,10},{7,11},{8,4},{9,5},... | collective-permute-start | bytes 184328 | tf_op jit(solution)/shard_map/ppermute | solution.py:369
  46.1 4.9 %collective-permute-start.11 = (bf16[240,128]{1,0:T(8,128)(2,1)S(1)}, bf16[240,128]{1,0:T(8,128)(2,1)S(1)}, u32[]{:S(2)}, u32[]{:S(2)}) collective-permute-start(bf16[240,128]{1,0:T(8,128)(2,1)S(1)} %get-tuple-element.69), channel_id=1, source_target_pairs={{0,2},{1,3},{2,0},{3,1},{4,6},{5,7},{6,4},{7,5},{8,10},{9,11},{10,... | collective-permute-start | bytes 184328 | tf_op jit(solution)/shard_map/ppermute | solution.py:369
  46.9 4.9 %collective-permute-start.12 = (bf16[240,128]{1,0:T(8,128)(2,1)S(1)}, bf16[240,128]{1,0:T(8,128)(2,1)S(1)}, u32[]{:S(2)}, u32[]{:S(2)}) collective-permute-start(bf16[240,128]{1,0:T(8,128)(2,1)S(1)} %collective-permute-done.8), channel_id=1, source_target_pairs={{0,2},{1,3},{2,0},{3,1},{4,6},{5,7},{6,4},{7,5},{8,10},{9,11},{10,... | collective-permute-start | bytes 184328 | tf_op jit(solution)/shard_map/ppermute | solution.py:369
  48.9 4.2 %collective-permute-start.13 = (bf16[240,128]{1,0:T(8,128)(2,1)S(1)}, bf16[240,128]{1,0:T(8,128)(2,1)S(1)}, u32[]{:S(2)}, u32[]{:S(2)}) collective-permute-start(bf16[240,128]{1,0:T(8,128)(2,1)S(1)} %collective-permute-done.9), channel_id=1, source_target_pairs={{0,2},{1,3},{2,0},{3,1},{4,6},{5,7},{6,4},{7,5},{8,10},{9,11},{10,... | collective-permute-start | bytes 184328 | tf_op jit(solution)/shard_map/ppermute | solution.py:369
  49.0 4.8 %collective-permute-start.14 = (bf16[240,128]{1,0:T(8,128)(2,1)S(1)}, bf16[240,128]{1,0:T(8,128)(2,1)S(1)}, u32[]{:S(2)}, u32[]{:S(2)}) collective-permute-start(bf16[240,128]{1,0:T(8,128)(2,1)S(1)} %collective-permute-done.10), channel_id=1, source_target_pairs={{0,2},{1,3},{2,0},{3,1},{4,6},{5,7},{6,4},{7,5},{8,10},{9,11},{10,... | collective-permute-start | bytes 184328 | tf_op jit(solution)/shard_map/ppermute | solution.py:369
  51.0 2.9 %collective-permute-start.15 = (bf16[5,240,128]{2,1,0:T(8,128)(2,1)S(1)}, bf16[5,240,128]{2,1,0:T(8,128)(2,1)S(1)}, u32[]{:S(2)}, u32[]{:S(2)}) collective-permute-start(bf16[5,240,128]{2,1,0:T(8,128)(2,1)S(1)} %get-tuple-element.76), channel_id=1, source_target_pairs={{0,1},{1,0},{2,3},{3,2},{4,5},{5,4},{6,7},{7,6},{8,9},{9,8},{10,11... | collective-permute-start | bytes 921608 | tf_op jit(solution)/shard_map/ppermute | solution.py:369
  53.8 1.5 %collective-permute-start.16 = (bf16[3,240,128]{2,1,0:T(8,128)(2,1)S(1)}, bf16[3,240,128]{2,1,0:T(8,128)(2,1)S(1)}, u32[]{:S(2)}, u32[]{:S(2)}) collective-permute-start(bf16[3,240,128]{2,1,0:T(8,128)(2,1)S(1)} %pad_maximum_fusion), channel_id=1, source_target_pairs={{0,1},{1,0},{2,3},{3,2},{4,5},{5,4},{6,7},{7,6},{8,9},{9,8},{10,11... | collective-permute-start | bytes 552968 | tf_op jit(solution)/shard_map/ppermute | solution.py:369

commit v7 on v6

--- a/solution.py
+++ b/solution.py
@@ -83,14 +83,12 @@
 
 
 def setup_kernel(
-    coords, beads, step_ref, cycle_ref, vectors_hbm, q_ref, one_ref, bias_one_ref, bias_two_ref, readout_ref,
+    coords, beads, step_ref, cycle_ref, q_ref, one_ref, bias_one_ref, bias_two_ref, readout_ref,
     p_ref, masses_ref, blocks_ref, two_ref,
     forward_ref, outer_forward_ref, backward_ref, two_t_ref, wide_ref,
     q_base_ref, q_map_ref, p_base_ref, pushed_ref, cosine_ref, finish_ref, half_ref,
-    modes_ref, modes_t_ref, vectors_ref, rows, semaphore
+    modes_ref, modes_t_ref, rows
 ):
-    copy = pltpu.make_async_copy(vectors_hbm, vectors_ref, semaphore)
-    copy.start()
     is_odd = lax.axis_index("space") % 2 == 1
     hidden = one_ref.shape[1]
     rows[: one_ref.shape[0], :] = one_ref[...].astype(f32)
@@ -156,7 +154,6 @@
     q_map_ref[...] = left_terms(close_dot(modes_ref[...], (half * drift[:, :1]) * modes_t))
     finish_ref[...] = jnp.concatenate([half / mass, 1.0 / mass], axis=1)
     half_ref[...] = jnp.full(half_ref.shape, half, f32)
-    copy.wait()
 
 
 def put_features(coords, beads, chosen, stage, features, top):
@@ -430,18 +427,18 @@
 
     (
         forward, outer_forward, backward, two_t, wide, q_base, q_map, p_base, pushed, cosine, finish, half,
-        modes, modes_t, wavevectors
+        modes, modes_t
     ) = call(
         functools.partial(setup_kernel, coords, beads),
         out_shape=(
             shape((hidden, width), bf16), shape((hidden, width), bf16), shape((width, hidden), bf16),
             shape((hidden, hidden), bf16), shape((2, hidden, CELLS), f32),
             field, square, field, field, field, shape((total, 2 * CELLS), f32), shape((8, CELLS), f32),
-            square, square, shape(wavevectors.shape, wavevectors.dtype),
+            square, square,
         ),
-        in_specs=[SMEM, SMEM, HBM] + [VMEM] * len(brought), out_specs=(VMEM,) * 15,
-        scratch_shapes=[pltpu.VMEM((width, hidden), f32), pltpu.SemaphoreType.DMA],
-    )(step_size, cycle_frequency, in_hbm(wavevectors), *brought)
+        in_specs=[SMEM, SMEM] + [VMEM] * len(brought), out_specs=(VMEM,) * 14,
+        scratch_shapes=[pltpu.VMEM((width, hidden), f32)],
+    )(step_size, cycle_frequency, *brought)
     layers = (backward, two, two_t, wide)
     stage = pltpu.VMEM((total, CELLS), f32)
 

time: 56.7 us -> 56 us (0.988)
  starting transfers between devices: 16.9 us -> 17.7 us
  Pallas kernels: 16 us -> 15.3 us
  waiting for transfers between devices: 20.2 us -> 19.5 us
    pallas_call x1, Pallas kernels: 1.58 us -> 0.86 us  [on_device(): call(functools.partial(setup_kernel, coords, beads), out_shape=(shape((hi...]
    ppermute x2, waiting for transfers between devices: 4.58 us -> 3.86 us  [neighbour_planes(): lax.ppermute(plane, 'space', [(i, (i + step[i]) % count) for i in range(c...]
    ppermute x2, starting transfers between devices: 7.37 us -> 8.09 us  [neighbour_planes(): lax.ppermute(plane, 'space', [(i, (i + step[i]) % count) for i in range(c...]
  transfers between devices with their start and end apart: 17 -> 17, of which waited for: 7 -> 7; matrix products, arithmetic and copies ran while one was open for 1% -> 1% of each run, Pallas kernels for 15% -> 14%
where the time goes in v7:
time: 56 us; the launch traced here: 55.8 us
  waiting for transfers between devices  19.5 us (35%)
  starting transfers between devices  17.7 us (32%)
  Pallas kernels  15.3 us (27%)
  between operations  2.45 us (4%)
  other arithmetic  0.69 us (1%)
    ppermute x2, waiting for transfers between devices, neighbour_planes(): lax.ppermute(plane, 'space', [(i, (i - 2 * step[i]) % count) for i in ran...  12.3 us
    ppermute x13, starting transfers between devices, swap(): lax.ppermute(value, 'space', [(i, i ^ distance) for i in range(lax.axis_s...  9.33 us
    ppermute x2, starting transfers between devices, neighbour_planes(): lax.ppermute(plane, 'space', [(i, (i + step[i]) % count) for i in range(c...  8.09 us
    pallas_call x2, Pallas kernels, forces(): call(functools.partial(own_kernel, coords, beads, len(tied)), out_shape=(...  5.07 us
    pallas_call x2, Pallas kernels, forces(): call(functools.partial(outer_kernel, coords, beads), out_shape=field, in_...  4.59 us
    ppermute x2, waiting for transfers between devices, neighbour_planes(): lax.ppermute(plane, 'space', [(i, (i + step[i]) % count) for i in range(c...  3.86 us
    ppermute x13, waiting for transfers between devices, swap(): lax.ppermute(value, 'space', [(i, i ^ distance) for i in range(lax.axis_s...  3.36 us
    pallas_call x1, Pallas kernels, on_device(): call(functools.partial(push_kernel, share, order), out_shape=(field, fiel...  1.51 us
  transfers between devices with their start and end apart: 17, of which 7 were waited for; matrix products, arithmetic and copies ran while one was open for 1% of the time, Pallas kernels for 14%

profile of v7, /device:TPU:0, one launch (start us, length us, event | category | flops | bytes accessed | tf_op | source)
XLA Modules:
  0.0 55.8 jit_solution(15037126152336650042)
XLA Ops:
  0.7 0.0 copy-start.4
  0.7 1.0 %shard_map.139 = (bf16[240,128]{1,0:T(8,128)(2,1)S(1)}, f32[240,128]{1,0:T(8,128)S(1)}) custom-call(f32[240,128]{1,0:T(8,128)} %bitcast.46), custom_call_target="tpu_custom_call" | custom-call | flops 10000000000 | bytes 100000000 | tf_op jit(solution)/shard_map/pallas_call | solution.py:420
  1.8 5.5 %collective-permute-start.1 = (bf16[240,128]{1,0:T(8,128)(2,1)S(1)}, bf16[240,128]{1,0:T(8,128)(2,1)S(1)}, u32[]{:S(2)}, u32[]{:S(2)}) collective-permute-start(bf16[240,128]{1,0:T(8,128)(2,1)S(1)} %get-tuple-element.41.own_ref), channel_id=1, source_target_pairs={{0,15},{1,2},{2,1},{3,4},{4,3},{5,6},{6,5},{7,8},{8,7},{9,10},{10,... | collective-permute-start | bytes 184328 | tf_op jit(solution)/shard_map/ppermute | solution.py:372
  7.3 0.0 collective-permute-start.2
  8.7 0.9 %shard_map.140 = (bf16[256,432]{1,0:T(8,128)(2,1)S(1)}, bf16[256,432]{1,0:T(8,128)(2,1)S(1)}, bf16[432,256]{1,0:T(8,128)(2,1)S(1)}, bf16[256,256]{1,0:T(8,128)(2...) custom-call(f32[1]{0:T(128)S(6)} %copy.28.step_ref, ...), custom_call_target="tpu_custom_call" | custom-call | tf_op jit(solution)/shard_map/pallas_call | solution.py:431
  9.5 0.0 collective-permute-done.1.outer_ref
  9.6 0.0 collective-permute-done.2.inner_ref
  9.6 2.5 %shard_map.141 = (f32[240,128]{1,0:T(8,128)S(1)}, f32[144,2048]{1,0:T(8,128)S(1)}, bf16[432,2048]{1,0:T(8,128)(2,1)S(1)}) custom-call(bf16[240,128]{1,0:T(8,128)(2,1)S(1)} %collective-permute-done.1.outer_ref, bf16[240,128]{1,0:T(8,128)(2,1)S(1)} %get-tuple-element.41.own_ref, bf16[240,128]{1,0:T(8,128)(2,1)S(1)} %collective-permute-done.2.inner_ref, ...), custom_call_target="tpu_custom_call" | custom-call | tf_op jit(solution)/shard_map/pallas_call | solution.py:447
  12.1 0.6 %collective-permute-start.3 = (f32[240,128]{1,0:T(8,128)S(1)}, f32[240,128]{1,0:T(8,128)S(1)}, u32[]{:S(2)}, u32[]{:S(2)}) collective-permute-start(f32[240,128]{1,0:T(8,128)S(1)} %get-tuple-element.49), channel_id=1, source_target_pairs={{0,1},{1,0},{2,3},{3,2},{4,5},{5,4},{6,7},{7,6},{8,9},{9,8},{10,11... | collective-permute-start | bytes 368648 | tf_op jit(solution)/shard_map/ppermute | solution.py:366
  12.7 0.0 collective-permute-start
  12.7 6.9 %collective-permute-done.outer2_ref = bf16[240,128]{1,0:T(8,128)(2,1)S(1)} collective-permute-done((bf16[240,128]{1,0:T(8,128)(2,1)S(1)}, bf16[240,128]{1,0:T(8,128)(2,1)S(1)}, u32[]{:S(2)}, u32[]{:S(2)}) %collective-permute-start) | collective-permute-done | bytes 61472 | tf_op jit(solution)/shard_map/ppermute | solution.py:374
  19.6 2.3 %shard_map.142.kept_ref = f32[240,128]{1,0:T(8,128)S(1)} custom-call(bf16[240,128]{1,0:T(8,128)(2,1)S(1)} %collective-permute-done.outer2_ref, bf16[432,2048]{1,0:T(8,128)(2,1)S(1)} %get-tuple-element.46.features_ref, f32[144,2048]{1,0:T(8,128)S(1)} %get-tuple-element.47.sums_ref, bf16[256,432]{1,0:T(8,128)(2,1)S(1)} %get-tuple-element.48.forward_ref, ...), custom_call_target="tpu_custom_call" | custom-call | tf_op jit(solution)/shard_map/pallas_call | solution.py:453
  21.9 0.0 copy-start.3
  21.9 0.0 collective-permute-done.3.came_ref
  21.9 0.3 shard_map.143
  22.2 2.6 %collective-permute-start.5 = (bf16[240,128]{1,0:T(8,128)(2,1)S(1)}, bf16[240,128]{1,0:T(8,128)(2,1)S(1)}, u32[]{:S(2)}, u32[]{:S(2)}) collective-permute-start(bf16[240,128]{1,0:T(8,128)(2,1)S(1)} %get-tuple-element.62.own_ref), channel_id=1, source_target_pairs={{0,15},{1,2},{2,1},{3,4},{4,3},{5,6},{6,5},{7,8},{8,7},{9,10},{10,... | collective-permute-start | bytes 184328 | tf_op jit(solution)/shard_map/ppermute | solution.py:372
  24.7 0.0 collective-permute-start.6
  24.7 3.9 %collective-permute-done.5.outer_ref = bf16[240,128]{1,0:T(8,128)(2,1)S(1)} collective-permute-done((bf16[240,128]{1,0:T(8,128)(2,1)S(1)}, bf16[240,128]{1,0:T(8,128)(2,1)S(1)}, u32[]{:S(2)}, u32[]{:S(2)}) %collective-permute-start.5) | collective-permute-done | bytes 61472 | tf_op jit(solution)/shard_map/ppermute | solution.py:372
  28.6 0.0 collective-permute-done.6.inner_ref
  28.6 2.5 %shard_map.145 = (f32[240,128]{1,0:T(8,128)S(1)}, f32[144,2048]{1,0:T(8,128)S(1)}, bf16[432,2048]{1,0:T(8,128)(2,1)S(1)}) custom-call(bf16[240,128]{1,0:T(8,128)(2,1)S(1)} %collective-permute-done.5.outer_ref, bf16[240,128]{1,0:T(8,128)(2,1)S(1)} %get-tuple-element.62.own_ref, bf16[240,128]{1,0:T(8,128)(2,1)S(1)} %collective-permute-done.6.inner_ref, ...), custom_call_target="tpu_custom_call" | custom-call | tf_op jit(solution)/shard_map/pallas_call | solution.py:447
  31.1 0.1 collective-permute-start.7
  31.2 0.2 collective-permute-start.4
  31.5 1.5 %shard_map.144 = (f32[240,128]{1,0:T(8,128)}, f32[240,128]{1,0:T(8,128)S(1)}, f32[240,128]{1,0:T(8,128)S(1)}, bf16[240,768]{1,0:T(8,128)(2,1)S(1)}, f32[2,16,256...) custom-call(f32[8,128]{1,0:T(8,128)S(1)} %get-tuple-element.38.half_ref, ...), custom_call_target="tpu_custom_call" | custom-call | tf_op jit(solution)/shard_map/pallas_call | solution.py:464
  33.0 5.4 %collective-permute-done.4.outer2_ref = bf16[240,128]{1,0:T(8,128)(2,1)S(1)} collective-permute-done((bf16[240,128]{1,0:T(8,128)(2,1)S(1)}, bf16[240,128]{1,0:T(8,128)(2,1)S(1)}, u32[]{:S(2)}, u32[]{:S(2)}) %collective-permute-start.4) | collective-permute-done | bytes 61472 | tf_op jit(solution)/shard_map/ppermute | solution.py:374
  38.4 2.3 %shard_map.146.kept_ref = f32[240,128]{1,0:T(8,128)S(1)} custom-call(bf16[240,128]{1,0:T(8,128)(2,1)S(1)} %collective-permute-done.4.outer2_ref, bf16[432,2048]{1,0:T(8,128)(2,1)S(1)} %get-tuple-element.63.features_ref, f32[144,2048]{1,0:T(8,128)S(1)} %get-tuple-element.64.sums_ref, bf16[256,432]{1,0:T(8,128)(2,1)S(1)} %get-tuple-element.48.forward_ref, ...), custom_call_target="tpu_custom_call" | custom-call | tf_op jit(solution)/shard_map/pallas_call | solution.py:453
  40.7 0.0 collective-permute-done.7.came_ref
  40.7 0.3 shard_map.147
  41.0 0.1 collective-permute-start.8
  41.0 0.1 collective-permute-start.9
  41.1 4.3 %collective-permute-start.10 = (bf16[240,128]{1,0:T(8,128)(2,1)S(1)}, bf16[240,128]{1,0:T(8,128)(2,1)S(1)}, u32[]{:S(2)}, u32[]{:S(2)}) collective-permute-start(bf16[240,128]{1,0:T(8,128)(2,1)S(1)} %get-tuple-element.67), channel_id=1, source_target_pairs={{0,12},{1,13},{2,14},{3,15},{4,8},{5,9},{6,10},{7,11},{8,4},{9,5},... | collective-permute-start | bytes 184328 | tf_op jit(solution)/shard_map/ppermute | solution.py:366
  45.4 0.1 collective-permute-start.11
  45.5 0.7 %sub.3 = f32[240,128]{1,0:T(8,128)} subtract(f32[240,128]{1,0:T(8,128)S(1)} %get-tuple-element.59, f32[240,128]{1,0:T(8,128)S(1)} %get-tuple-element.66) | non-fusion elementwise | flops 30720 | bytes 368640 | tf_op jit(solution)/shard_map/sub | solution.py:475
  46.2 0.0 collective-permute-done.8
  46.2 2.0 %collective-permute-start.12 = (bf16[240,128]{1,0:T(8,128)(2,1)S(1)}, bf16[240,128]{1,0:T(8,128)(2,1)S(1)}, u32[]{:S(2)}, u32[]{:S(2)}) collective-permute-start(bf16[240,128]{1,0:T(8,128)(2,1)S(1)} %collective-permute-done.8), channel_id=1, source_target_pairs={{0,2},{1,3},{2,0},{3,1},{4,6},{5,7},{6,4},{7,5},{8,10},{9,11},{10,... | collective-permute-start | bytes 184328 | tf_op jit(solution)/shard_map/ppermute | solution.py:366
  48.2 0.0 collective-permute-done.9
  48.2 0.1 collective-permute-start.13
  48.3 0.0 collective-permute-done.10
  48.3 2.0 %collective-permute-start.14 = (bf16[240,128]{1,0:T(8,128)(2,1)S(1)}, bf16[240,128]{1,0:T(8,128)(2,1)S(1)}, u32[]{:S(2)}, u32[]{:S(2)}) collective-permute-start(bf16[240,128]{1,0:T(8,128)(2,1)S(1)} %collective-permute-done.10), channel_id=1, source_target_pairs={{0,2},{1,3},{2,0},{3,1},{4,6},{5,7},{6,4},{7,5},{8,10},{9,11},{10,... | collective-permute-start | bytes 184328 | tf_op jit(solution)/shard_map/ppermute | solution.py:366
  50.3 0.0 collective-permute-done.11
  50.3 0.1 collective-permute-start.15
  50.4 0.6 %collective-permute-done.12 = bf16[240,128]{1,0:T(8,128)(2,1)S(1)} collective-permute-done((bf16[240,128]{1,0:T(8,128)(2,1)S(1)}, bf16[240,128]{1,0:T(8,128)(2,1)S(1)}, u32[]{:S(2)}, u32[]{:S(2)}) %collective-permute-start.12) | collective-permute-done | bytes 61472 | tf_op jit(solution)/shard_map/ppermute | solution.py:366
  51.0 1.4 %collective-permute-done.13 = bf16[240,128]{1,0:T(8,128)(2,1)S(1)} collective-permute-done((bf16[240,128]{1,0:T(8,128)(2,1)S(1)}, bf16[240,128]{1,0:T(8,128)(2,1)S(1)}, u32[]{:S(2)}, u32[]{:S(2)}) %collective-permute-start.13) | collective-permute-done | bytes 61472 | tf_op jit(solution)/shard_map/ppermute | solution.py:366
  52.4 0.7 %collective-permute-done.14 = bf16[240,128]{1,0:T(8,128)(2,1)S(1)} collective-permute-done((bf16[240,128]{1,0:T(8,128)(2,1)S(1)}, bf16[240,128]{1,0:T(8,128)(2,1)S(1)}, u32[]{:S(2)}, u32[]{:S(2)}) %collective-permute-start.14) | collective-permute-done | bytes 61472 | tf_op jit(solution)/shard_map/ppermute | solution.py:366
  53.1 0.1 collective-permute-start.16
  53.2 0.0 collective-permute-done.15.other_ref
  53.2 0.7 %shard_map.148.near_ref = f32[480,256]{1,0:T(8,128)S(1)} custom-call(bf16[8,240,128]{2,1,0:T(8,128)(2,1)S(1)} %constant_dynamic-update-slice_fusion.own_ref, bf16[5,240,128]{2,1,0:T(8,128)(2,1)S(1)} %collective-permute-done.15.other_ref, f32[2,16,256]{2,1,0:T(8,128)S(1)} %get-tuple-element.68.planes_ref, f32[2,128,256]{2,1,0:T(8,128)S(1)} %get-tuple-element.69.cells_ref, ...), custom_call_target="tpu_custom_call" | custom-call | tf_op jit(solution)/shard_map/pallas_call | solution.py:478
  53.9 0.7 %collective-permute-done.16.velocity_ref = bf16[3,240,128]{2,1,0:T(8,128)(2,1)S(1)} collective-permute-done((bf16[3,240,128]{2,1,0:T(8,128)(2,1)S(1)}, bf16[3,240,128]{2,1,0:T(8,128)(2,1)S(1)}, u32[]{:S(2)}, u32[]{:S(2)}) %collective-permute-start.16) | collective-permute-done | bytes 184352 | tf_op jit(solution)/shard_map/ppermute | solution.py:366
  54.6 1.1 %shard_map.149 = f32[480,256]{1,0:T(8,128)} custom-call(f32[480,256]{1,0:T(8,128)S(1)} %shard_map.148.near_ref, bf16[3,240,128]{2,1,0:T(8,128)(2,1)S(1)} %collective-permute-done.16.velocity_ref, bf16[2,1024,256]{2,1,0:T(8,128)(2,1)S(1)} %get-tuple-element.70.trig_ref), custom_call_target="tpu_custom_call" | custom-call | tf_op jit(solution)/shard_map/pallas_call | solution.py:481
  (25 shorter events, 0.2 us)
Async XLA Ops:
  0.6 8.0 %copy-start = (bf16[256,256]{1,0:T(8,128)(2,1)S(1)}, bf16[256,256]{1,0:T(8,128)(2,1)}, u32[]{:S(2)}) copy-start(bf16[256,256]{1,0:T(8,128)(2,1)} %two_ref.9) | copy-start | bytes 393220
  0.6 8.0 %copy-start.1 = (bf16[256,405]{0,1:T(8,128)(2,1)S(1)}, bf16[256,405]{0,1:T(8,128)(2,1)}, u32[]{:S(2)}) copy-start(bf16[256,405]{0,1:T(8,128)(2,1)} %param.17) | copy-start | bytes 622084
  0.7 8.0 %copy-start.2 = (f32[15,16,1,128]{3,2,1,0:T(1,128)S(1)}, f32[15,16,1,128]{3,2,1,0:T(1,128)}, u32[]{:S(2)}) copy-start(f32[15,16,1,128]{3,2,1,0:T(1,128)} %param.13) | copy-start | bytes 368644
  0.7 8.0 %copy-start.4 = (f32[64,256]{1,0:T(8,128)S(1)}, f32[64,256]{1,0:T(8,128)}, u32[]{:S(2)}) copy-start(f32[64,256]{1,0:T(8,128)} %constant.2.clone.blocks_ref) | copy-start | bytes 196612
  0.7 8.0 %copy-start.5 = (f32[256]{0:T(256)S(1)}, f32[256]{0:T(256)}, u32[]{:S(2)}) copy-start(f32[256]{0:T(256)} %param.18) | copy-start | bytes 3076
  0.7 8.0 %copy-start.6 = (f32[256]{0:T(256)S(1)}, f32[256]{0:T(256)}, u32[]{:S(2)}) copy-start(f32[256]{0:T(256)} %param.20) | copy-start | bytes 3076
  0.7 8.0 %copy-start.7 = (f32[256]{0:T(256)S(1)}, f32[256]{0:T(256)}, u32[]{:S(2)}) copy-start(f32[256]{0:T(256)} %param.21) | copy-start | bytes 3076
  0.7 8.0 %copy-start.8 = (f32[15]{0:T(128)S(1)}, f32[15]{0:T(128)}, u32[]{:S(2)}) copy-start(f32[15]{0:T(128)} %param.14) | copy-start | bytes 184
  1.8 7.8 %collective-permute-start.1 = (bf16[240,128]{1,0:T(8,128)(2,1)S(1)}, bf16[240,128]{1,0:T(8,128)(2,1)S(1)}, u32[]{:S(2)}, u32[]{:S(2)}) collective-permute-start(bf16[240,128]{1,0:T(8,128)(2,1)S(1)} %get-tuple-element.41.own_ref), channel_id=1, source_target_pairs={{0,15},{1,2},{2,1},{3,4},{4,3},{5,6},{6,5},{7,8},{8,7},{9,10},{10,... | collective-permute-start | bytes 184328 | tf_op jit(solution)/shard_map/ppermute | solution.py:372
  7.3 2.3 %collective-permute-start.2 = (bf16[240,128]{1,0:T(8,128)(2,1)S(1)}, bf16[240,128]{1,0:T(8,128)(2,1)S(1)}, u32[]{:S(2)}, u32[]{:S(2)}) collective-permute-start(bf16[240,128]{1,0:T(8,128)(2,1)S(1)} %get-tuple-element.41.own_ref), channel_id=1, source_target_pairs={{0,1},{1,0},{2,3},{3,2},{4,5},{5,4},{6,7},{7,6},{8,9},{9,8},{10,11... | collective-permute-start | bytes 184328 | tf_op jit(solution)/shard_map/ppermute | solution.py:366
  12.1 9.8 %collective-permute-start.3 = (f32[240,128]{1,0:T(8,128)S(1)}, f32[240,128]{1,0:T(8,128)S(1)}, u32[]{:S(2)}, u32[]{:S(2)}) collective-permute-start(f32[240,128]{1,0:T(8,128)S(1)} %get-tuple-element.49), channel_id=1, source_target_pairs={{0,1},{1,0},{2,3},{3,2},{4,5},{5,4},{6,7},{7,6},{8,9},{9,8},{10,11... | collective-permute-start | bytes 368648 | tf_op jit(solution)/shard_map/ppermute | solution.py:366
  12.7 6.9 %collective-permute-start = (bf16[240,128]{1,0:T(8,128)(2,1)S(1)}, bf16[240,128]{1,0:T(8,128)(2,1)S(1)}, u32[]{:S(2)}, u32[]{:S(2)}) collective-permute-start(bf16[240,128]{1,0:T(8,128)(2,1)S(1)} %get-tuple-element.41.own_ref), channel_id=1, source_target_pairs={{0,2},{1,15},{2,4},{3,1},{4,6},{5,3},{6,8},{7,5},{8,10},{9,7},{10,... | collective-permute-start | bytes 184328 | tf_op jit(solution)/shard_map/ppermute | solution.py:374
  21.9 9.6 %copy-start.3 = (s32[3,4096]{1,0:T(4,128)S(1)}, s32[3,4096]{1,0:T(4,128)}, u32[]{:S(2)}) copy-start(s32[3,4096]{1,0:T(4,128)} %vectors_ref.1) | copy-start | bytes 147460
  22.2 6.4 %collective-permute-start.5 = (bf16[240,128]{1,0:T(8,128)(2,1)S(1)}, bf16[240,128]{1,0:T(8,128)(2,1)S(1)}, u32[]{:S(2)}, u32[]{:S(2)}) collective-permute-start(bf16[240,128]{1,0:T(8,128)(2,1)S(1)} %get-tuple-element.62.own_ref), channel_id=1, source_target_pairs={{0,15},{1,2},{2,1},{3,4},{4,3},{5,6},{6,5},{7,8},{8,7},{9,10},{10,... | collective-permute-start | bytes 184328 | tf_op jit(solution)/shard_map/ppermute | solution.py:372
  24.7 3.9 %collective-permute-start.6 = (bf16[240,128]{1,0:T(8,128)(2,1)S(1)}, bf16[240,128]{1,0:T(8,128)(2,1)S(1)}, u32[]{:S(2)}, u32[]{:S(2)}) collective-permute-start(bf16[240,128]{1,0:T(8,128)(2,1)S(1)} %get-tuple-element.62.own_ref), channel_id=1, source_target_pairs={{0,1},{1,0},{2,3},{3,2},{4,5},{5,4},{6,7},{7,6},{8,9},{9,8},{10,11... | collective-permute-start | bytes 184328 | tf_op jit(solution)/shard_map/ppermute | solution.py:366
  31.1 9.5 %collective-permute-start.7 = (f32[240,128]{1,0:T(8,128)S(1)}, f32[240,128]{1,0:T(8,128)S(1)}, u32[]{:S(2)}, u32[]{:S(2)}) collective-permute-start(f32[240,128]{1,0:T(8,128)S(1)} %get-tuple-element.65), channel_id=1, source_target_pairs={{0,1},{1,0},{2,3},{3,2},{4,5},{5,4},{6,7},{7,6},{8,9},{9,8},{10,11... | collective-permute-start | bytes 368648 | tf_op jit(solution)/shard_map/ppermute | solution.py:366
  31.2 7.2 %collective-permute-start.4 = (bf16[240,128]{1,0:T(8,128)(2,1)S(1)}, bf16[240,128]{1,0:T(8,128)(2,1)S(1)}, u32[]{:S(2)}, u32[]{:S(2)}) collective-permute-start(bf16[240,128]{1,0:T(8,128)(2,1)S(1)} %get-tuple-element.62.own_ref), channel_id=1, source_target_pairs={{0,2},{1,15},{2,4},{3,1},{4,6},{5,3},{6,8},{7,5},{8,10},{9,7},{10,... | collective-permute-start | bytes 184328 | tf_op jit(solution)/shard_map/ppermute | solution.py:374
  41.0 5.2 %collective-permute-start.8 = (bf16[240,128]{1,0:T(8,128)(2,1)S(1)}, bf16[240,128]{1,0:T(8,128)(2,1)S(1)}, u32[]{:S(2)}, u32[]{:S(2)}) collective-permute-start(bf16[240,128]{1,0:T(8,128)(2,1)S(1)} %get-tuple-element.67), channel_id=1, source_target_pairs={{0,4},{1,5},{2,6},{3,7},{4,0},{5,1},{6,2},{7,3},{8,12},{9,13},{10,... | collective-permute-start | bytes 184328 | tf_op jit(solution)/shard_map/ppermute | solution.py:366
  41.0 7.1 %collective-permute-start.9 = (bf16[240,128]{1,0:T(8,128)(2,1)S(1)}, bf16[240,128]{1,0:T(8,128)(2,1)S(1)}, u32[]{:S(2)}, u32[]{:S(2)}) collective-permute-start(bf16[240,128]{1,0:T(8,128)(2,1)S(1)} %get-tuple-element.67), channel_id=1, source_target_pairs={{0,8},{1,9},{2,10},{3,11},{4,12},{5,13},{6,14},{7,15},{8,0},{9,1},... | collective-permute-start | bytes 184328 | tf_op jit(solution)/shard_map/ppermute | solution.py:366
  41.1 7.1 %collective-permute-start.10 = (bf16[240,128]{1,0:T(8,128)(2,1)S(1)}, bf16[240,128]{1,0:T(8,128)(2,1)S(1)}, u32[]{:S(2)}, u32[]{:S(2)}) collective-permute-start(bf16[240,128]{1,0:T(8,128)(2,1)S(1)} %get-tuple-element.67), channel_id=1, source_target_pairs={{0,12},{1,13},{2,14},{3,15},{4,8},{5,9},{6,10},{7,11},{8,4},{9,5},... | collective-permute-start | bytes 184328 | tf_op jit(solution)/shard_map/ppermute | solution.py:366
  45.4 4.9 %collective-permute-start.11 = (bf16[240,128]{1,0:T(8,128)(2,1)S(1)}, bf16[240,128]{1,0:T(8,128)(2,1)S(1)}, u32[]{:S(2)}, u32[]{:S(2)}) collective-permute-start(bf16[240,128]{1,0:T(8,128)(2,1)S(1)} %get-tuple-element.67), channel_id=1, source_target_pairs={{0,2},{1,3},{2,0},{3,1},{4,6},{5,7},{6,4},{7,5},{8,10},{9,11},{10,... | collective-permute-start | bytes 184328 | tf_op jit(solution)/shard_map/ppermute | solution.py:366
  46.2 4.9 %collective-permute-start.12 = (bf16[240,128]{1,0:T(8,128)(2,1)S(1)}, bf16[240,128]{1,0:T(8,128)(2,1)S(1)}, u32[]{:S(2)}, u32[]{:S(2)}) collective-permute-start(bf16[240,128]{1,0:T(8,128)(2,1)S(1)} %collective-permute-done.8), channel_id=1, source_target_pairs={{0,2},{1,3},{2,0},{3,1},{4,6},{5,7},{6,4},{7,5},{8,10},{9,11},{10,... | collective-permute-start | bytes 184328 | tf_op jit(solution)/shard_map/ppermute | solution.py:366
  48.2 4.2 %collective-permute-start.13 = (bf16[240,128]{1,0:T(8,128)(2,1)S(1)}, bf16[240,128]{1,0:T(8,128)(2,1)S(1)}, u32[]{:S(2)}, u32[]{:S(2)}) collective-permute-start(bf16[240,128]{1,0:T(8,128)(2,1)S(1)} %collective-permute-done.9), channel_id=1, source_target_pairs={{0,2},{1,3},{2,0},{3,1},{4,6},{5,7},{6,4},{7,5},{8,10},{9,11},{10,... | collective-permute-start | bytes 184328 | tf_op jit(solution)/shard_map/ppermute | solution.py:366
  48.3 4.8 %collective-permute-start.14 = (bf16[240,128]{1,0:T(8,128)(2,1)S(1)}, bf16[240,128]{1,0:T(8,128)(2,1)S(1)}, u32[]{:S(2)}, u32[]{:S(2)}) collective-permute-start(bf16[240,128]{1,0:T(8,128)(2,1)S(1)} %collective-permute-done.10), channel_id=1, source_target_pairs={{0,2},{1,3},{2,0},{3,1},{4,6},{5,7},{6,4},{7,5},{8,10},{9,11},{10,... | collective-permute-start | bytes 184328 | tf_op jit(solution)/shard_map/ppermute | solution.py:366
  50.3 2.9 %collective-permute-start.15 = (bf16[5,240,128]{2,1,0:T(8,128)(2,1)S(1)}, bf16[5,240,128]{2,1,0:T(8,128)(2,1)S(1)}, u32[]{:S(2)}, u32[]{:S(2)}) collective-permute-start(bf16[5,240,128]{2,1,0:T(8,128)(2,1)S(1)} %get-tuple-element.74), channel_id=1, source_target_pairs={{0,1},{1,0},{2,3},{3,2},{4,5},{5,4},{6,7},{7,6},{8,9},{9,8},{10,11... | collective-permute-start | bytes 921608 | tf_op jit(solution)/shard_map/ppermute | solution.py:366
  53.1 1.5 %collective-permute-start.16 = (bf16[3,240,128]{2,1,0:T(8,128)(2,1)S(1)}, bf16[3,240,128]{2,1,0:T(8,128)(2,1)S(1)}, u32[]{:S(2)}, u32[]{:S(2)}) collective-permute-start(bf16[3,240,128]{2,1,0:T(8,128)(2,1)S(1)} %pad_maximum_fusion), channel_id=1, source_target_pairs={{0,1},{1,0},{2,3},{3,2},{4,5},{5,4},{6,7},{7,6},{8,9},{9,8},{10,11... | collective-permute-start | bytes 552968 | tf_op jit(solution)/shard_map/ppermute | solution.py:366
